TPU v7x, 256 devices: a whole 4x4x8 slice. The times are simulated.
256 devices in a mesh: section: 8 (over x, core), dp: 32 (over y, z).
Axes of the slice: x: 4, y: 4, z: 8, core: 2. Of those that a mesh axis runs over, the one named last changes fastest.
Arguments:
- inputs: bfloat16 [2, 32, 64, 1792], P(None, 'dp'), may hold values from -6 to 6
- cotangent: bfloat16 [2, 32, 64, 1792], P(None, 'dp'), may hold values from -180 to 180
- value_weight: bfloat16 [8, 1792, 1024], P('section', 'dp'), may hold values from -1 to 1
- output_weight: bfloat16 [8, 1024, 1792], P('section', 'dp'), may hold values from -1 to 1
- norm_gain: float32 [8, 1792], P('section'), may hold values from 0.5 to 2
- value_noise: float32 [8, 1792, 1024], P('section', 'dp'), may hold values from -6 to 6
- output_noise: float32 [8, 1024, 1792], P('section', 'dp'), may hold values from -6 to 6
Outputs:
- value_grad: float32 [8, 1792, 1024], P('section', 'dp')
- output_grad: float32 [8, 1024, 1792], P('section', 'dp')
All inputs are finite; a program needn't handle non-finite values.
Results may differ from a plain program's by a relative error of at most 0.018.
Values may be sent and summed in bfloat16 or wider, within the bound.
A program may use at most 64 MiB of HBM per device.

v0:
```python
import math

import jax
import jax.numpy as jnp
from jax import lax
from jax.sharding import PartitionSpec as P


def from_behind(block, axis, distance):
    devices = range(lax.axis_size(axis))
    route = [(i - distance, i) for i in devices if i - distance in devices]
    return lax.ppermute(block, axis, route)


def norm_parts(current, gains):
    widened = current.astype(jnp.float32)
    inverse = lax.rsqrt(jnp.mean(widened * widened, axis=-1, keepdims=True) + 1e-06)
    normed = (widened * inverse * gains).astype(jnp.bfloat16)
    return (widened, inverse, normed)


def layer_forward(current, gains, value_matrix, output_matrix):
    widened, inverse, normed = norm_parts(current, gains)
    values = jnp.dot(normed, value_matrix, preferred_element_type=jnp.float32).astype(jnp.bfloat16)
    result = (widened + jnp.dot(values, output_matrix, preferred_element_type=jnp.float32)).astype(
        jnp.bfloat16
    )
    return (values, result)


def layer_backward(current, incoming, gains, value_matrix, output_matrix):
    widened, inverse, normed = norm_parts(current, gains)
    dvalues = jnp.dot(incoming, output_matrix.T, preferred_element_type=jnp.float32).astype(
        jnp.bfloat16
    )
    dnormed = jnp.dot(dvalues, value_matrix.T, preferred_element_type=jnp.float32) * gains
    centred = widened * inverse
    through = inverse * (dnormed - centred * jnp.mean(dnormed * centred, axis=-1, keepdims=True))
    before = (incoming.astype(jnp.float32) + through).astype(jnp.bfloat16)
    return (normed, dvalues, before)


def example_sums(left, right, seq_len):
    first = left.reshape(-1, seq_len, left.shape[-1])
    second = right.reshape(-1, seq_len, right.shape[-1])
    per_example = jnp.einsum("eth,etd->ehd", first, second, preferred_element_type=jnp.float32)
    return jnp.sum(per_example * per_example, axis=(1, 2))


def forward_chain(feed_rows, gains, value_matrix, output_matrix):
    section_count = lax.axis_size("section")
    section_place = lax.axis_index("section")
    micro_count, row_count, feature_width = feed_rows.shape
    head_width = value_matrix.shape[1]

    def forward_active_step(source):
        return layer_forward(source, gains, value_matrix, output_matrix)

    def forward_spare_step(source):
        return (
            jnp.zeros((row_count, head_width), jnp.bfloat16),
            jnp.zeros((row_count, feature_width), jnp.bfloat16),
        )

    def forward_time_step(counter, carried):
        incoming, kept_inputs, kept_values = carried
        which_micro = counter - section_place
        active = (which_micro >= 0) & (which_micro < micro_count)
        slot_index = jnp.clip(which_micro, 0, micro_count - 1)
        source = jnp.where(
            section_place == 0,
            lax.dynamic_index_in_dim(feed_rows, slot_index, 0, keepdims=False),
            incoming,
        )
        values, result = lax.cond(active, forward_active_step, forward_spare_step, source)
        old_inputs = lax.dynamic_index_in_dim(kept_inputs, slot_index, 0, keepdims=False)
        old_values = lax.dynamic_index_in_dim(kept_values, slot_index, 0, keepdims=False)
        kept_inputs = lax.dynamic_update_index_in_dim(
            kept_inputs, jnp.where(active, source, old_inputs), slot_index, 0
        )
        kept_values = lax.dynamic_update_index_in_dim(
            kept_values, jnp.where(active, values, old_values), slot_index, 0
        )
        incoming = from_behind(result, "section", 1)
        return (incoming, kept_inputs, kept_values)

    start_state = (
        jnp.zeros((row_count, feature_width), jnp.bfloat16),
        jnp.zeros((micro_count, row_count, feature_width), jnp.bfloat16),
        jnp.zeros((micro_count, row_count, head_width), jnp.bfloat16),
    )
    final_state = lax.fori_loop(0, section_count + micro_count - 1, forward_time_step, start_state)
    return (final_state[1], final_state[2])


def backward_chain(kept_inputs, kept_values, cot_rows, gains, value_matrix, output_matrix, seq_len):
    section_count = lax.axis_size("section")
    section_place = lax.axis_index("section")
    micro_count, row_count, feature_width = kept_inputs.shape
    head_width = kept_values.shape[-1]
    example_here = row_count // seq_len
    last_place = section_count - 1

    def backward_active_step(operands):
        inputs_here, values_here, grad_here = operands
        normed, dvalues, before = layer_backward(
            inputs_here, grad_here, gains, value_matrix, output_matrix
        )
        squares = example_sums(normed, dvalues, seq_len) + example_sums(
            values_here, grad_here, seq_len
        )
        return (before, dvalues, squares)

    def backward_spare_step(operands):
        return (
            jnp.zeros((row_count, feature_width), jnp.bfloat16),
            jnp.zeros((row_count, head_width), jnp.bfloat16),
            jnp.zeros((example_here,), jnp.float32),
        )

    def backward_time_step(counter, carried):
        incoming, kept_grads, kept_dvalues, squares_all = carried
        which_micro = counter - (last_place - section_place)
        active = (which_micro >= 0) & (which_micro < micro_count)
        slot_index = jnp.clip(which_micro, 0, micro_count - 1)
        grad_here = jnp.where(
            section_place == last_place,
            lax.dynamic_index_in_dim(cot_rows, slot_index, 0, keepdims=False),
            incoming,
        )
        inputs_here = lax.dynamic_index_in_dim(kept_inputs, slot_index, 0, keepdims=False)
        values_here = lax.dynamic_index_in_dim(kept_values, slot_index, 0, keepdims=False)
        before, dvalues, squares = lax.cond(
            active, backward_active_step, backward_spare_step, (inputs_here, values_here, grad_here)
        )
        old_grads = lax.dynamic_index_in_dim(kept_grads, slot_index, 0, keepdims=False)
        old_dvalues = lax.dynamic_index_in_dim(kept_dvalues, slot_index, 0, keepdims=False)
        old_squares = lax.dynamic_index_in_dim(squares_all, slot_index, 0, keepdims=False)
        kept_grads = lax.dynamic_update_index_in_dim(
            kept_grads, jnp.where(active, grad_here, old_grads), slot_index, 0
        )
        kept_dvalues = lax.dynamic_update_index_in_dim(
            kept_dvalues, jnp.where(active, dvalues, old_dvalues), slot_index, 0
        )
        squares_all = lax.dynamic_update_index_in_dim(
            squares_all, jnp.where(active, squares, old_squares), slot_index, 0
        )
        incoming = from_behind(before, "section", -1)
        return (incoming, kept_grads, kept_dvalues, squares_all)

    start_state = (
        jnp.zeros((row_count, feature_width), jnp.bfloat16),
        jnp.zeros((micro_count, row_count, feature_width), jnp.bfloat16),
        jnp.zeros((micro_count, row_count, head_width), jnp.bfloat16),
        jnp.zeros((micro_count, example_here), jnp.float32),
    )
    final_state = lax.fori_loop(0, section_count + micro_count - 1, backward_time_step, start_state)
    return (final_state[1], final_state[2], final_state[3])


def on_device(inputs, cotangent, value_weight, output_weight, norm_gain, value_noise, output_noise):
    micro_count, example_count, seq_len, feature_width = inputs.shape
    feed_rows = inputs.reshape(micro_count, example_count * seq_len, feature_width)
    cot_rows = cotangent.reshape(micro_count, example_count * seq_len, feature_width)
    gathered_value, gathered_output = (
        lax.all_gather(value_weight, "dp", axis=1, tiled=True),
        lax.all_gather(output_weight, "dp", axis=1, tiled=True),
    )
    value_matrix = gathered_value[0]
    output_matrix = gathered_output[0]
    head_width = value_matrix.shape[1]
    gains = norm_gain[0]
    kept_inputs, kept_values = forward_chain(feed_rows, gains, value_matrix, output_matrix)
    kept_grads, kept_dvalues, partial_squares = backward_chain(
        kept_inputs, kept_values, cot_rows, gains, value_matrix, output_matrix, seq_len
    )
    total_squares = lax.psum(partial_squares, "section")
    clip_weight = 1.0 / (jnp.sqrt(total_squares) + 0.01)
    token_weight = jnp.repeat(clip_weight, seq_len, axis=1)[:, :, None]
    scaled_dvalues = (
        (kept_dvalues.astype(jnp.float32) * token_weight)
        .astype(jnp.bfloat16)
        .reshape(-1, head_width)
    )
    scaled_grads = (
        (kept_grads.astype(jnp.float32) * token_weight)
        .astype(jnp.bfloat16)
        .reshape(-1, feature_width)
    )
    unused_wide, unused_inverse, normed_rows = norm_parts(
        kept_inputs.reshape(-1, feature_width), gains
    )
    value_rows = kept_values.reshape(-1, head_width)
    columns = normed_rows
    value_part = lax.psum_scatter(
        lax.dot_general(
            columns, scaled_dvalues, (((0,), (0,)), ((), ())), preferred_element_type=jnp.float32
        ).astype(jnp.bfloat16),
        "dp",
        scatter_dimension=0,
        tiled=True,
    ).astype(jnp.float32)
    columns = value_rows
    output_part = lax.psum_scatter(
        lax.dot_general(
            columns, scaled_grads, (((0,), (0,)), ((), ())), preferred_element_type=jnp.float32
        ).astype(jnp.bfloat16),
        "dp",
        scatter_dimension=0,
        tiled=True,
    ).astype(jnp.float32)
    grad_scale = math.sqrt(feature_width * head_width)
    value_grad = (value_part * grad_scale + value_noise[0])[None]
    output_grad = (output_part * grad_scale + output_noise[0])[None]
    return (value_grad, output_grad)


def solution(mesh):
    return jax.shard_map(
        on_device,
        mesh=mesh,
        in_specs=(
            P(None, "dp", None, None),
            P(None, "dp", None, None),
            P("section", "dp", None),
            P("section", "dp", None),
            P("section", None),
            P("section", "dp", None),
            P("section", "dp", None),
        ),
        out_specs=(P("section", "dp", None), P("section", "dp", None)),
        check_vma=False,
    )
```

profile of v0, /device:TPU:4, one launch (start us, length us, event | category | flops | bytes accessed | tf_op | source)
XLA Modules:
  0.0 912.9 jit_solution(4904539429757416502)
XLA Ops:
  8.7 85.8 %all-gather.3.cloned.1.call-done = bf16[1,1792,1024]{2,1,0:T(8,128)(2,1)} async-done(((bf16[1,56,1024]{2,1,0:T(8,128)(2,1)}), bf16[1,1792,1024]{2,1,0:T(8,128)(2,1)}) %all-gather.3.cloned.1.call-update) | async-done | bytes 3670032 | tf_op jit(solution)/shard_map/all_gather | solution.py:166
  94.5 80.4 %all-gather.5.cloned.1.call-done = bf16[1,1024,1792]{2,1,0:T(8,128)(2,1)} async-done(((bf16[1,32,1792]{2,1,0:T(8,128)(2,1)}), bf16[1,1024,1792]{2,1,0:T(8,128)(2,1)}) %all-gather.5.cloned.1.call-update) | async-done | bytes 3670032 | tf_op jit(solution)/shard_map/all_gather | solution.py:167
  175.0 103.8 %while.39 = (s32[]{:T(128)}, bf16[64,1792]{1,0:T(8,128)(2,1)S(1)}, bf16[2,64,1792]{2,1,0:T(8,128)(2,1)S(1)}, bf16[2,64,1024]{2,1,0:T(8,128)(2,1)S(1)}, s32[]{:T(...) while((s32[]{:T(128)}, bf16[64,1792]{1,0:T(8,128)(2,1)S(1)}, ...), condition=%wide.region_4.5_spmd, body=%wide.region_0.4_spmd.sunk | while | flops 471269440 | bytes 26401092 | solution.py:92
  178.8 5.3 collective-permute-done
  187.9 5.3 collective-permute-done
  197.0 5.3 collective-permute-done
  206.1 15.8 %collective-permute-done = bf16[64,1792]{1,0:T(8,128)(2,1)S(1)} collective-permute-done((bf16[64,1792]{1,0:T(8,128)(2,1)S(1)}, bf16[64,1792]{1,0:T(8,128)(2,1)S(1)}, u32[]{:S(2)}, u32[]{:S(2)}) %collective-permute-start) | collective-permute-done | bytes 229408 | tf_op jit(solution)/shard_map/while/body/eval_jaxpr/ppermute | solution.py:12
  223.0 6.2 conditional.4
  223.9 3.6 convolution_convert_fusion
  232.1 4.4 collective-permute-done
  237.6 6.2 conditional.4
  238.5 3.6 convolution_convert_fusion
  246.7 4.4 collective-permute-done
  252.9 3.5 collective-permute-start
  256.5 3.8 collective-permute-done
  264.0 5.3 collective-permute-done
  271.1 6.5 collective-permute-start
  278.9 148.0 %while.40 = (s32[]{:T(128)}, bf16[64,1792]{1,0:T(8,128)(2,1)S(1)}, bf16[2,64,1792]{2,1,0:T(8,128)(2,1)S(1)}, bf16[2,64,1024]{2,1,0:T(8,128)(2,1)S(1)}, f32[2,1]{...) while((s32[]{:T(128)}, bf16[64,1792]{1,0:T(8,128)(2,1)S(1)}, ...), condition=%wide.region_13.14_spmd, body=%wide.region_6.0_spmd.sunk | while | flops 949518400 | bytes 14905603 | solution.py:157
  282.4 3.9 collective-permute-done.1
  289.9 4.7 collective-permute-done.1
  298.1 38.1 %collective-permute-done.1 = bf16[64,1792]{1,0:T(8,128)(2,1)S(1)} collective-permute-done((bf16[64,1792]{1,0:T(8,128)(2,1)S(1)}, bf16[64,1792]{1,0:T(8,128)(2,1)S(1)}, u32[]{:S(2)}, u32[]{:S(2)}) %collective-permute-start.1) | collective-permute-done | bytes 229408 | tf_op jit(solution)/shard_map/while/body/eval_jaxpr/ppermute | solution.py:12
  336.3 13.9 %conditional.5 = (bf16[64,1792]{1,0:T(8,128)(2,1)S(1)}, bf16[64,1024]{1,0:T(8,128)(2,1)S(1)}, f32[1]{0:T(128)}) conditional(s32[]{:T(128)} %convert_element_type.146, () %tuple.100, (bf16[64,1792]{1,0:T(8,128)(2,1)S(1)}, bf16[2,64,1792]{2,1,0:T(8,128)(2,1)S(1)}, s32[]{:T(128)}, bf16[1024,1792]{1,0:T(8,128)(2,1)}, bf16[1792,1024]{1,0:T(8,128)(2,1)}, ...), branch_computations={%region_7.7_spmd, %region_8.12_spmd} | conditional | flops 949223488 | bytes 11726744 | solution.py:133
  339.8 3.4 fusion.10
  353.5 4.1 collective-permute-done.1
  357.6 13.9 %conditional.5 = (bf16[64,1792]{1,0:T(8,128)(2,1)S(1)}, bf16[64,1024]{1,0:T(8,128)(2,1)S(1)}, f32[1]{0:T(128)}) conditional(s32[]{:T(128)} %convert_element_type.146, () %tuple.100, (bf16[64,1792]{1,0:T(8,128)(2,1)S(1)}, bf16[2,64,1792]{2,1,0:T(8,128)(2,1)S(1)}, s32[]{:T(128)}, bf16[1024,1792]{1,0:T(8,128)(2,1)}, bf16[1792,1024]{1,0:T(8,128)(2,1)}, ...), branch_computations={%region_7.7_spmd, %region_8.12_spmd} | conditional | flops 949223488 | bytes 11726744 | solution.py:133
  377.2 17.6 %collective-permute-start.1 = (bf16[64,1792]{1,0:T(8,128)(2,1)S(1)}, bf16[64,1792]{1,0:T(8,128)(2,1)S(1)}, u32[]{:S(2)}, u32[]{:S(2)}) collective-permute-start(bf16[64,1792]{1,0:T(8,128)(2,1)S(1)} %get-tuple-element.768), channel_id=1, source_target_pairs={{32,0},{64,32},{96,64},{128,96},{160,128},{192,160},{224,192},{33,... | collective-permute-start | bytes 688136 | tf_op jit(solution)/shard_map/while/body/eval_jaxpr/ppermute | solution.py:12
  398.6 3.8 collective-permute-start.1
  406.1 9.7 %collective-permute-start.1 = (bf16[64,1792]{1,0:T(8,128)(2,1)S(1)}, bf16[64,1792]{1,0:T(8,128)(2,1)S(1)}, u32[]{:S(2)}, u32[]{:S(2)}) collective-permute-start(bf16[64,1792]{1,0:T(8,128)(2,1)S(1)} %get-tuple-element.768), channel_id=1, source_target_pairs={{32,0},{64,32},{96,64},{128,96},{160,128},{192,160},{224,192},{33,... | collective-permute-start | bytes 688136 | tf_op jit(solution)/shard_map/while/body/eval_jaxpr/ppermute | solution.py:12
  419.6 3.8 collective-permute-start.1
  426.9 33.5 %psum.7 = f32[2,1]{0,1:T(1,128)S(1)} all-reduce(f32[2,1]{0,1:T(1,128)S(1)} %get-tuple-element.560), channel_id=1, replica_groups=mesh['section'=8,'dp'=32] {'section'}, use_global_device_ids=true, to_apply=%region_14.15 | all-reduce | flops 2 | bytes 16 | tf_op jit(solution)/shard_map/psum | solution.py:177
  467.4 215.2 %reduce-scatter.5.cloned.1.call-done = bf16[32,1792]{1,0:T(8,128)(2,1)} async-done(((bf16[1024,1792]{1,0:T(8,128)(2,1)}), bf16[32,1792]{1,0:T(8,128)(2,1)}) %reduce-scatter.5.cloned.1.call-update) | async-done | bytes 114704 | tf_op jit(solution)/shard_map/reduce_scatter | solution.py:204
  684.3 220.4 %reduce-scatter.3.cloned.1.call-done = bf16[56,1024]{1,0:T(8,128)(2,1)} async-done(((bf16[1792,1024]{1,0:T(8,128)(2,1)}), bf16[56,1024]{1,0:T(8,128)(2,1)}) %reduce-scatter.3.cloned.1.call-update) | async-done | bytes 114704 | tf_op jit(solution)/shard_map/reduce_scatter | solution.py:195
  (222 shorter events, 103.2 us)
Async XLA Ops:
  7.2 87.3 %all-gather.3.cloned.1.call-start = ((), (), s32[]{:S(2)}) async-start(), calls=%async_computation.2 | async-start | bytes 3784704 | tf_op jit(solution)/shard_map/all_gather | solution.py:166
  7.9 167.0 %all-gather.5.cloned.1.call-start = ((), (), s32[]{:S(2)}) async-start(), calls=%async_computation.3 | async-start | bytes 3784704 | tf_op jit(solution)/shard_map/all_gather | solution.py:167
  8.6 674.0 %reduce-scatter.5.cloned.1.call-start = ((), (), s32[]{:S(2)}) async-start(), calls=%async_computation.5 | async-start | bytes 3784704 | tf_op jit(solution)/shard_map/reduce_scatter | solution.py:204
  175.0 103.9 %copy-start.3 = (bf16[2,1,64,1792]{3,2,1,0:T(8,128)(2,1)S(1)}, bf16[2,1,64,1792]{3,2,1,0:T(8,128)(2,1)}, u32[]{:S(2)}) copy-start(bf16[2,1,64,1792]{3,2,1,0:T(8,128)(2,1)} %param.16) | copy-start | bytes 1376260
  176.8 7.3 collective-permute-start
  185.9 7.3 collective-permute-start
  195.0 7.3 collective-permute-start
  204.1 17.8 %collective-permute-start = (bf16[64,1792]{1,0:T(8,128)(2,1)S(1)}, bf16[64,1792]{1,0:T(8,128)(2,1)S(1)}, u32[]{:S(2)}, u32[]{:S(2)}) collective-permute-start(bf16[64,1792]{1,0:T(8,128)(2,1)S(1)} %get-tuple-element.751), channel_id=1, source_target_pairs={{0,32},{32,64},{64,96},{96,128},{128,160},{160,192},{192,224},{1,3... | collective-permute-start | bytes 688136 | tf_op jit(solution)/shard_map/while/body/eval_jaxpr/ppermute | solution.py:12
  223.9 3.7 copy-start
  229.2 7.3 collective-permute-start
  238.5 3.7 copy-start
  243.8 7.3 collective-permute-start
  252.9 7.3 collective-permute-start
  262.0 7.3 collective-permute-start
  271.1 7.6 collective-permute-start
  279.1 7.2 collective-permute-start.1
  286.5 8.1 collective-permute-start.1
  294.8 41.4 %collective-permute-start.1 = (bf16[64,1792]{1,0:T(8,128)(2,1)S(1)}, bf16[64,1792]{1,0:T(8,128)(2,1)S(1)}, u32[]{:S(2)}, u32[]{:S(2)}) collective-permute-start(bf16[64,1792]{1,0:T(8,128)(2,1)S(1)} %get-tuple-element.768), channel_id=1, source_target_pairs={{32,0},{64,32},{96,64},{128,96},{160,128},{192,160},{224,192},{33,... | collective-permute-start | bytes 688136 | tf_op jit(solution)/shard_map/while/body/eval_jaxpr/ppermute | solution.py:12
  336.3 3.5 copy-start.4
  339.7 6.5 copy-start.1
  346.2 4.0 copy-start.2
  350.2 7.3 collective-permute-start.1
  361.1 6.5 copy-start.1
  367.6 4.0 copy-start.2
  371.5 5.4 collective-permute-start.1
  377.2 21.2 %collective-permute-start.1 = (bf16[64,1792]{1,0:T(8,128)(2,1)S(1)}, bf16[64,1792]{1,0:T(8,128)(2,1)S(1)}, u32[]{:S(2)}, u32[]{:S(2)}) collective-permute-start(bf16[64,1792]{1,0:T(8,128)(2,1)S(1)} %get-tuple-element.768), channel_id=1, source_target_pairs={{32,0},{64,32},{96,64},{128,96},{160,128},{192,160},{224,192},{33,... | collective-permute-start | bytes 688136 | tf_op jit(solution)/shard_map/while/body/eval_jaxpr/ppermute | solution.py:12
  398.6 7.3 collective-permute-start.1
  406.1 13.3 %collective-permute-start.1 = (bf16[64,1792]{1,0:T(8,128)(2,1)S(1)}, bf16[64,1792]{1,0:T(8,128)(2,1)S(1)}, u32[]{:S(2)}, u32[]{:S(2)}) collective-permute-start(bf16[64,1792]{1,0:T(8,128)(2,1)S(1)} %get-tuple-element.768), channel_id=1, source_target_pairs={{32,0},{64,32},{96,64},{128,96},{160,128},{192,160},{224,192},{33,... | collective-permute-start | bytes 688136 | tf_op jit(solution)/shard_map/while/body/eval_jaxpr/ppermute | solution.py:12
  419.6 7.3 collective-permute-start.1
  463.5 441.3 %reduce-scatter.3.cloned.1.call-start = ((), (), s32[]{:S(2)}) async-start(), calls=%async_computation.4 | async-start | bytes 3784704 | tf_op jit(solution)/shard_map/reduce_scatter | solution.py:195
  467.4 215.3 %copy-start.6 = (f32[1,32,1792]{2,1,0:T(8,128)S(1)}, f32[1,32,1792]{2,1,0:T(8,128)}, u32[]{:S(2)}) copy-start(f32[1,32,1792]{2,1,0:T(8,128)} %param.21) | copy-start | bytes 688132
  467.4 437.3 %copy-start.7 = (f32[1,56,1024]{2,1,0:T(8,128)S(1)}, f32[1,56,1024]{2,1,0:T(8,128)}, u32[]{:S(2)}) copy-start(f32[1,56,1024]{2,1,0:T(8,128)} %param.20) | copy-start | bytes 688132
  (2 other events, 4.1 us)
Sparse Core Ops, SparseCore 0:
  10.6 83.8 all-gather.2
  97.0 77.7 all-gather.4
  463.6 219.0 reduce-scatter.4
  686.9 217.7 reduce-scatter.2
where the time goes:
time: 914 us; the launch traced here: 913 us
  waiting for transfers between devices  715 us (78%)
  starting transfers between devices  68.3 us (7%)
  matrix products  40.9 us (4%)
  blocking collectives  33.5 us (4%)
  other arithmetic  18.8 us (2%)
  between operations  13.8 us (2%)
  local copies, waits for them, and re-layouts  12.5 us (1%)
  loops' own time  9.78 us (1%)
    reduce_scatter x1, waiting for transfers between devices, on_device(): lax.psum_scatter(lax.dot_general(columns, scaled_dvalues, (((0,), (0,)),...  220 us
    reduce_scatter x1, waiting for transfers between devices, on_device(): lax.psum_scatter(lax.dot_general(columns, scaled_grads, (((0,), (0,)), ((...  215 us
    ppermute x18, waiting for transfers between devices, from_behind(): return lax.ppermute(block, axis, route)  112 us
    all_gather x1, waiting for transfers between devices, on_device(): lax.all_gather(value_weight, 'dp', axis=1, tiled=True)  85.8 us
    all_gather x1, waiting for transfers between devices, on_device(): lax.all_gather(output_weight, 'dp', axis=1, tiled=True)  80.4 us
    ppermute x18, starting transfers between devices, from_behind(): return lax.ppermute(block, axis, route)  68.1 us
    psum x1, blocking collectives, on_device(): total_squares = lax.psum(partial_squares, 'section')  33.5 us
  transfers between devices with their start and end apart: 22, of which 22 were waited for; matrix products, arithmetic and copies ran while one was open for 2% of the time, Pallas kernels for 0%

commit v1 on v0

--- a/solution.py
+++ b/solution.py
@@ -3,7 +3,7 @@
 import jax
 import jax.numpy as jnp
 from jax import lax
-from jax.sharding import PartitionSpec as P
+from jax.sharding import Mesh, PartitionSpec as P
 
 
 def from_behind(block, axis, distance):
@@ -158,16 +158,39 @@
     return (final_state[1], final_state[2], final_state[3])
 
 
+DP = ("y", "z")
+
+
+def gather_rows(shard):
+    inner = lax.all_gather(shard, "z", axis=0, tiled=True)
+    return lax.all_gather(inner, "y", axis=0, tiled=True)
+
+
+def exchange_rows(shard):
+    count = lax.axis_size(DP)
+    copies = jnp.broadcast_to(shard[None], (count,) + shard.shape)
+    parts = lax.all_to_all(copies, DP, 0, 0, tiled=False)
+    return parts.reshape((-1,) + shard.shape[1:])
+
+
+def scatter_in_stages(block):
+    inner = lax.psum_scatter(block, "y", scatter_dimension=0, tiled=True)
+    return lax.psum_scatter(inner, "z", scatter_dimension=0, tiled=True).astype(jnp.float32)
+
+
+def scatter_by_exchange(block):
+    count = lax.axis_size(DP)
+    parts = block.reshape((count, block.shape[0] // count) + block.shape[1:])
+    arrived = lax.all_to_all(parts, DP, 0, 0, tiled=False)
+    return jnp.sum(arrived.astype(jnp.float32), axis=0)
+
+
 def on_device(inputs, cotangent, value_weight, output_weight, norm_gain, value_noise, output_noise):
     micro_count, example_count, seq_len, feature_width = inputs.shape
     feed_rows = inputs.reshape(micro_count, example_count * seq_len, feature_width)
     cot_rows = cotangent.reshape(micro_count, example_count * seq_len, feature_width)
-    gathered_value, gathered_output = (
-        lax.all_gather(value_weight, "dp", axis=1, tiled=True),
-        lax.all_gather(output_weight, "dp", axis=1, tiled=True),
-    )
-    value_matrix = gathered_value[0]
-    output_matrix = gathered_output[0]
+    value_matrix = gather_rows(value_weight[0])
+    output_matrix = exchange_rows(output_weight[0])
     head_width = value_matrix.shape[1]
     gains = norm_gain[0]
     kept_inputs, kept_values = forward_chain(feed_rows, gains, value_matrix, output_matrix)
@@ -192,42 +215,49 @@
     )
     value_rows = kept_values.reshape(-1, head_width)
     columns = normed_rows
-    value_part = lax.psum_scatter(
+    value_part = scatter_in_stages(
         lax.dot_general(
             columns, scaled_dvalues, (((0,), (0,)), ((), ())), preferred_element_type=jnp.float32
-        ).astype(jnp.bfloat16),
-        "dp",
-        scatter_dimension=0,
-        tiled=True,
-    ).astype(jnp.float32)
+        ).astype(jnp.bfloat16)
+    )
     columns = value_rows
-    output_part = lax.psum_scatter(
+    output_part = scatter_by_exchange(
         lax.dot_general(
             columns, scaled_grads, (((0,), (0,)), ((), ())), preferred_element_type=jnp.float32
-        ).astype(jnp.bfloat16),
-        "dp",
-        scatter_dimension=0,
-        tiled=True,
-    ).astype(jnp.float32)
+        ).astype(jnp.bfloat16)
+    )
     grad_scale = math.sqrt(feature_width * head_width)
     value_grad = (value_part * grad_scale + value_noise[0])[None]
     output_grad = (output_part * grad_scale + output_noise[0])[None]
     return (value_grad, output_grad)
 
 
+def split_dp(mesh):
+    devices = mesh.devices
+    sections, count = devices.shape
+    try:
+        across = len({d.coords[1] for d in devices[0]})
+    except (AttributeError, IndexError, TypeError):
+        across = 1
+    if across < 1 or count % across:
+        across = 1
+    return Mesh(devices.reshape(sections, across, count // across), ("section",) + DP)
+
+
 def solution(mesh):
+    grid = split_dp(mesh)
     return jax.shard_map(
         on_device,
-        mesh=mesh,
+        mesh=grid,
         in_specs=(
-            P(None, "dp", None, None),
-            P(None, "dp", None, None),
-            P("section", "dp", None),
-            P("section", "dp", None),
+            P(None, DP, None, None),
+            P(None, DP, None, None),
+            P("section", DP, None),
+            P("section", DP, None),
             P("section", None),
-            P("section", "dp", None),
-            P("section", "dp", None),
+            P("section", DP, None),
+            P("section", DP, None),
         ),
-        out_specs=(P("section", "dp", None), P("section", "dp", None)),
+        out_specs=(P("section", DP, None), P("section", DP, None)),
         check_vma=False,
     )

time: 914 us -> 590 us (0.65)
  waiting for transfers between devices: 715 us -> 266 us
  blocking collectives: 33.5 us -> 139 us
  starting transfers between devices: 68.3 us -> 90.3 us
    reduce_scatter x2, waiting for transfers between devices: 436 us -> 85.9 us  [the longest x1 63.1 us: scatter_in_stages(): inner = lax.psum_scatter(block, 'y', scatter_dimension=0, tiled=True)]
    all_gather x2 -> x1, waiting for transfers between devices: 166 us -> 44.9 us  [gather_rows(): return lax.all_gather(inner, 'y', axis=0, tiled=True)]
    all_gather x0 -> x1, blocking collectives: none -> 106 us  [gather_rows(): inner = lax.all_gather(shard, 'z', axis=0, tiled=True)]
    all_to_all x0 -> x2, waiting for transfers between devices: none -> 21.4 us  [the longest x1 21.4 us: scatter_by_exchange(): arrived = lax.all_to_all(parts, DP, 0, 0, tiled=False)]
    all_to_all x0 -> x2, starting transfers between devices: none -> 20.7 us  [the longest x1 11.7 us: exchange_rows(): parts = lax.all_to_all(copies, DP, 0, 0, tiled=False)]
  transfers between devices with their start and end apart: 22 -> 23, of which waited for: 22 -> 22; matrix products, arithmetic and copies ran while one was open for 2% -> 3% of each run, Pallas kernels for 0% -> 0%
where the time goes in v1:
time: 590 us; the launch traced here: 589 us
  waiting for transfers between devices  266 us (45%)
  blocking collectives  139 us (24%)
  starting transfers between devices  90.3 us (15%)
  matrix products  43.4 us (7%)
  local copies, waits for them, and re-layouts  15.1 us (3%)
  between operations  13.9 us (2%)
  other arithmetic  10.6 us (2%)
  loops' own time  9.86 us (2%)
    ppermute x18, waiting for transfers between devices, from_behind(): return lax.ppermute(block, axis, route)  114 us
    all_gather x1, blocking collectives, gather_rows(): inner = lax.all_gather(shard, 'z', axis=0, tiled=True)  106 us
    ppermute x18, starting transfers between devices, from_behind(): return lax.ppermute(block, axis, route)  69.5 us
    reduce_scatter x1, waiting for transfers between devices, scatter_in_stages(): inner = lax.psum_scatter(block, 'y', scatter_dimension=0, tiled=True)  63.1 us
    all_gather x1, waiting for transfers between devices, gather_rows(): return lax.all_gather(inner, 'y', axis=0, tiled=True)  44.9 us
    psum x1, blocking collectives, on_device(): total_squares = lax.psum(partial_squares, 'section')  33.8 us
    reduce_scatter x1, waiting for transfers between devices, scatter_in_stages(): lax.psum_scatter(inner, 'z', scatter_dimension=0, tiled=True)  22.9 us
    all_to_all x1, waiting for transfers between devices, scatter_by_exchange(): arrived = lax.all_to_all(parts, DP, 0, 0, tiled=False)  21.4 us
  transfers between devices with their start and end apart: 23, of which 22 were waited for; matrix products, arithmetic and copies ran while one was open for 3% of the time, Pallas kernels for 0%

profile of v1, /device:TPU:4, one launch (start us, length us, event | category | flops | bytes accessed | tf_op | source)
XLA Modules:
  0.0 588.7 jit_solution(12497531110454642045)
XLA Ops:
  10.4 11.7 %all-to-all-start = ((bf16[32,32,1792]{2,1,0:T(8,128)(2,1)}), bf16[32,32,1792]{2,1,0:T(8,128)(2,1)}, u32[]{:S(2)}, u32[]{:S(2)}) async-start(bf16[32,32,1792]{2,1,0:T(8,128)(2,1)} %broadcast_in_dim.63), calls=%async_computation | async-start | bytes 7340032 | tf_op jit(solution)/shard_map/all_to_all | solution.py:172
  22.2 105.7 %all-gather = bf16[1,448,1024]{2,1,0:T(8,128)(2,1)} all-gather(bf16[1,56,1024]{2,1,0:T(8,128)(2,1)S(1)} %copy-done.7), channel_id=2, replica_groups=mesh['section'=8,'y'=4,'z'=8] {'z'}, dimensions={1}, use_global_device_ids=true | all-gather | bytes 1032192 | tf_op jit(solution)/shard_map/all_gather | solution.py:165
  128.0 44.9 %all-gather.4.cloned.1.call-done = bf16[1,1792,1024]{2,1,0:T(8,128)(2,1)} async-done(((bf16[1,448,1024]{2,1,0:T(8,128)(2,1)}), bf16[1,1792,1024]{2,1,0:T(8,128)(2,1)}) %all-gather.4.cloned.1.call-update) | async-done | bytes 3670032 | tf_op jit(solution)/shard_map/all_gather | solution.py:166
  173.0 98.2 %while.39 = (s32[]{:T(128)}, bf16[64,1792]{1,0:T(8,128)(2,1)S(1)}, bf16[2,64,1792]{2,1,0:T(8,128)(2,1)S(1)}, bf16[2,64,1024]{2,1,0:T(8,128)(2,1)S(1)}, s32[]{:T(...) while((s32[]{:T(128)}, bf16[64,1792]{1,0:T(8,128)(2,1)S(1)}, ...), condition=%wide.region_4.5_spmd, body=%wide.region_0.4_spmd.sunk | while | flops 471269440 | bytes 11721002 | solution.py:92
  175.9 5.3 collective-permute-done
  184.1 5.3 collective-permute-done
  192.2 5.3 collective-permute-done
  200.4 17.2 %collective-permute-done = bf16[64,1792]{1,0:T(8,128)(2,1)S(1)} collective-permute-done((bf16[64,1792]{1,0:T(8,128)(2,1)S(1)}, bf16[64,1792]{1,0:T(8,128)(2,1)S(1)}, u32[]{:S(2)}, u32[]{:S(2)}) %collective-permute-start) | collective-permute-done | bytes 229408 | tf_op jit(solution)/shard_map/while/body/eval_jaxpr/ppermute | solution.py:12
  217.7 6.6 %conditional.4 = (bf16[64,1024]{1,0:T(8,128)(2,1)}, bf16[64,1792]{1,0:T(8,128)(2,1)S(1)}) conditional(s32[]{:T(128)} %convert_element_type.145, () %tuple.96, (bf16[64,1792]{1,0:T(8,128)(2,1)S(1)}, f32[1,1792]{1,0:T(1,128)S(1)}, bf16[1792,1024]{1,0:T(8,128)(2,1)}, bf16[1024,1792]{1,0:T(8,128)(2,1)}) %tuple.97), branch_computations={%region_1.1_spmd, %region_2.3_spmd} | conditional | flops 470974528 | bytes 8542228 | solution.py:75
  217.9 3.5 convolution_convert_fusion
  227.2 4.4 collective-permute-done
  231.8 6.6 %conditional.4 = (bf16[64,1024]{1,0:T(8,128)(2,1)}, bf16[64,1792]{1,0:T(8,128)(2,1)S(1)}) conditional(s32[]{:T(128)} %convert_element_type.145, () %tuple.96, (bf16[64,1792]{1,0:T(8,128)(2,1)S(1)}, f32[1,1792]{1,0:T(1,128)S(1)}, bf16[1792,1024]{1,0:T(8,128)(2,1)}, bf16[1024,1792]{1,0:T(8,128)(2,1)}) %tuple.97), branch_computations={%region_1.1_spmd, %region_2.3_spmd} | conditional | flops 470974528 | bytes 8542228 | solution.py:75
  241.3 4.4 collective-permute-done
  246.5 3.8 collective-permute-start
  256.7 5.3 collective-permute-done
  262.9 7.3 %collective-permute-start = (bf16[64,1792]{1,0:T(8,128)(2,1)S(1)}, bf16[64,1792]{1,0:T(8,128)(2,1)S(1)}, u32[]{:S(2)}, u32[]{:S(2)}) collective-permute-start(bf16[64,1792]{1,0:T(8,128)(2,1)S(1)} %get-tuple-element.751), channel_id=1, source_target_pairs={{0,32},{32,64},{64,96},{96,128},{128,160},{160,192},{192,224},{1,3... | collective-permute-start | bytes 688136 | tf_op jit(solution)/shard_map/while/body/eval_jaxpr/ppermute | solution.py:12
  271.5 149.4 %while.40 = (s32[]{:T(128)}, bf16[64,1792]{1,0:T(8,128)(2,1)S(1)}, bf16[2,64,1792]{2,1,0:T(8,128)(2,1)S(1)}, bf16[2,64,1024]{2,1,0:T(8,128)(2,1)S(1)}, f32[2,1]{...) while((s32[]{:T(128)}, bf16[64,1792]{1,0:T(8,128)(2,1)S(1)}, ...), condition=%wide.region_13.14_spmd, body=%wide.region_6.0_spmd.sunk | while | flops 949518400 | bytes 14876903 | solution.py:157
  275.0 3.9 collective-permute-done.1
  282.6 4.7 collective-permute-done.1
  290.7 38.9 %collective-permute-done.1 = bf16[64,1792]{1,0:T(8,128)(2,1)S(1)} collective-permute-done((bf16[64,1792]{1,0:T(8,128)(2,1)S(1)}, bf16[64,1792]{1,0:T(8,128)(2,1)S(1)}, u32[]{:S(2)}, u32[]{:S(2)}) %collective-permute-start.1) | collective-permute-done | bytes 229408 | tf_op jit(solution)/shard_map/while/body/eval_jaxpr/ppermute | solution.py:12
  329.7 14.0 %conditional.5 = (bf16[64,1792]{1,0:T(8,128)(2,1)S(1)}, bf16[64,1024]{1,0:T(8,128)(2,1)S(1)}, f32[1]{0:T(128)}) conditional(s32[]{:T(128)} %convert_element_type.146, () %tuple.100, (bf16[64,1792]{1,0:T(8,128)(2,1)S(1)}, bf16[2,64,1792]{2,1,0:T(8,128)(2,1)S(1)}, s32[]{:T(128)}, bf16[1024,1792]{1,0:T(8,128)(2,1)}, bf16[1792,1024]{1,0:T(8,128)(2,1)}, ...), branch_computations={%region_7.7_spmd, %region_8.12_spmd} | conditional | flops 949223488 | bytes 11698044 | solution.py:133
  347.0 4.1 collective-permute-done.1
  351.2 14.0 %conditional.5 = (bf16[64,1792]{1,0:T(8,128)(2,1)S(1)}, bf16[64,1024]{1,0:T(8,128)(2,1)S(1)}, f32[1]{0:T(128)}) conditional(s32[]{:T(128)} %convert_element_type.146, () %tuple.100, (bf16[64,1792]{1,0:T(8,128)(2,1)S(1)}, bf16[2,64,1792]{2,1,0:T(8,128)(2,1)S(1)}, s32[]{:T(128)}, bf16[1024,1792]{1,0:T(8,128)(2,1)}, bf16[1792,1024]{1,0:T(8,128)(2,1)}, ...), branch_computations={%region_7.7_spmd, %region_8.12_spmd} | conditional | flops 949223488 | bytes 11698044 | solution.py:133
  370.9 17.8 %collective-permute-start.1 = (bf16[64,1792]{1,0:T(8,128)(2,1)S(1)}, bf16[64,1792]{1,0:T(8,128)(2,1)S(1)}, u32[]{:S(2)}, u32[]{:S(2)}) collective-permute-start(bf16[64,1792]{1,0:T(8,128)(2,1)S(1)} %get-tuple-element.768), channel_id=1, source_target_pairs={{32,0},{64,32},{96,64},{128,96},{160,128},{192,160},{224,192},{33,... | collective-permute-start | bytes 688136 | tf_op jit(solution)/shard_map/while/body/eval_jaxpr/ppermute | solution.py:12
  392.4 3.8 collective-permute-start.1
  399.9 9.9 %collective-permute-start.1 = (bf16[64,1792]{1,0:T(8,128)(2,1)S(1)}, bf16[64,1792]{1,0:T(8,128)(2,1)S(1)}, u32[]{:S(2)}, u32[]{:S(2)}) collective-permute-start(bf16[64,1792]{1,0:T(8,128)(2,1)S(1)} %get-tuple-element.768), channel_id=1, source_target_pairs={{32,0},{64,32},{96,64},{128,96},{160,128},{192,160},{224,192},{33,... | collective-permute-start | bytes 688136 | tf_op jit(solution)/shard_map/while/body/eval_jaxpr/ppermute | solution.py:12
  413.5 3.8 collective-permute-start.1
  420.9 33.8 %psum.7 = f32[2,1]{0,1:T(1,128)S(1)} all-reduce(f32[2,1]{0,1:T(1,128)S(1)} %get-tuple-element.560), channel_id=1, replica_groups=mesh['section'=8,'y'=4,'z'=8] {'section'}, use_global_device_ids=true, to_apply=%region_14.15 | all-reduce | flops 2 | bytes 16 | tf_op jit(solution)/shard_map/psum | solution.py:200
  460.9 8.9 %all-to-all-start.1 = ((bf16[32,32,1792]{2,1,0:T(8,128)(2,1)}), bf16[32,32,1792]{2,1,0:T(8,128)(2,1)}, u32[]{:S(2)}, u32[]{:S(2)}) async-start(bf16[32,32,1792]{2,1,0:T(8,128)(2,1)} %bitcast.99), calls=%async_computation.3 | async-start | bytes 7340032 | tf_op jit(solution)/shard_map/all_to_all | solution.py:184
  469.9 63.1 %reduce-scatter.3.cloned.1.call-done = bf16[448,1024]{1,0:T(8,128)(2,1)} async-done(((bf16[1792,1024]{1,0:T(8,128)(2,1)}), bf16[448,1024]{1,0:T(8,128)(2,1)}) %reduce-scatter.3.cloned.1.call-update) | async-done | bytes 917520 | tf_op jit(solution)/shard_map/reduce_scatter | solution.py:177
  533.0 21.4 %all-to-all-done.1 = bf16[32,32,1792]{2,1,0:T(8,128)(2,1)} async-done(((bf16[32,32,1792]{2,1,0:T(8,128)(2,1)}), bf16[32,32,1792]{2,1,0:T(8,128)(2,1)}, u32[]{:S(2)}, u32[]{:S(2)}) %all-to-all-start.1) | async-done | bytes 3670048 | tf_op jit(solution)/shard_map/all_to_all | solution.py:184
  557.7 22.9 %reduce-scatter.5.cloned.1.call-done = bf16[56,1024]{1,0:T(8,128)(2,1)} async-done(((bf16[448,1024]{1,0:T(8,128)(2,1)}), bf16[56,1024]{1,0:T(8,128)(2,1)}) %reduce-scatter.5.cloned.1.call-update) | async-done | bytes 114704 | tf_op jit(solution)/shard_map/reduce_scatter | solution.py:178
  (222 shorter events, 109.2 us)
Async XLA Ops:
  10.4 11.8 %copy-start.7 = (bf16[1,56,1024]{2,1,0:T(8,128)(2,1)S(1)}, bf16[1,56,1024]{2,1,0:T(8,128)(2,1)}, u32[]{:S(2)}) copy-start(bf16[1,56,1024]{2,1,0:T(8,128)(2,1)} %param.17) | copy-start | bytes 344068
  10.4 117.5 %copy-start.4 = (f32[1,1792]{1,0:T(1,128)S(1)}, f32[1,1792]{1,0:T(1,128)}, u32[]{:S(2)}) copy-start(f32[1,1792]{1,0:T(1,128)} %param.19) | copy-start | bytes 21508
  10.4 162.6 %copy-start.2 = (bf16[2,1,64,1792]{3,2,1,0:T(8,128)(2,1)S(1)}, bf16[2,1,64,1792]{3,2,1,0:T(8,128)(2,1)}, u32[]{:S(2)}) copy-start(bf16[2,1,64,1792]{3,2,1,0:T(8,128)(2,1)} %param.15) | copy-start | bytes 1376260
  10.4 162.5 %all-to-all-start = ((bf16[32,32,1792]{2,1,0:T(8,128)(2,1)}), bf16[32,32,1792]{2,1,0:T(8,128)(2,1)}, u32[]{:S(2)}, u32[]{:S(2)}) async-start(bf16[32,32,1792]{2,1,0:T(8,128)(2,1)} %broadcast_in_dim.63), calls=%async_computation | async-start | bytes 7340032 | tf_op jit(solution)/shard_map/all_to_all | solution.py:172
  22.1 150.8 %all-gather.4.cloned.1.call-start = ((), (), s32[]{:S(2)}) async-start(), calls=%async_computation.6 | async-start | bytes 4587520 | tf_op jit(solution)/shard_map/all_gather | solution.py:166
  127.9 405.1 %reduce-scatter.3.cloned.1.call-start = ((), (), s32[]{:S(2)}) async-start(), calls=%async_computation.4 | async-start | bytes 4587520 | tf_op jit(solution)/shard_map/reduce_scatter | solution.py:177
  173.0 98.5 %copy-start.3 = (bf16[2,1,64,1792]{3,2,1,0:T(8,128)(2,1)S(1)}, bf16[2,1,64,1792]{3,2,1,0:T(8,128)(2,1)}, u32[]{:S(2)}) copy-start(bf16[2,1,64,1792]{3,2,1,0:T(8,128)(2,1)} %param.16) | copy-start | bytes 1376260
  173.9 7.3 %collective-permute-start = (bf16[64,1792]{1,0:T(8,128)(2,1)S(1)}, bf16[64,1792]{1,0:T(8,128)(2,1)S(1)}, u32[]{:S(2)}, u32[]{:S(2)}) collective-permute-start(bf16[64,1792]{1,0:T(8,128)(2,1)S(1)} %get-tuple-element.751), channel_id=1, source_target_pairs={{0,32},{32,64},{64,96},{96,128},{128,160},{160,192},{192,224},{1,3... | collective-permute-start | bytes 688136 | tf_op jit(solution)/shard_map/while/body/eval_jaxpr/ppermute | solution.py:12
  182.1 7.3 %collective-permute-start = (bf16[64,1792]{1,0:T(8,128)(2,1)S(1)}, bf16[64,1792]{1,0:T(8,128)(2,1)S(1)}, u32[]{:S(2)}, u32[]{:S(2)}) collective-permute-start(bf16[64,1792]{1,0:T(8,128)(2,1)S(1)} %get-tuple-element.751), channel_id=1, source_target_pairs={{0,32},{32,64},{64,96},{96,128},{128,160},{160,192},{192,224},{1,3... | collective-permute-start | bytes 688136 | tf_op jit(solution)/shard_map/while/body/eval_jaxpr/ppermute | solution.py:12
  190.2 7.3 %collective-permute-start = (bf16[64,1792]{1,0:T(8,128)(2,1)S(1)}, bf16[64,1792]{1,0:T(8,128)(2,1)S(1)}, u32[]{:S(2)}, u32[]{:S(2)}) collective-permute-start(bf16[64,1792]{1,0:T(8,128)(2,1)S(1)} %get-tuple-element.751), channel_id=1, source_target_pairs={{0,32},{32,64},{64,96},{96,128},{128,160},{160,192},{192,224},{1,3... | collective-permute-start | bytes 688136 | tf_op jit(solution)/shard_map/while/body/eval_jaxpr/ppermute | solution.py:12
  198.4 19.2 %collective-permute-start = (bf16[64,1792]{1,0:T(8,128)(2,1)S(1)}, bf16[64,1792]{1,0:T(8,128)(2,1)S(1)}, u32[]{:S(2)}, u32[]{:S(2)}) collective-permute-start(bf16[64,1792]{1,0:T(8,128)(2,1)S(1)} %get-tuple-element.751), channel_id=1, source_target_pairs={{0,32},{32,64},{64,96},{96,128},{128,160},{160,192},{192,224},{1,3... | collective-permute-start | bytes 688136 | tf_op jit(solution)/shard_map/while/body/eval_jaxpr/ppermute | solution.py:12
  224.3 7.3 %collective-permute-start = (bf16[64,1792]{1,0:T(8,128)(2,1)S(1)}, bf16[64,1792]{1,0:T(8,128)(2,1)S(1)}, u32[]{:S(2)}, u32[]{:S(2)}) collective-permute-start(bf16[64,1792]{1,0:T(8,128)(2,1)S(1)} %get-tuple-element.751), channel_id=1, source_target_pairs={{0,32},{32,64},{64,96},{96,128},{128,160},{160,192},{192,224},{1,3... | collective-permute-start | bytes 688136 | tf_op jit(solution)/shard_map/while/body/eval_jaxpr/ppermute | solution.py:12
  238.4 7.3 %collective-permute-start = (bf16[64,1792]{1,0:T(8,128)(2,1)S(1)}, bf16[64,1792]{1,0:T(8,128)(2,1)S(1)}, u32[]{:S(2)}, u32[]{:S(2)}) collective-permute-start(bf16[64,1792]{1,0:T(8,128)(2,1)S(1)} %get-tuple-element.751), channel_id=1, source_target_pairs={{0,32},{32,64},{64,96},{96,128},{128,160},{160,192},{192,224},{1,3... | collective-permute-start | bytes 688136 | tf_op jit(solution)/shard_map/while/body/eval_jaxpr/ppermute | solution.py:12
  246.5 7.3 %collective-permute-start = (bf16[64,1792]{1,0:T(8,128)(2,1)S(1)}, bf16[64,1792]{1,0:T(8,128)(2,1)S(1)}, u32[]{:S(2)}, u32[]{:S(2)}) collective-permute-start(bf16[64,1792]{1,0:T(8,128)(2,1)S(1)} %get-tuple-element.751), channel_id=1, source_target_pairs={{0,32},{32,64},{64,96},{96,128},{128,160},{160,192},{192,224},{1,3... | collective-permute-start | bytes 688136 | tf_op jit(solution)/shard_map/while/body/eval_jaxpr/ppermute | solution.py:12
  254.7 7.3 %collective-permute-start = (bf16[64,1792]{1,0:T(8,128)(2,1)S(1)}, bf16[64,1792]{1,0:T(8,128)(2,1)S(1)}, u32[]{:S(2)}, u32[]{:S(2)}) collective-permute-start(bf16[64,1792]{1,0:T(8,128)(2,1)S(1)} %get-tuple-element.751), channel_id=1, source_target_pairs={{0,32},{32,64},{64,96},{96,128},{128,160},{160,192},{192,224},{1,3... | collective-permute-start | bytes 688136 | tf_op jit(solution)/shard_map/while/body/eval_jaxpr/ppermute | solution.py:12
  262.9 8.4 %collective-permute-start = (bf16[64,1792]{1,0:T(8,128)(2,1)S(1)}, bf16[64,1792]{1,0:T(8,128)(2,1)S(1)}, u32[]{:S(2)}, u32[]{:S(2)}) collective-permute-start(bf16[64,1792]{1,0:T(8,128)(2,1)S(1)} %get-tuple-element.751), channel_id=1, source_target_pairs={{0,32},{32,64},{64,96},{96,128},{128,160},{160,192},{192,224},{1,3... | collective-permute-start | bytes 688136 | tf_op jit(solution)/shard_map/while/body/eval_jaxpr/ppermute | solution.py:12
  271.7 7.2 %collective-permute-start.1 = (bf16[64,1792]{1,0:T(8,128)(2,1)S(1)}, bf16[64,1792]{1,0:T(8,128)(2,1)S(1)}, u32[]{:S(2)}, u32[]{:S(2)}) collective-permute-start(bf16[64,1792]{1,0:T(8,128)(2,1)S(1)} %get-tuple-element.768), channel_id=1, source_target_pairs={{32,0},{64,32},{96,64},{128,96},{160,128},{192,160},{224,192},{33,... | collective-permute-start | bytes 688136 | tf_op jit(solution)/shard_map/while/body/eval_jaxpr/ppermute | solution.py:12
  279.1 8.1 %collective-permute-start.1 = (bf16[64,1792]{1,0:T(8,128)(2,1)S(1)}, bf16[64,1792]{1,0:T(8,128)(2,1)S(1)}, u32[]{:S(2)}, u32[]{:S(2)}) collective-permute-start(bf16[64,1792]{1,0:T(8,128)(2,1)S(1)} %get-tuple-element.768), channel_id=1, source_target_pairs={{32,0},{64,32},{96,64},{128,96},{160,128},{192,160},{224,192},{33,... | collective-permute-start | bytes 688136 | tf_op jit(solution)/shard_map/while/body/eval_jaxpr/ppermute | solution.py:12
  287.4 42.1 %collective-permute-start.1 = (bf16[64,1792]{1,0:T(8,128)(2,1)S(1)}, bf16[64,1792]{1,0:T(8,128)(2,1)S(1)}, u32[]{:S(2)}, u32[]{:S(2)}) collective-permute-start(bf16[64,1792]{1,0:T(8,128)(2,1)S(1)} %get-tuple-element.768), channel_id=1, source_target_pairs={{32,0},{64,32},{96,64},{128,96},{160,128},{192,160},{224,192},{33,... | collective-permute-start | bytes 688136 | tf_op jit(solution)/shard_map/while/body/eval_jaxpr/ppermute | solution.py:12
  333.1 6.5 %copy-start = (bf16[64,1024]{1,0:T(8,128)(2,1)}, bf16[64,1024]{1,0:T(8,128)(2,1)S(1)}, u32[]{:S(2)}) copy-start(bf16[64,1024]{1,0:T(8,128)(2,1)S(1)} %convolution_convert_fusion.1) | copy-start | bytes 393220 | tf_op jit(solution)/shard_map/while/body/eval_jaxpr/cond
  339.7 4.1 copy-start.1
  343.7 7.3 %collective-permute-start.1 = (bf16[64,1792]{1,0:T(8,128)(2,1)S(1)}, bf16[64,1792]{1,0:T(8,128)(2,1)S(1)}, u32[]{:S(2)}, u32[]{:S(2)}) collective-permute-start(bf16[64,1792]{1,0:T(8,128)(2,1)S(1)} %get-tuple-element.768), channel_id=1, source_target_pairs={{32,0},{64,32},{96,64},{128,96},{160,128},{192,160},{224,192},{33,... | collective-permute-start | bytes 688136 | tf_op jit(solution)/shard_map/while/body/eval_jaxpr/ppermute | solution.py:12
  354.7 6.5 %copy-start = (bf16[64,1024]{1,0:T(8,128)(2,1)}, bf16[64,1024]{1,0:T(8,128)(2,1)S(1)}, u32[]{:S(2)}) copy-start(bf16[64,1024]{1,0:T(8,128)(2,1)S(1)} %convolution_convert_fusion.1) | copy-start | bytes 393220 | tf_op jit(solution)/shard_map/while/body/eval_jaxpr/cond
  365.2 5.4 collective-permute-start.1
  370.9 21.3 %collective-permute-start.1 = (bf16[64,1792]{1,0:T(8,128)(2,1)S(1)}, bf16[64,1792]{1,0:T(8,128)(2,1)S(1)}, u32[]{:S(2)}, u32[]{:S(2)}) collective-permute-start(bf16[64,1792]{1,0:T(8,128)(2,1)S(1)} %get-tuple-element.768), channel_id=1, source_target_pairs={{32,0},{64,32},{96,64},{128,96},{160,128},{192,160},{224,192},{33,... | collective-permute-start | bytes 688136 | tf_op jit(solution)/shard_map/while/body/eval_jaxpr/ppermute | solution.py:12
  392.4 7.3 %collective-permute-start.1 = (bf16[64,1792]{1,0:T(8,128)(2,1)S(1)}, bf16[64,1792]{1,0:T(8,128)(2,1)S(1)}, u32[]{:S(2)}, u32[]{:S(2)}) collective-permute-start(bf16[64,1792]{1,0:T(8,128)(2,1)S(1)} %get-tuple-element.768), channel_id=1, source_target_pairs={{32,0},{64,32},{96,64},{128,96},{160,128},{192,160},{224,192},{33,... | collective-permute-start | bytes 688136 | tf_op jit(solution)/shard_map/while/body/eval_jaxpr/ppermute | solution.py:12
  399.9 13.4 %collective-permute-start.1 = (bf16[64,1792]{1,0:T(8,128)(2,1)S(1)}, bf16[64,1792]{1,0:T(8,128)(2,1)S(1)}, u32[]{:S(2)}, u32[]{:S(2)}) collective-permute-start(bf16[64,1792]{1,0:T(8,128)(2,1)S(1)} %get-tuple-element.768), channel_id=1, source_target_pairs={{32,0},{64,32},{96,64},{128,96},{160,128},{192,160},{224,192},{33,... | collective-permute-start | bytes 688136 | tf_op jit(solution)/shard_map/while/body/eval_jaxpr/ppermute | solution.py:12
  413.5 7.3 %collective-permute-start.1 = (bf16[64,1792]{1,0:T(8,128)(2,1)S(1)}, bf16[64,1792]{1,0:T(8,128)(2,1)S(1)}, u32[]{:S(2)}, u32[]{:S(2)}) collective-permute-start(bf16[64,1792]{1,0:T(8,128)(2,1)S(1)} %get-tuple-element.768), channel_id=1, source_target_pairs={{32,0},{64,32},{96,64},{128,96},{160,128},{192,160},{224,192},{33,... | collective-permute-start | bytes 688136 | tf_op jit(solution)/shard_map/while/body/eval_jaxpr/ppermute | solution.py:12
  460.9 93.5 %all-to-all-start.1 = ((bf16[32,32,1792]{2,1,0:T(8,128)(2,1)}), bf16[32,32,1792]{2,1,0:T(8,128)(2,1)}, u32[]{:S(2)}, u32[]{:S(2)}) async-start(bf16[32,32,1792]{2,1,0:T(8,128)(2,1)} %bitcast.99), calls=%async_computation.3 | async-start | bytes 7340032 | tf_op jit(solution)/shard_map/all_to_all | solution.py:184
  469.8 87.1 %copy-start.6 = (f32[1,32,1792]{2,1,0:T(8,128)S(1)}, f32[1,32,1792]{2,1,0:T(8,128)}, u32[]{:S(2)}) copy-start(f32[1,32,1792]{2,1,0:T(8,128)} %param.21) | copy-start | bytes 688132
  469.9 110.7 %copy-start.5 = (f32[1,56,1024]{2,1,0:T(8,128)S(1)}, f32[1,56,1024]{2,1,0:T(8,128)}, u32[]{:S(2)}) copy-start(f32[1,56,1024]{2,1,0:T(8,128)} %param.20) | copy-start | bytes 688132
  469.9 110.7 %reduce-scatter.5.cloned.1.call-start = ((), (), s32[]{:S(2)}) async-start(), calls=%async_computation.5 | async-start | bytes 1032192 | tf_op jit(solution)/shard_map/reduce_scatter | solution.py:178
  (1 other events, 4.1 us)
Sparse Core Ops, SparseCore 0:
  128.0 44.8 all-gather.3
  457.9 74.9 reduce-scatter.2
  535.5 45.0 reduce-scatter.4

commit v2 on v1

--- a/solution.py
+++ b/solution.py
@@ -43,8 +43,9 @@
 def example_sums(left, right, seq_len):
     first = left.reshape(-1, seq_len, left.shape[-1])
     second = right.reshape(-1, seq_len, right.shape[-1])
-    per_example = jnp.einsum("eth,etd->ehd", first, second, preferred_element_type=jnp.float32)
-    return jnp.sum(per_example * per_example, axis=(1, 2))
+    gram_first = jnp.einsum("eth,esh->ets", first, first, preferred_element_type=jnp.float32)
+    gram_second = jnp.einsum("eth,esh->ets", second, second, preferred_element_type=jnp.float32)
+    return jnp.sum(gram_first * gram_second, axis=(1, 2))
 
 
 def forward_chain(feed_rows, gains, value_matrix, output_matrix):
@@ -98,7 +99,6 @@
     section_place = lax.axis_index("section")
     micro_count, row_count, feature_width = kept_inputs.shape
     head_width = kept_values.shape[-1]
-    example_here = row_count // seq_len
     last_place = section_count - 1
 
     def backward_active_step(operands):
@@ -106,20 +106,16 @@
         normed, dvalues, before = layer_backward(
             inputs_here, grad_here, gains, value_matrix, output_matrix
         )
-        squares = example_sums(normed, dvalues, seq_len) + example_sums(
-            values_here, grad_here, seq_len
-        )
-        return (before, dvalues, squares)
+        return (before, dvalues)
 
     def backward_spare_step(operands):
         return (
             jnp.zeros((row_count, feature_width), jnp.bfloat16),
             jnp.zeros((row_count, head_width), jnp.bfloat16),
-            jnp.zeros((example_here,), jnp.float32),
         )
 
     def backward_time_step(counter, carried):
-        incoming, kept_grads, kept_dvalues, squares_all = carried
+        incoming, kept_grads, kept_dvalues = carried
         which_micro = counter - (last_place - section_place)
         active = (which_micro >= 0) & (which_micro < micro_count)
         slot_index = jnp.clip(which_micro, 0, micro_count - 1)
@@ -130,40 +126,30 @@
         )
         inputs_here = lax.dynamic_index_in_dim(kept_inputs, slot_index, 0, keepdims=False)
         values_here = lax.dynamic_index_in_dim(kept_values, slot_index, 0, keepdims=False)
-        before, dvalues, squares = lax.cond(
+        before, dvalues = lax.cond(
             active, backward_active_step, backward_spare_step, (inputs_here, values_here, grad_here)
         )
         old_grads = lax.dynamic_index_in_dim(kept_grads, slot_index, 0, keepdims=False)
         old_dvalues = lax.dynamic_index_in_dim(kept_dvalues, slot_index, 0, keepdims=False)
-        old_squares = lax.dynamic_index_in_dim(squares_all, slot_index, 0, keepdims=False)
         kept_grads = lax.dynamic_update_index_in_dim(
             kept_grads, jnp.where(active, grad_here, old_grads), slot_index, 0
         )
         kept_dvalues = lax.dynamic_update_index_in_dim(
             kept_dvalues, jnp.where(active, dvalues, old_dvalues), slot_index, 0
         )
-        squares_all = lax.dynamic_update_index_in_dim(
-            squares_all, jnp.where(active, squares, old_squares), slot_index, 0
-        )
         incoming = from_behind(before, "section", -1)
-        return (incoming, kept_grads, kept_dvalues, squares_all)
+        return (incoming, kept_grads, kept_dvalues)
 
     start_state = (
         jnp.zeros((row_count, feature_width), jnp.bfloat16),
         jnp.zeros((micro_count, row_count, feature_width), jnp.bfloat16),
         jnp.zeros((micro_count, row_count, head_width), jnp.bfloat16),
-        jnp.zeros((micro_count, example_here), jnp.float32),
     )
     final_state = lax.fori_loop(0, section_count + micro_count - 1, backward_time_step, start_state)
-    return (final_state[1], final_state[2], final_state[3])
+    return (final_state[1], final_state[2])
 
 
 DP = ("y", "z")
-
-
-def gather_rows(shard):
-    inner = lax.all_gather(shard, "z", axis=0, tiled=True)
-    return lax.all_gather(inner, "y", axis=0, tiled=True)
 
 
 def exchange_rows(shard):
@@ -189,13 +175,24 @@
     micro_count, example_count, seq_len, feature_width = inputs.shape
     feed_rows = inputs.reshape(micro_count, example_count * seq_len, feature_width)
     cot_rows = cotangent.reshape(micro_count, example_count * seq_len, feature_width)
-    value_matrix = gather_rows(value_weight[0])
+    value_matrix = lax.all_gather(value_weight[0], DP, axis=0, tiled=True)
     output_matrix = exchange_rows(output_weight[0])
     head_width = value_matrix.shape[1]
     gains = norm_gain[0]
     kept_inputs, kept_values = forward_chain(feed_rows, gains, value_matrix, output_matrix)
-    kept_grads, kept_dvalues, partial_squares = backward_chain(
+    kept_grads, kept_dvalues = backward_chain(
         kept_inputs, kept_values, cot_rows, gains, value_matrix, output_matrix, seq_len
+    )
+    unused_wide, unused_inverse, normed_rows = norm_parts(
+        kept_inputs.reshape(-1, feature_width), gains
+    )
+    normed_kept = normed_rows.reshape(kept_inputs.shape)
+    partial_squares = jnp.stack(
+        [
+            example_sums(normed_kept[m], kept_dvalues[m], seq_len)
+            + example_sums(kept_values[m], kept_grads[m], seq_len)
+            for m in range(micro_count)
+        ]
     )
     total_squares = lax.psum(partial_squares, "section")
     clip_weight = 1.0 / (jnp.sqrt(total_squares) + 0.01)
@@ -209,9 +206,6 @@
         (kept_grads.astype(jnp.float32) * token_weight)
         .astype(jnp.bfloat16)
         .reshape(-1, feature_width)
-    )
-    unused_wide, unused_inverse, normed_rows = norm_parts(
-        kept_inputs.reshape(-1, feature_width), gains
     )
     value_rows = kept_values.reshape(-1, head_width)
     columns = normed_rows

time: 590 us -> 498 us (0.84)
  blocking collectives: 139 us -> 20.1 us
  waiting for transfers between devices: 266 us -> 319 us
  starting transfers between devices: 90.3 us -> 75.5 us
  loops' own time: 9.86 us -> 1.15 us
    all_gather x1 -> x0, blocking collectives: 106 us -> none  [gather_rows(): inner = lax.all_gather(shard, 'z', axis=0, tiled=True)]
    all_to_all x1, waiting for transfers between devices: 0.01 us -> 94.2 us  [exchange_rows(): parts = lax.all_to_all(copies, DP, 0, 0, tiled=False)]
    all_gather x1, waiting for transfers between devices: 44.9 us -> 13.9 us  [on_device(): value_matrix = lax.all_gather(value_weight[0], DP, axis=0, tiled=True)]
    psum x1, blocking collectives: 33.8 us -> 20.1 us  [on_device(): total_squares = lax.psum(partial_squares, 'section')]
    ppermute x18, starting transfers between devices: 69.5 us -> 56.5 us  [from_behind(): return lax.ppermute(block, axis, route)]
    ppermute x18, waiting for transfers between devices: 114 us -> 103 us  [from_behind(): return lax.ppermute(block, axis, route)]
    dot_general x4 -> x8, matrix products: 11.2 us -> 3.96 us  [the longest x4 2.02 us: example_sums(): jnp.einsum('eth,esh->ets', first, first, preferred_element_type=jnp.float32)]
    another operation x1, loops' own time: 6.3 us -> 0.35 us  [backward_chain(): lax.fori_loop(0, section_count + micro_count - 1, backward_time_step, sta...]
  transfers between devices with their start and end apart: 23 -> 23, of which waited for: 22 -> 23; matrix products, arithmetic and copies ran while one was open for 3% -> 2% of each run, Pallas kernels for 0% -> 0%
where the time goes in v2:
time: 498 us; the launch traced here: 497 us
  waiting for transfers between devices  319 us (64%)
  starting transfers between devices  75.5 us (15%)
  matrix products  37.6 us (8%)
  blocking collectives  20.1 us (4%)
  between operations  16.5 us (3%)
  local copies, waits for them, and re-layouts  13.7 us (3%)
  other arithmetic  12.8 us (3%)
    ppermute x18, waiting for transfers between devices, from_behind(): return lax.ppermute(block, axis, route)  103 us
    all_to_all x1, waiting for transfers between devices, exchange_rows(): parts = lax.all_to_all(copies, DP, 0, 0, tiled=False)  94.2 us
    reduce_scatter x1, waiting for transfers between devices, scatter_in_stages(): inner = lax.psum_scatter(block, 'y', scatter_dimension=0, tiled=True)  63 us
    ppermute x18, starting transfers between devices, from_behind(): return lax.ppermute(block, axis, route)  56.5 us
    reduce_scatter x1, waiting for transfers between devices, scatter_in_stages(): lax.psum_scatter(inner, 'z', scatter_dimension=0, tiled=True)  22.8 us
    all_to_all x1, waiting for transfers between devices, scatter_by_exchange(): arrived = lax.all_to_all(parts, DP, 0, 0, tiled=False)  21.5 us
    psum x1, blocking collectives, on_device(): total_squares = lax.psum(partial_squares, 'section')  20.1 us
    all_gather x1, waiting for transfers between devices, on_device(): value_matrix = lax.all_gather(value_weight[0], DP, axis=0, tiled=True)  13.9 us
  transfers between devices with their start and end apart: 23, of which 23 were waited for; matrix products, arithmetic and copies ran while one was open for 2% of the time, Pallas kernels for 0%

profile of v2, /device:TPU:4, one launch (start us, length us, event | category | flops | bytes accessed | tf_op | source)
XLA Modules:
  0.0 496.6 jit_solution(14034924475920169265)
XLA Ops:
  10.4 11.7 %all-to-all-start = ((bf16[32,32,1792]{2,1,0:T(8,128)(2,1)}), bf16[32,32,1792]{2,1,0:T(8,128)(2,1)}, u32[]{:S(2)}, u32[]{:S(2)}) async-start(bf16[32,32,1792]{2,1,0:T(8,128)(2,1)} %broadcast_in_dim.53), calls=%async_computation | async-start | bytes 7340032 | tf_op jit(solution)/shard_map/all_to_all | solution.py:158
  23.0 94.2 %all-to-all-done = bf16[32,32,1792]{2,1,0:T(8,128)(2,1)} async-done(((bf16[32,32,1792]{2,1,0:T(8,128)(2,1)}), bf16[32,32,1792]{2,1,0:T(8,128)(2,1)}, u32[]{:S(2)}, u32[]{:S(2)}) %all-to-all-start) | async-done | bytes 3670048 | tf_op jit(solution)/shard_map/all_to_all | solution.py:158
  117.1 13.9 %all-gather.3.cloned.1.call-done = bf16[1,1792,1024]{2,1,0:T(8,128)(2,1)} async-done(((bf16[1,56,1024]{2,1,0:T(8,128)(2,1)}), bf16[1,1792,1024]{2,1,0:T(8,128)(2,1)}) %all-gather.3.cloned.1.call-update) | async-done | bytes 3670032 | tf_op jit(solution)/shard_map/all_gather | solution.py:178
  131.1 98.1 %while.37 = (s32[]{:T(128)}, bf16[64,1792]{1,0:T(8,128)(2,1)S(1)}, bf16[2,64,1792]{2,1,0:T(8,128)(2,1)S(1)}, bf16[2,64,1024]{2,1,0:T(8,128)(2,1)S(1)}, s32[]{:T(...) while((s32[]{:T(128)}, bf16[64,1792]{1,0:T(8,128)(2,1)S(1)}, ...), condition=%wide.region_4.5_spmd, body=%wide.region_0.4_spmd.sunk | while | flops 471269440 | bytes 11721002 | solution.py:93
  134.0 5.3 %collective-permute-done = bf16[64,1792]{1,0:T(8,128)(2,1)S(1)} collective-permute-done((bf16[64,1792]{1,0:T(8,128)(2,1)S(1)}, bf16[64,1792]{1,0:T(8,128)(2,1)S(1)}, u32[]{:S(2)}, u32[]{:S(2)}) %collective-permute-start) | collective-permute-done | bytes 229408 | tf_op jit(solution)/shard_map/while/body/eval_jaxpr/ppermute | solution.py:12
  142.1 5.3 %collective-permute-done = bf16[64,1792]{1,0:T(8,128)(2,1)S(1)} collective-permute-done((bf16[64,1792]{1,0:T(8,128)(2,1)S(1)}, bf16[64,1792]{1,0:T(8,128)(2,1)S(1)}, u32[]{:S(2)}, u32[]{:S(2)}) %collective-permute-start) | collective-permute-done | bytes 229408 | tf_op jit(solution)/shard_map/while/body/eval_jaxpr/ppermute | solution.py:12
  150.3 5.3 %collective-permute-done = bf16[64,1792]{1,0:T(8,128)(2,1)S(1)} collective-permute-done((bf16[64,1792]{1,0:T(8,128)(2,1)S(1)}, bf16[64,1792]{1,0:T(8,128)(2,1)S(1)}, u32[]{:S(2)}, u32[]{:S(2)}) %collective-permute-start) | collective-permute-done | bytes 229408 | tf_op jit(solution)/shard_map/while/body/eval_jaxpr/ppermute | solution.py:12
  158.4 17.2 %collective-permute-done = bf16[64,1792]{1,0:T(8,128)(2,1)S(1)} collective-permute-done((bf16[64,1792]{1,0:T(8,128)(2,1)S(1)}, bf16[64,1792]{1,0:T(8,128)(2,1)S(1)}, u32[]{:S(2)}, u32[]{:S(2)}) %collective-permute-start) | collective-permute-done | bytes 229408 | tf_op jit(solution)/shard_map/while/body/eval_jaxpr/ppermute | solution.py:12
  175.7 6.6 %conditional.4 = (bf16[64,1024]{1,0:T(8,128)(2,1)}, bf16[64,1792]{1,0:T(8,128)(2,1)S(1)}) conditional(s32[]{:T(128)} %convert_element_type.143, () %tuple.93, (bf16[64,1792]{1,0:T(8,128)(2,1)S(1)}, f32[1,1792]{1,0:T(1,128)S(1)}, bf16[1792,1024]{1,0:T(8,128)(2,1)}, bf16[1024,1792]{1,0:T(8,128)(2,1)}) %tuple.94), branch_computations={%region_1.1_spmd, %region_2.3_spmd} | conditional | flops 470974528 | bytes 8542228 | solution.py:76
  185.2 4.4 collective-permute-done
  189.8 6.6 %conditional.4 = (bf16[64,1024]{1,0:T(8,128)(2,1)}, bf16[64,1792]{1,0:T(8,128)(2,1)S(1)}) conditional(s32[]{:T(128)} %convert_element_type.143, () %tuple.93, (bf16[64,1792]{1,0:T(8,128)(2,1)S(1)}, f32[1,1792]{1,0:T(1,128)S(1)}, bf16[1792,1024]{1,0:T(8,128)(2,1)}, bf16[1024,1792]{1,0:T(8,128)(2,1)}) %tuple.94), branch_computations={%region_1.1_spmd, %region_2.3_spmd} | conditional | flops 470974528 | bytes 8542228 | solution.py:76
  199.3 4.4 collective-permute-done
  204.5 3.8 collective-permute-start
  214.7 5.3 %collective-permute-done = bf16[64,1792]{1,0:T(8,128)(2,1)S(1)} collective-permute-done((bf16[64,1792]{1,0:T(8,128)(2,1)S(1)}, bf16[64,1792]{1,0:T(8,128)(2,1)S(1)}, u32[]{:S(2)}, u32[]{:S(2)}) %collective-permute-start) | collective-permute-done | bytes 229408 | tf_op jit(solution)/shard_map/while/body/eval_jaxpr/ppermute | solution.py:12
  220.9 7.3 %collective-permute-start = (bf16[64,1792]{1,0:T(8,128)(2,1)S(1)}, bf16[64,1792]{1,0:T(8,128)(2,1)S(1)}, u32[]{:S(2)}, u32[]{:S(2)}) collective-permute-start(bf16[64,1792]{1,0:T(8,128)(2,1)S(1)} %get-tuple-element.664), channel_id=1, source_target_pairs={{0,32},{32,64},{64,96},{96,128},{128,160},{160,192},{192,224},{1,3... | collective-permute-start | bytes 688136 | tf_op jit(solution)/shard_map/while/body/eval_jaxpr/ppermute | solution.py:12
  230.2 107.9 %while.38 = (s32[]{:T(128)}, bf16[64,1792]{1,0:T(8,128)(2,1)S(1)}, bf16[2,64,1792]{2,1,0:T(8,128)(2,1)S(1)}, bf16[2,64,1024]{2,1,0:T(8,128)(2,1)S(1)}, s32[]{:T(...) while((s32[]{:T(128)}, bf16[64,1792]{1,0:T(8,128)(2,1)S(1)}, ...), condition=%wide.region_11.12_spmd, body=%wide.region_6.11_spmd.sunk | while | flops 471957568 | bytes 13098574 | solution.py:148
  233.1 5.2 %collective-permute-done.1 = bf16[64,1792]{1,0:T(8,128)(2,1)S(1)} collective-permute-done((bf16[64,1792]{1,0:T(8,128)(2,1)S(1)}, bf16[64,1792]{1,0:T(8,128)(2,1)S(1)}, u32[]{:S(2)}, u32[]{:S(2)}) %collective-permute-start.1) | collective-permute-done | bytes 229408 | tf_op jit(solution)/shard_map/while/body/eval_jaxpr/ppermute | solution.py:12
  241.2 6.0 %collective-permute-done.1 = bf16[64,1792]{1,0:T(8,128)(2,1)S(1)} collective-permute-done((bf16[64,1792]{1,0:T(8,128)(2,1)S(1)}, bf16[64,1792]{1,0:T(8,128)(2,1)S(1)}, u32[]{:S(2)}, u32[]{:S(2)}) %collective-permute-start.1) | collective-permute-done | bytes 229408 | tf_op jit(solution)/shard_map/while/body/eval_jaxpr/ppermute | solution.py:12
  250.0 19.6 %collective-permute-done.1 = bf16[64,1792]{1,0:T(8,128)(2,1)S(1)} collective-permute-done((bf16[64,1792]{1,0:T(8,128)(2,1)S(1)}, bf16[64,1792]{1,0:T(8,128)(2,1)S(1)}, u32[]{:S(2)}, u32[]{:S(2)}) %collective-permute-start.1) | collective-permute-done | bytes 229408 | tf_op jit(solution)/shard_map/while/body/eval_jaxpr/ppermute | solution.py:12
  269.8 7.8 %conditional.5 = (bf16[64,1792]{1,0:T(8,128)(2,1)S(1)}, bf16[64,1024]{1,0:T(8,128)(2,1)}) conditional(s32[]{:T(128)} %convert_element_type.144, () %tuple.97, (bf16[64,1792]{1,0:T(8,128)(2,1)S(1)}, bf16[2,64,1792]{2,1,0:T(8,128)(2,1)S(1)}, s32[]{:T(128)}, bf16[1024,1792]{1,0:T(8,128)(2,1)}, bf16[1792,1024]{1,0:T(8,128)(2,1)}, ...), branch_computations={%region_7.7_spmd, %region_8.10_spmd} | conditional | flops 471662656 | bytes 9919776 | solution.py:129
  269.9 3.9 convolution_convert_fusion.1
  280.5 4.4 collective-permute-done.1
  285.1 7.8 %conditional.5 = (bf16[64,1792]{1,0:T(8,128)(2,1)S(1)}, bf16[64,1024]{1,0:T(8,128)(2,1)}) conditional(s32[]{:T(128)} %convert_element_type.144, () %tuple.97, (bf16[64,1792]{1,0:T(8,128)(2,1)S(1)}, bf16[2,64,1792]{2,1,0:T(8,128)(2,1)S(1)}, s32[]{:T(128)}, bf16[1024,1792]{1,0:T(8,128)(2,1)}, bf16[1792,1024]{1,0:T(8,128)(2,1)}, ...), branch_computations={%region_7.7_spmd, %region_8.10_spmd} | conditional | flops 471662656 | bytes 9919776 | solution.py:129
  285.2 3.9 convolution_convert_fusion.1
  299.2 10.9 %collective-permute-start.1 = (bf16[64,1792]{1,0:T(8,128)(2,1)S(1)}, bf16[64,1792]{1,0:T(8,128)(2,1)S(1)}, u32[]{:S(2)}, u32[]{:S(2)}) collective-permute-start(bf16[64,1792]{1,0:T(8,128)(2,1)S(1)} %get-tuple-element.679), channel_id=1, source_target_pairs={{32,0},{64,32},{96,64},{128,96},{160,128},{192,160},{224,192},{33,... | collective-permute-start | bytes 688136 | tf_op jit(solution)/shard_map/while/body/eval_jaxpr/ppermute | solution.py:12
  314.4 3.8 collective-permute-start.1
  330.8 3.8 collective-permute-start.1
  344.3 20.1 %psum.7 = f32[2,1]{0,1:T(1,128)S(1)} all-reduce(f32[2,1]{0,1:T(1,128)S(1)} %pad_maximum_fusion), channel_id=1, replica_groups=mesh['section'=8,'y'=4,'z'=8] {'section'}, use_global_device_ids=true, to_apply=%region_16.17 | all-reduce | flops 2 | bytes 16 | tf_op jit(solution)/shard_map/psum | solution.py:197
  370.6 7.1 %all-to-all-start.1 = ((bf16[32,32,1792]{2,1,0:T(8,128)(2,1)}), bf16[32,32,1792]{2,1,0:T(8,128)(2,1)}, u32[]{:S(2)}, u32[]{:S(2)}) async-start(bf16[32,32,1792]{2,1,0:T(8,128)(2,1)} %bitcast.106), calls=%async_computation.3 | async-start | bytes 7340032 | tf_op jit(solution)/shard_map/all_to_all | solution.py:170
  377.8 63.0 %reduce-scatter.3.cloned.1.call-done = bf16[448,1024]{1,0:T(8,128)(2,1)} async-done(((bf16[1792,1024]{1,0:T(8,128)(2,1)}), bf16[448,1024]{1,0:T(8,128)(2,1)}) %reduce-scatter.3.cloned.1.call-update) | async-done | bytes 917520 | tf_op jit(solution)/shard_map/reduce_scatter | solution.py:163
  440.8 21.5 %all-to-all-done.1 = bf16[32,32,1792]{2,1,0:T(8,128)(2,1)} async-done(((bf16[32,32,1792]{2,1,0:T(8,128)(2,1)}), bf16[32,32,1792]{2,1,0:T(8,128)(2,1)}, u32[]{:S(2)}, u32[]{:S(2)}) %all-to-all-start.1) | async-done | bytes 3670048 | tf_op jit(solution)/shard_map/all_to_all | solution.py:170
  465.6 22.8 %reduce-scatter.5.cloned.1.call-done = bf16[56,1024]{1,0:T(8,128)(2,1)} async-done(((bf16[448,1024]{1,0:T(8,128)(2,1)}), bf16[56,1024]{1,0:T(8,128)(2,1)}) %reduce-scatter.5.cloned.1.call-update) | async-done | bytes 114704 | tf_op jit(solution)/shard_map/reduce_scatter | solution.py:164
  (199 shorter events, 114.6 us)
Async XLA Ops:
  10.4 12.5 %copy-start.2 = (f32[1,1792]{1,0:T(1,128)S(1)}, f32[1,1792]{1,0:T(1,128)}, u32[]{:S(2)}) copy-start(f32[1,1792]{1,0:T(1,128)} %param.19) | copy-start | bytes 21508
  10.4 120.7 %copy-start = (bf16[2,1,64,1792]{3,2,1,0:T(8,128)(2,1)S(1)}, bf16[2,1,64,1792]{3,2,1,0:T(8,128)(2,1)}, u32[]{:S(2)}) copy-start(bf16[2,1,64,1792]{3,2,1,0:T(8,128)(2,1)} %param.15) | copy-start | bytes 1376260
  10.4 106.7 %all-to-all-start = ((bf16[32,32,1792]{2,1,0:T(8,128)(2,1)}), bf16[32,32,1792]{2,1,0:T(8,128)(2,1)}, u32[]{:S(2)}, u32[]{:S(2)}) async-start(bf16[32,32,1792]{2,1,0:T(8,128)(2,1)} %broadcast_in_dim.53), calls=%async_computation | async-start | bytes 7340032 | tf_op jit(solution)/shard_map/all_to_all | solution.py:158
  22.1 108.8 %all-gather.3.cloned.1.call-start = ((), (), s32[]{:S(2)}) async-start(), calls=%async_computation.6 | async-start | bytes 3784704 | tf_op jit(solution)/shard_map/all_gather | solution.py:178
  22.9 417.9 %reduce-scatter.3.cloned.1.call-start = ((), (), s32[]{:S(2)}) async-start(), calls=%async_computation.4 | async-start | bytes 4587520 | tf_op jit(solution)/shard_map/reduce_scatter | solution.py:163
  131.1 99.1 %copy-start.1 = (bf16[2,1,64,1792]{3,2,1,0:T(8,128)(2,1)S(1)}, bf16[2,1,64,1792]{3,2,1,0:T(8,128)(2,1)}, u32[]{:S(2)}) copy-start(bf16[2,1,64,1792]{3,2,1,0:T(8,128)(2,1)} %param.16) | copy-start | bytes 1376260
  132.0 7.3 %collective-permute-start = (bf16[64,1792]{1,0:T(8,128)(2,1)S(1)}, bf16[64,1792]{1,0:T(8,128)(2,1)S(1)}, u32[]{:S(2)}, u32[]{:S(2)}) collective-permute-start(bf16[64,1792]{1,0:T(8,128)(2,1)S(1)} %get-tuple-element.664), channel_id=1, source_target_pairs={{0,32},{32,64},{64,96},{96,128},{128,160},{160,192},{192,224},{1,3... | collective-permute-start | bytes 688136 | tf_op jit(solution)/shard_map/while/body/eval_jaxpr/ppermute | solution.py:12
  140.1 7.3 %collective-permute-start = (bf16[64,1792]{1,0:T(8,128)(2,1)S(1)}, bf16[64,1792]{1,0:T(8,128)(2,1)S(1)}, u32[]{:S(2)}, u32[]{:S(2)}) collective-permute-start(bf16[64,1792]{1,0:T(8,128)(2,1)S(1)} %get-tuple-element.664), channel_id=1, source_target_pairs={{0,32},{32,64},{64,96},{96,128},{128,160},{160,192},{192,224},{1,3... | collective-permute-start | bytes 688136 | tf_op jit(solution)/shard_map/while/body/eval_jaxpr/ppermute | solution.py:12
  148.3 7.3 %collective-permute-start = (bf16[64,1792]{1,0:T(8,128)(2,1)S(1)}, bf16[64,1792]{1,0:T(8,128)(2,1)S(1)}, u32[]{:S(2)}, u32[]{:S(2)}) collective-permute-start(bf16[64,1792]{1,0:T(8,128)(2,1)S(1)} %get-tuple-element.664), channel_id=1, source_target_pairs={{0,32},{32,64},{64,96},{96,128},{128,160},{160,192},{192,224},{1,3... | collective-permute-start | bytes 688136 | tf_op jit(solution)/shard_map/while/body/eval_jaxpr/ppermute | solution.py:12
  156.4 19.2 %collective-permute-start = (bf16[64,1792]{1,0:T(8,128)(2,1)S(1)}, bf16[64,1792]{1,0:T(8,128)(2,1)S(1)}, u32[]{:S(2)}, u32[]{:S(2)}) collective-permute-start(bf16[64,1792]{1,0:T(8,128)(2,1)S(1)} %get-tuple-element.664), channel_id=1, source_target_pairs={{0,32},{32,64},{64,96},{96,128},{128,160},{160,192},{192,224},{1,3... | collective-permute-start | bytes 688136 | tf_op jit(solution)/shard_map/while/body/eval_jaxpr/ppermute | solution.py:12
  182.3 7.3 %collective-permute-start = (bf16[64,1792]{1,0:T(8,128)(2,1)S(1)}, bf16[64,1792]{1,0:T(8,128)(2,1)S(1)}, u32[]{:S(2)}, u32[]{:S(2)}) collective-permute-start(bf16[64,1792]{1,0:T(8,128)(2,1)S(1)} %get-tuple-element.664), channel_id=1, source_target_pairs={{0,32},{32,64},{64,96},{96,128},{128,160},{160,192},{192,224},{1,3... | collective-permute-start | bytes 688136 | tf_op jit(solution)/shard_map/while/body/eval_jaxpr/ppermute | solution.py:12
  196.4 7.3 %collective-permute-start = (bf16[64,1792]{1,0:T(8,128)(2,1)S(1)}, bf16[64,1792]{1,0:T(8,128)(2,1)S(1)}, u32[]{:S(2)}, u32[]{:S(2)}) collective-permute-start(bf16[64,1792]{1,0:T(8,128)(2,1)S(1)} %get-tuple-element.664), channel_id=1, source_target_pairs={{0,32},{32,64},{64,96},{96,128},{128,160},{160,192},{192,224},{1,3... | collective-permute-start | bytes 688136 | tf_op jit(solution)/shard_map/while/body/eval_jaxpr/ppermute | solution.py:12
  204.5 7.3 %collective-permute-start = (bf16[64,1792]{1,0:T(8,128)(2,1)S(1)}, bf16[64,1792]{1,0:T(8,128)(2,1)S(1)}, u32[]{:S(2)}, u32[]{:S(2)}) collective-permute-start(bf16[64,1792]{1,0:T(8,128)(2,1)S(1)} %get-tuple-element.664), channel_id=1, source_target_pairs={{0,32},{32,64},{64,96},{96,128},{128,160},{160,192},{192,224},{1,3... | collective-permute-start | bytes 688136 | tf_op jit(solution)/shard_map/while/body/eval_jaxpr/ppermute | solution.py:12
  212.7 7.3 %collective-permute-start = (bf16[64,1792]{1,0:T(8,128)(2,1)S(1)}, bf16[64,1792]{1,0:T(8,128)(2,1)S(1)}, u32[]{:S(2)}, u32[]{:S(2)}) collective-permute-start(bf16[64,1792]{1,0:T(8,128)(2,1)S(1)} %get-tuple-element.664), channel_id=1, source_target_pairs={{0,32},{32,64},{64,96},{96,128},{128,160},{160,192},{192,224},{1,3... | collective-permute-start | bytes 688136 | tf_op jit(solution)/shard_map/while/body/eval_jaxpr/ppermute | solution.py:12
  220.9 8.4 %collective-permute-start = (bf16[64,1792]{1,0:T(8,128)(2,1)S(1)}, bf16[64,1792]{1,0:T(8,128)(2,1)S(1)}, u32[]{:S(2)}, u32[]{:S(2)}) collective-permute-start(bf16[64,1792]{1,0:T(8,128)(2,1)S(1)} %get-tuple-element.664), channel_id=1, source_target_pairs={{0,32},{32,64},{64,96},{96,128},{128,160},{160,192},{192,224},{1,3... | collective-permute-start | bytes 688136 | tf_op jit(solution)/shard_map/while/body/eval_jaxpr/ppermute | solution.py:12
  231.1 7.2 %collective-permute-start.1 = (bf16[64,1792]{1,0:T(8,128)(2,1)S(1)}, bf16[64,1792]{1,0:T(8,128)(2,1)S(1)}, u32[]{:S(2)}, u32[]{:S(2)}) collective-permute-start(bf16[64,1792]{1,0:T(8,128)(2,1)S(1)} %get-tuple-element.679), channel_id=1, source_target_pairs={{32,0},{64,32},{96,64},{128,96},{160,128},{192,160},{224,192},{33,... | collective-permute-start | bytes 688136 | tf_op jit(solution)/shard_map/while/body/eval_jaxpr/ppermute | solution.py:12
  239.1 8.1 %collective-permute-start.1 = (bf16[64,1792]{1,0:T(8,128)(2,1)S(1)}, bf16[64,1792]{1,0:T(8,128)(2,1)S(1)}, u32[]{:S(2)}, u32[]{:S(2)}) collective-permute-start(bf16[64,1792]{1,0:T(8,128)(2,1)S(1)} %get-tuple-element.679), channel_id=1, source_target_pairs={{32,0},{64,32},{96,64},{128,96},{160,128},{192,160},{224,192},{33,... | collective-permute-start | bytes 688136 | tf_op jit(solution)/shard_map/while/body/eval_jaxpr/ppermute | solution.py:12
  248.0 21.6 %collective-permute-start.1 = (bf16[64,1792]{1,0:T(8,128)(2,1)S(1)}, bf16[64,1792]{1,0:T(8,128)(2,1)S(1)}, u32[]{:S(2)}, u32[]{:S(2)}) collective-permute-start(bf16[64,1792]{1,0:T(8,128)(2,1)S(1)} %get-tuple-element.679), channel_id=1, source_target_pairs={{32,0},{64,32},{96,64},{128,96},{160,128},{192,160},{224,192},{33,... | collective-permute-start | bytes 688136 | tf_op jit(solution)/shard_map/while/body/eval_jaxpr/ppermute | solution.py:12
  277.6 7.3 %collective-permute-start.1 = (bf16[64,1792]{1,0:T(8,128)(2,1)S(1)}, bf16[64,1792]{1,0:T(8,128)(2,1)S(1)}, u32[]{:S(2)}, u32[]{:S(2)}) collective-permute-start(bf16[64,1792]{1,0:T(8,128)(2,1)S(1)} %get-tuple-element.679), channel_id=1, source_target_pairs={{32,0},{64,32},{96,64},{128,96},{160,128},{192,160},{224,192},{33,... | collective-permute-start | bytes 688136 | tf_op jit(solution)/shard_map/while/body/eval_jaxpr/ppermute | solution.py:12
  292.9 5.4 %collective-permute-start.1 = (bf16[64,1792]{1,0:T(8,128)(2,1)S(1)}, bf16[64,1792]{1,0:T(8,128)(2,1)S(1)}, u32[]{:S(2)}, u32[]{:S(2)}) collective-permute-start(bf16[64,1792]{1,0:T(8,128)(2,1)S(1)} %get-tuple-element.679), channel_id=1, source_target_pairs={{32,0},{64,32},{96,64},{128,96},{160,128},{192,160},{224,192},{33,... | collective-permute-start | bytes 688136 | tf_op jit(solution)/shard_map/while/body/eval_jaxpr/ppermute | solution.py:12
  299.2 14.4 %collective-permute-start.1 = (bf16[64,1792]{1,0:T(8,128)(2,1)S(1)}, bf16[64,1792]{1,0:T(8,128)(2,1)S(1)}, u32[]{:S(2)}, u32[]{:S(2)}) collective-permute-start(bf16[64,1792]{1,0:T(8,128)(2,1)S(1)} %get-tuple-element.679), channel_id=1, source_target_pairs={{32,0},{64,32},{96,64},{128,96},{160,128},{192,160},{224,192},{33,... | collective-permute-start | bytes 688136 | tf_op jit(solution)/shard_map/while/body/eval_jaxpr/ppermute | solution.py:12
  314.4 7.3 %collective-permute-start.1 = (bf16[64,1792]{1,0:T(8,128)(2,1)S(1)}, bf16[64,1792]{1,0:T(8,128)(2,1)S(1)}, u32[]{:S(2)}, u32[]{:S(2)}) collective-permute-start(bf16[64,1792]{1,0:T(8,128)(2,1)S(1)} %get-tuple-element.679), channel_id=1, source_target_pairs={{32,0},{64,32},{96,64},{128,96},{160,128},{192,160},{224,192},{33,... | collective-permute-start | bytes 688136 | tf_op jit(solution)/shard_map/while/body/eval_jaxpr/ppermute | solution.py:12
  322.6 7.3 %collective-permute-start.1 = (bf16[64,1792]{1,0:T(8,128)(2,1)S(1)}, bf16[64,1792]{1,0:T(8,128)(2,1)S(1)}, u32[]{:S(2)}, u32[]{:S(2)}) collective-permute-start(bf16[64,1792]{1,0:T(8,128)(2,1)S(1)} %get-tuple-element.679), channel_id=1, source_target_pairs={{32,0},{64,32},{96,64},{128,96},{160,128},{192,160},{224,192},{33,... | collective-permute-start | bytes 688136 | tf_op jit(solution)/shard_map/while/body/eval_jaxpr/ppermute | solution.py:12
  330.8 7.3 %collective-permute-start.1 = (bf16[64,1792]{1,0:T(8,128)(2,1)S(1)}, bf16[64,1792]{1,0:T(8,128)(2,1)S(1)}, u32[]{:S(2)}, u32[]{:S(2)}) collective-permute-start(bf16[64,1792]{1,0:T(8,128)(2,1)S(1)} %get-tuple-element.679), channel_id=1, source_target_pairs={{32,0},{64,32},{96,64},{128,96},{160,128},{192,160},{224,192},{33,... | collective-permute-start | bytes 688136 | tf_op jit(solution)/shard_map/while/body/eval_jaxpr/ppermute | solution.py:12
  370.6 91.7 %all-to-all-start.1 = ((bf16[32,32,1792]{2,1,0:T(8,128)(2,1)}), bf16[32,32,1792]{2,1,0:T(8,128)(2,1)}, u32[]{:S(2)}, u32[]{:S(2)}) async-start(bf16[32,32,1792]{2,1,0:T(8,128)(2,1)} %bitcast.106), calls=%async_computation.3 | async-start | bytes 7340032 | tf_op jit(solution)/shard_map/all_to_all | solution.py:170
  377.7 87.2 %copy-start.4 = (f32[1,32,1792]{2,1,0:T(8,128)S(1)}, f32[1,32,1792]{2,1,0:T(8,128)}, u32[]{:S(2)}) copy-start(f32[1,32,1792]{2,1,0:T(8,128)} %param.21) | copy-start | bytes 688132
  377.7 110.7 %copy-start.3 = (f32[1,56,1024]{2,1,0:T(8,128)S(1)}, f32[1,56,1024]{2,1,0:T(8,128)}, u32[]{:S(2)}) copy-start(f32[1,56,1024]{2,1,0:T(8,128)} %param.20) | copy-start | bytes 688132
  377.7 110.7 %reduce-scatter.5.cloned.1.call-start = ((), (), s32[]{:S(2)}) async-start(), calls=%async_computation.5 | async-start | bytes 1032192 | tf_op jit(solution)/shard_map/reduce_scatter | solution.py:164
Sparse Core Ops, SparseCore 0:
  25.6 105.3 all-gather.2
  367.6 73.0 reduce-scatter.2
  443.3 45.0 reduce-scatter.4

commit v3 on v2

v3 whole, which is shorter than its diff:
```python
import functools
import math

import jax
import jax.numpy as jnp
from jax import lax
from jax.experimental import pallas as pl
from jax.experimental.pallas import tpu as pltpu
from jax.sharding import Mesh, PartitionSpec as P


def norm_parts(current, gains):
    widened = current.astype(jnp.float32)
    inverse = lax.rsqrt(jnp.mean(widened * widened, axis=-1, keepdims=True) + 1e-06)
    normed = (widened * inverse * gains).astype(jnp.bfloat16)
    return (widened, inverse, normed)


def layer_forward(current, gains, value_matrix, output_matrix):
    widened, inverse, normed = norm_parts(current, gains)
    values = jnp.dot(normed, value_matrix, preferred_element_type=jnp.float32).astype(jnp.bfloat16)
    result = (widened + jnp.dot(values, output_matrix, preferred_element_type=jnp.float32)).astype(
        jnp.bfloat16
    )
    return (values, result)


def layer_backward(current, incoming, gains, value_matrix, output_matrix):
    widened, inverse, normed = norm_parts(current, gains)
    dvalues = jnp.dot(incoming, output_matrix.T, preferred_element_type=jnp.float32).astype(
        jnp.bfloat16
    )
    dnormed = jnp.dot(dvalues, value_matrix.T, preferred_element_type=jnp.float32) * gains
    centred = widened * inverse
    through = inverse * (dnormed - centred * jnp.mean(dnormed * centred, axis=-1, keepdims=True))
    before = (incoming.astype(jnp.float32) + through).astype(jnp.bfloat16)
    return (normed, dvalues, before)


def example_sums(left, right, seq_len):
    first = left.reshape(-1, seq_len, left.shape[-1])
    second = right.reshape(-1, seq_len, right.shape[-1])
    gram_first = jnp.einsum("eth,esh->ets", first, first, preferred_element_type=jnp.float32)
    gram_second = jnp.einsum("eth,esh->ets", second, second, preferred_element_type=jnp.float32)
    return jnp.sum(gram_first * gram_second, axis=(1, 2))


TILE = 256


def chain_kernel(
    sections,
    seed_ref, cot_ref, gain_ref, wv_ref, wo_ref,
    kin_ref, kval_ref, kgrad_ref, kdv_ref,
    fbuf, fres, bbuf, bres, work, fsend, frecv, bsend, brecv,
):
    place = lax.axis_index("section")
    micro_count, rows, width = seed_ref.shape
    heads = wv_ref.shape[1]
    ahead = lax.rem(place + 1, sections)
    behind = lax.rem(place + sections - 1, sections)
    first = place == 0
    last = place == sections - 1

    barrier = pltpu.get_barrier_semaphore()

    @pl.when(place > 0)
    def _():
        pl.semaphore_signal(barrier, inc=1, device_id={"section": behind}, device_id_type=pl.DeviceIdType.MESH)

    @pl.when(place < sections - 1)
    def _():
        pl.semaphore_signal(barrier, inc=1, device_id={"section": ahead}, device_id_type=pl.DeviceIdType.MESH)

    peers = (place + sections - 1) // sections + (2 * sections - 2 - place) // sections
    pl.semaphore_wait(barrier, peers)

    @pl.when(first)
    def _():
        fbuf[...] = seed_ref[...]

    @pl.when(last)
    def _():
        bbuf[...] = cot_ref[...]

    def forward_copy(m):
        return pltpu.make_async_remote_copy(
            src_ref=fres.at[m], dst_ref=fbuf.at[m], send_sem=fsend.at[m], recv_sem=frecv.at[m],
            device_id={"section": ahead}, device_id_type=pl.DeviceIdType.MESH,
        )

    def backward_copy(m):
        return pltpu.make_async_remote_copy(
            src_ref=bres.at[m], dst_ref=bbuf.at[m], send_sem=bsend.at[m], recv_sem=brecv.at[m],
            device_id={"section": behind}, device_id_type=pl.DeviceIdType.MESH,
        )

    def columns(i):
        return pl.ds(pl.multiple_of(i * TILE, TILE), TILE)

    for m in range(micro_count):
        @pl.when(place > 0)
        def _():
            forward_copy(m).wait_recv()

        x = fbuf[m]
        kin_ref[m] = x
        wide = x.astype(jnp.float32)
        inverse = lax.rsqrt(jnp.mean(wide * wide, axis=-1, keepdims=True) + 1e-06)
        normed = (wide * inverse * gain_ref[...]).astype(jnp.bfloat16)

        def value_tile(i, carry):
            kval_ref[m, :, columns(i)] = jnp.dot(
                normed, wv_ref[:, columns(i)], preferred_element_type=jnp.float32
            ).astype(jnp.bfloat16)
            return carry

        lax.fori_loop(0, heads // TILE, value_tile, 0)
        values = kval_ref[m]

        def result_tile(i, carry):
            fres[m, :, columns(i)] = (
                fbuf[m, :, columns(i)].astype(jnp.float32)
                + jnp.dot(values, wo_ref[:, columns(i)], preferred_element_type=jnp.float32)
            ).astype(jnp.bfloat16)
            return carry

        lax.fori_loop(0, width // TILE, result_tile, 0)

        @pl.when(place < sections - 1)
        def _():
            forward_copy(m).start()

    contract = (((1,), (1,)), ((), ()))
    for m in range(micro_count):
        @pl.when(place < sections - 1)
        def _():
            backward_copy(m).wait_recv()

        grad = bbuf[m]
        kgrad_ref[m] = grad

        def dvalue_tile(i, carry):
            kdv_ref[m, :, columns(i)] = lax.dot_general(
                grad, wo_ref[columns(i), :], contract, preferred_element_type=jnp.float32
            ).astype(jnp.bfloat16)
            return carry

        lax.fori_loop(0, heads // TILE, dvalue_tile, 0)
        dvalues = kdv_ref[m]

        def dnormed_tile(i, carry):
            work[:, columns(i)] = lax.dot_general(
                dvalues, wv_ref[columns(i), :], contract, preferred_element_type=jnp.float32
            ) * gain_ref[:, columns(i)]
            return carry

        lax.fori_loop(0, width // TILE, dnormed_tile, 0)
        wide = kin_ref[m].astype(jnp.float32)
        inverse = lax.rsqrt(jnp.mean(wide * wide, axis=-1, keepdims=True) + 1e-06)
        dnormed = work[...]
        centred = wide * inverse
        through = inverse * (dnormed - centred * jnp.mean(dnormed * centred, axis=-1, keepdims=True))
        bres[m] = (grad.astype(jnp.float32) + through).astype(jnp.bfloat16)

        @pl.when(place > 0)
        def _():
            backward_copy(m).start()

    for m in range(micro_count):
        @pl.when(place < sections - 1)
        def _():
            forward_copy(m).wait_send()

        @pl.when(place > 0)
        def _():
            backward_copy(m).wait_send()


def run_chain(feed_rows, cot_rows, gains, value_matrix, output_matrix):
    sections = lax.axis_size("section")
    micro_count, rows, width = feed_rows.shape
    heads = value_matrix.shape[1]
    vmem = pl.BlockSpec(memory_space=pltpu.VMEM)
    act = jax.ShapeDtypeStruct((micro_count, rows, width), jnp.bfloat16)
    head_act = jax.ShapeDtypeStruct((micro_count, rows, heads), jnp.bfloat16)
    return pl.pallas_call(
        functools.partial(chain_kernel, sections),
        out_shape=(act, head_act, act, head_act),
        in_specs=[vmem] * 5,
        out_specs=(vmem,) * 4,
        scratch_shapes=[
            pltpu.VMEM((micro_count, rows, width), jnp.bfloat16),
            pltpu.VMEM((micro_count, rows, width), jnp.bfloat16),
            pltpu.VMEM((micro_count, rows, width), jnp.bfloat16),
            pltpu.VMEM((micro_count, rows, width), jnp.bfloat16),
            pltpu.VMEM((rows, width), jnp.float32),
            pltpu.SemaphoreType.DMA((micro_count,)),
            pltpu.SemaphoreType.DMA((micro_count,)),
            pltpu.SemaphoreType.DMA((micro_count,)),
            pltpu.SemaphoreType.DMA((micro_count,)),
        ],
        compiler_params=pltpu.CompilerParams(
            collective_id=0, has_side_effects=True, vmem_limit_bytes=48 * 1024 * 1024
        ),
    )(feed_rows, cot_rows, gains.reshape(1, width), value_matrix, output_matrix)


DP = ("y", "z")


def exchange_rows(shard):
    count = lax.axis_size(DP)
    copies = jnp.broadcast_to(shard[None], (count,) + shard.shape)
    parts = lax.all_to_all(copies, DP, 0, 0, tiled=False)
    return parts.reshape((-1,) + shard.shape[1:])


def scatter_in_stages(block):
    inner = lax.psum_scatter(block, "y", scatter_dimension=0, tiled=True)
    return lax.psum_scatter(inner, "z", scatter_dimension=0, tiled=True).astype(jnp.float32)


def scatter_by_exchange(block):
    count = lax.axis_size(DP)
    parts = block.reshape((count, block.shape[0] // count) + block.shape[1:])
    arrived = lax.all_to_all(parts, DP, 0, 0, tiled=False)
    return jnp.sum(arrived.astype(jnp.float32), axis=0)


def on_device(inputs, cotangent, value_weight, output_weight, norm_gain, value_noise, output_noise):
    micro_count, example_count, seq_len, feature_width = inputs.shape
    feed_rows = inputs.reshape(micro_count, example_count * seq_len, feature_width)
    cot_rows = cotangent.reshape(micro_count, example_count * seq_len, feature_width)
    value_matrix = lax.all_gather(value_weight[0], DP, axis=0, tiled=True)
    output_matrix = exchange_rows(output_weight[0])
    head_width = value_matrix.shape[1]
    gains = norm_gain[0]
    kept_inputs, kept_values, kept_grads, kept_dvalues = run_chain(
        feed_rows, cot_rows, gains, value_matrix, output_matrix
    )
    unused_wide, unused_inverse, normed_rows = norm_parts(
        kept_inputs.reshape(-1, feature_width), gains
    )
    normed_kept = normed_rows.reshape(kept_inputs.shape)
    partial_squares = jnp.stack(
        [
            example_sums(normed_kept[m], kept_dvalues[m], seq_len)
            + example_sums(kept_values[m], kept_grads[m], seq_len)
            for m in range(micro_count)
        ]
    )
    total_squares = lax.psum(partial_squares, "section")
    clip_weight = 1.0 / (jnp.sqrt(total_squares) + 0.01)
    token_weight = jnp.repeat(clip_weight, seq_len, axis=1)[:, :, None]
    scaled_dvalues = (
        (kept_dvalues.astype(jnp.float32) * token_weight)
        .astype(jnp.bfloat16)
        .reshape(-1, head_width)
    )
    scaled_grads = (
        (kept_grads.astype(jnp.float32) * token_weight)
        .astype(jnp.bfloat16)
        .reshape(-1, feature_width)
    )
    value_rows = kept_values.reshape(-1, head_width)
    columns = normed_rows
    value_part = scatter_in_stages(
        lax.dot_general(
            columns, scaled_dvalues, (((0,), (0,)), ((), ())), preferred_element_type=jnp.float32
        ).astype(jnp.bfloat16)
    )
    columns = value_rows
    output_part = scatter_by_exchange(
        lax.dot_general(
            columns, scaled_grads, (((0,), (0,)), ((), ())), preferred_element_type=jnp.float32
        ).astype(jnp.bfloat16)
    )
    grad_scale = math.sqrt(feature_width * head_width)
    value_grad = (value_part * grad_scale + value_noise[0])[None]
    output_grad = (output_part * grad_scale + output_noise[0])[None]
    return (value_grad, output_grad)


def split_dp(mesh):
    devices = mesh.devices
    sections, count = devices.shape
    try:
        across = len({d.coords[1] for d in devices[0]})
    except (AttributeError, IndexError, TypeError):
        across = 1
    if across < 1 or count % across:
        across = 1
    return Mesh(devices.reshape(sections, across, count // across), ("section",) + DP)


def solution(mesh):
    grid = split_dp(mesh)
    return jax.shard_map(
        on_device,
        mesh=grid,
        in_specs=(
            P(None, DP, None, None),
            P(None, DP, None, None),
            P("section", DP, None),
            P("section", DP, None),
            P("section", None),
            P("section", DP, None),
            P("section", DP, None),
        ),
        out_specs=(P("section", DP, None), P("section", DP, None)),
        check_vma=False,
    )
```

time: 498 us -> 383 us (0.77)
  waiting for transfers between devices: 319 us -> 218 us
  Pallas kernels: 0 us -> 76.3 us
  starting transfers between devices: 75.5 us -> 19 us
  matrix products: 37.6 us -> 10.2 us
  blocking collectives: 20.1 us -> 31.8 us
  local copies, waits for them, and re-layouts: 13.7 us -> 5.31 us
  other arithmetic: 12.8 us -> 5.46 us
    ppermute x18 -> x0, waiting for transfers between devices: 103 us -> none  [from_behind(): return lax.ppermute(block, axis, route)]
    pallas_call x0 -> x1, Pallas kernels: none -> 76.3 us  [run_chain(): pl.pallas_call(functools.partial(chain_kernel, sections), out_shape=(act,...]
    ppermute x18 -> x0, starting transfers between devices: 56.5 us -> none  [from_behind(): return lax.ppermute(block, axis, route)]
    dot_general x8 -> x0, matrix products: 27.5 us -> none  [the longest x2 7.83 us: layer_backward(): jnp.dot(incoming, output_matrix.T, preferred_element_type=jnp.float32)]
    psum x1, blocking collectives: 20.1 us -> 31.8 us  [on_device(): total_squares = lax.psum(partial_squares, 'section')]
    another operation x34 -> x0, local copies, waits for them, and re-layouts: 9.75 us -> none
    dynamic_update_slice x36 -> x0, other arithmetic: 6.25 us -> none  [the longest x9 2.24 us: backward_time_step(): lax.dynamic_update_index_in_dim(kept_dvalues, jnp.where(active, dvalues,...]
  transfers between devices with their start and end apart: 23 -> 5, of which waited for: 23 -> 5; matrix products, arithmetic and copies ran while one was open for 2% -> 2% of each run, Pallas kernels for 0% -> 0%
where the time goes in v3:
time: 383 us; the launch traced here: 382 us
  waiting for transfers between devices  218 us (57%)
  Pallas kernels  76.3 us (20%)
  blocking collectives  31.8 us (8%)
  starting transfers between devices  19 us (5%)
  between operations  16.4 us (4%)
  matrix products  10.2 us (3%)
  other arithmetic  5.46 us (1%)
  local copies, waits for them, and re-layouts  5.31 us (1%)
    all_to_all x1, waiting for transfers between devices, exchange_rows(): parts = lax.all_to_all(copies, DP, 0, 0, tiled=False)  94.2 us
    pallas_call x1, Pallas kernels, run_chain(): pl.pallas_call(functools.partial(chain_kernel, sections), out_shape=(act,...  76.3 us
    reduce_scatter x1, waiting for transfers between devices, scatter_in_stages(): inner = lax.psum_scatter(block, 'y', scatter_dimension=0, tiled=True)  65.4 us
    psum x1, blocking collectives, on_device(): total_squares = lax.psum(partial_squares, 'section')  31.8 us
    reduce_scatter x1, waiting for transfers between devices, scatter_in_stages(): lax.psum_scatter(inner, 'z', scatter_dimension=0, tiled=True)  24.4 us
    all_to_all x1, waiting for transfers between devices, scatter_by_exchange(): arrived = lax.all_to_all(parts, DP, 0, 0, tiled=False)  19.1 us
    all_gather x1, waiting for transfers between devices, on_device(): value_matrix = lax.all_gather(value_weight[0], DP, axis=0, tiled=True)  13.9 us
    all_to_all x1, starting transfers between devices, exchange_rows(): parts = lax.all_to_all(copies, DP, 0, 0, tiled=False)  11.7 us
  transfers between devices with their start and end apart: 5, of which 5 were waited for; matrix products, arithmetic and copies ran while one was open for 2% of the time, Pallas kernels for 0%

profile of v3, /device:TPU:4, one launch (start us, length us, event | category | flops | bytes accessed | tf_op | source)
XLA Modules:
  0.0 382.1 jit_solution(17207911449359269754)
XLA Ops:
  7.2 3.2 broadcast_in_dim.14
  10.3 11.7 %all-to-all-start = ((bf16[32,32,1792]{2,1,0:T(8,128)(2,1)}), bf16[32,32,1792]{2,1,0:T(8,128)(2,1)}, u32[]{:S(2)}, u32[]{:S(2)}) async-start(bf16[32,32,1792]{2,1,0:T(8,128)(2,1)} %broadcast_in_dim.14), calls=%async_computation | async-start | bytes 7340032 | tf_op jit(solution)/shard_map/all_to_all | solution.py:215
  22.1 0.0 all-gather.3.cloned.1.call-start
  22.1 0.7 all-gather.3.cloned.1.call-update
  22.8 0.0 reduce-scatter.3.cloned.1.call-start
  22.9 94.2 %all-to-all-done = bf16[32,32,1792]{2,1,0:T(8,128)(2,1)} async-done(((bf16[32,32,1792]{2,1,0:T(8,128)(2,1)}), bf16[32,32,1792]{2,1,0:T(8,128)(2,1)}, u32[]{:S(2)}, u32[]{:S(2)}) %all-to-all-start) | async-done | bytes 3670048 | tf_op jit(solution)/shard_map/all_to_all | solution.py:215
  117.1 13.9 %all-gather.3.cloned.1.call-done = bf16[1,1792,1024]{2,1,0:T(8,128)(2,1)} async-done(((bf16[1,56,1024]{2,1,0:T(8,128)(2,1)}), bf16[1,1792,1024]{2,1,0:T(8,128)(2,1)}) %all-gather.3.cloned.1.call-update) | async-done | bytes 3670032 | tf_op jit(solution)/shard_map/all_gather | solution.py:235
  130.9 2.0 copy-done
  133.0 76.3 %shard_map.86 = (bf16[2,64,1792]{2,1,0:T(8,128)(2,1)S(1)}, bf16[2,64,1024]{2,1,0:T(8,128)(2,1)S(1)}, bf16[2,64,1792]{2,1,0:T(8,128)(2,1)S(1)}, bf16[2,64,1024]{2,1,0:T(8,128)(2,1)S(1)}) custom-call(bf16[2,64,1792]{2,1,0:T(8,128)(2,1)S(1)} %bitcast.48, bf16[2,64,1792]{2,1,0:T(8,128)(2,1)S(1)} %bitcast.49, f32[1,1792]{1,0:T(1,128)S(1)} %copy-done.3, ...), custom_call_target="tpu_custom_call" | custom-call | tf_op jit(solution)/shard_map/pallas_call | solution.py:187
  209.3 0.2 multiply_reduce_fusion
  209.5 0.1 rsqrt.13
  209.6 0.2 fusion.1
  209.7 0.2 fusion.13
  209.9 0.2 fusion.11
  210.2 0.2 fusion.18
  210.4 0.2 fusion.16
  210.6 0.8 fusion.2
  211.3 0.8 fusion.4
  212.1 0.9 fusion.3
  213.0 0.8 fusion.5
  216.3 0.1 pad_maximum_fusion
  216.4 31.8 %psum.7 = f32[2,1]{0,1:T(1,128)S(1)} all-reduce(f32[2,1]{0,1:T(1,128)S(1)} %pad_maximum_fusion), channel_id=1, replica_groups=mesh['section'=8,'y'=4,'z'=8] {'section'}, use_global_device_ids=true, to_apply=%region_5.0 | all-reduce | flops 2 | bytes 16 | tf_op jit(solution)/shard_map/psum | solution.py:253
  248.2 3.1 bitcast_convert_fusion.1
  251.3 3.1 bitcast_convert_fusion
  254.4 7.1 %all-to-all-start.1 = ((bf16[32,32,1792]{2,1,0:T(8,128)(2,1)}), bf16[32,32,1792]{2,1,0:T(8,128)(2,1)}, u32[]{:S(2)}, u32[]{:S(2)}) async-start(bf16[32,32,1792]{2,1,0:T(8,128)(2,1)} %bitcast.50), calls=%async_computation.3 | async-start | bytes 7340032 | tf_op jit(solution)/shard_map/all_to_all | solution.py:227
  261.6 0.0 reduce-scatter.5.cloned.1.call-start
  261.6 65.4 %reduce-scatter.3.cloned.1.call-done = bf16[448,1024]{1,0:T(8,128)(2,1)} async-done(((bf16[1792,1024]{1,0:T(8,128)(2,1)}), bf16[448,1024]{1,0:T(8,128)(2,1)}) %reduce-scatter.3.cloned.1.call-update) | async-done | bytes 917520 | tf_op jit(solution)/shard_map/reduce_scatter | solution.py:220
  327.0 19.1 %all-to-all-done.1 = bf16[32,32,1792]{2,1,0:T(8,128)(2,1)} async-done(((bf16[32,32,1792]{2,1,0:T(8,128)(2,1)}), bf16[32,32,1792]{2,1,0:T(8,128)(2,1)}, u32[]{:S(2)}, u32[]{:S(2)}) %all-to-all-start.1) | async-done | bytes 3670048 | tf_op jit(solution)/shard_map/all_to_all | solution.py:227
  346.2 2.7 convert_reduce_fusion
  348.8 0.7 bitcast_add_fusion
  349.6 24.4 %reduce-scatter.5.cloned.1.call-done = bf16[56,1024]{1,0:T(8,128)(2,1)} async-done(((bf16[448,1024]{1,0:T(8,128)(2,1)}), bf16[56,1024]{1,0:T(8,128)(2,1)}) %reduce-scatter.5.cloned.1.call-update) | async-done | bytes 114704 | tf_op jit(solution)/shard_map/reduce_scatter | solution.py:221
  374.0 1.6 fusion.15
  (16 shorter events, 0.1 us)
Async XLA Ops:
  10.3 12.5 %copy-start.3 = (f32[1,1792]{1,0:T(1,128)S(1)}, f32[1,1792]{1,0:T(1,128)}, u32[]{:S(2)}) copy-start(f32[1,1792]{1,0:T(1,128)} %gain_ref.1) | copy-start | bytes 21508
  10.3 120.6 %copy-start.1 = (bf16[2,1,64,1792]{3,2,1,0:T(8,128)(2,1)S(1)}, bf16[2,1,64,1792]{3,2,1,0:T(8,128)(2,1)}, u32[]{:S(2)}) copy-start(bf16[2,1,64,1792]{3,2,1,0:T(8,128)(2,1)} %param.7) | copy-start | bytes 1376260
  10.3 120.6 %copy-start.2 = (bf16[2,1,64,1792]{3,2,1,0:T(8,128)(2,1)S(1)}, bf16[2,1,64,1792]{3,2,1,0:T(8,128)(2,1)}, u32[]{:S(2)}) copy-start(bf16[2,1,64,1792]{3,2,1,0:T(8,128)(2,1)} %param.8) | copy-start | bytes 1376260
  10.3 106.7 %all-to-all-start = ((bf16[32,32,1792]{2,1,0:T(8,128)(2,1)}), bf16[32,32,1792]{2,1,0:T(8,128)(2,1)}, u32[]{:S(2)}, u32[]{:S(2)}) async-start(bf16[32,32,1792]{2,1,0:T(8,128)(2,1)} %broadcast_in_dim.14), calls=%async_computation | async-start | bytes 7340032 | tf_op jit(solution)/shard_map/all_to_all | solution.py:215
  22.1 108.8 %all-gather.3.cloned.1.call-start = ((), (), s32[]{:S(2)}) async-start(), calls=%async_computation.6 | async-start | bytes 3784704 | tf_op jit(solution)/shard_map/all_gather | solution.py:235
  22.8 304.2 %reduce-scatter.3.cloned.1.call-start = ((), (), s32[]{:S(2)}) async-start(), calls=%async_computation.4 | async-start | bytes 4587520 | tf_op jit(solution)/shard_map/reduce_scatter | solution.py:220
  130.9 2.0 copy-start
  254.4 91.8 %all-to-all-start.1 = ((bf16[32,32,1792]{2,1,0:T(8,128)(2,1)}), bf16[32,32,1792]{2,1,0:T(8,128)(2,1)}, u32[]{:S(2)}, u32[]{:S(2)}) async-start(bf16[32,32,1792]{2,1,0:T(8,128)(2,1)} %bitcast.50), calls=%async_computation.3 | async-start | bytes 7340032 | tf_op jit(solution)/shard_map/all_to_all | solution.py:227
  261.6 87.3 %copy-start.5 = (f32[1,32,1792]{2,1,0:T(8,128)S(1)}, f32[1,32,1792]{2,1,0:T(8,128)}, u32[]{:S(2)}) copy-start(f32[1,32,1792]{2,1,0:T(8,128)} %param.13) | copy-start | bytes 688132
  261.6 112.4 %copy-start.4 = (f32[1,56,1024]{2,1,0:T(8,128)S(1)}, f32[1,56,1024]{2,1,0:T(8,128)}, u32[]{:S(2)}) copy-start(f32[1,56,1024]{2,1,0:T(8,128)} %param.12) | copy-start | bytes 688132
  261.6 112.4 %reduce-scatter.5.cloned.1.call-start = ((), (), s32[]{:S(2)}) async-start(), calls=%async_computation.5 | async-start | bytes 1032192 | tf_op jit(solution)/shard_map/reduce_scatter | solution.py:221
Sparse Core Ops, SparseCore 0:
  25.5 105.3 all-gather.2
  251.5 75.4 reduce-scatter.2
  329.6 44.3 reduce-scatter.4

commit v4 on v3

--- a/solution.py
+++ b/solution.py
@@ -206,14 +206,108 @@
     )(feed_rows, cot_rows, gains.reshape(1, width), value_matrix, output_matrix)
 
 
+def gather_kernel(ys, zs, wv_ref, wo_ref, wv_all, wo_all, own_sem, va_send, va_recv, vb_send, vb_recv, oa_send, oa_recv, ob_send, ob_recv):
+    y = lax.axis_index("y")
+    z = lax.axis_index("z")
+    mesh_ids = pl.DeviceIdType.MESH
+    barrier = pltpu.get_barrier_semaphore()
+    for k in range(1, zs):
+        pl.semaphore_signal(barrier, inc=1, device_id={"z": lax.rem(z + k, zs)}, device_id_type=mesh_ids)
+    for k in range(1, ys):
+        pl.semaphore_signal(barrier, inc=1, device_id={"y": lax.rem(y + k, ys)}, device_id_type=mesh_ids)
+    pl.semaphore_wait(barrier, zs + ys - 2)
+
+    own_v = pltpu.make_async_copy(wv_ref, wv_all.at[y, z], own_sem.at[0])
+    own_o = pltpu.make_async_copy(wo_ref, wo_all.at[y, z], own_sem.at[1])
+    own_v.start()
+    own_o.start()
+
+    def v_first(k, target):
+        return pltpu.make_async_remote_copy(
+            src_ref=wv_ref, dst_ref=wv_all.at[y, z], send_sem=va_send.at[k - 1],
+            recv_sem=va_recv.at[k - 1], device_id={"z": target}, device_id_type=mesh_ids,
+        )
+
+    def o_first(k, target):
+        return pltpu.make_async_remote_copy(
+            src_ref=wo_ref, dst_ref=wo_all.at[y, z], send_sem=oa_send.at[k - 1],
+            recv_sem=oa_recv.at[k - 1], device_id={"y": target}, device_id_type=mesh_ids,
+        )
+
+    def v_second(k, row, target):
+        return pltpu.make_async_remote_copy(
+            src_ref=wv_all.at[pl.ds(row, 1)], dst_ref=wv_all.at[pl.ds(row, 1)],
+            send_sem=vb_send.at[k - 1], recv_sem=vb_recv.at[k - 1],
+            device_id={"y": target}, device_id_type=mesh_ids,
+        )
+
+    def o_second(k, column, target):
+        return pltpu.make_async_remote_copy(
+            src_ref=wo_all.at[:, pl.ds(column, 1)], dst_ref=wo_all.at[:, pl.ds(column, 1)],
+            send_sem=ob_send.at[k - 1], recv_sem=ob_recv.at[k - 1],
+            device_id={"z": target}, device_id_type=mesh_ids,
+        )
+
+    for k in range(1, zs):
+        v_first(k, lax.rem(z + k, zs)).start()
+    for k in range(1, ys):
+        o_first(k, lax.rem(y + k, ys)).start()
+    own_v.wait()
+    own_o.wait()
+    for k in range(1, zs):
+        pltpu.make_async_remote_copy(
+            src_ref=wv_ref, dst_ref=wv_all.at[y, lax.rem(z + zs - k, zs)], send_sem=va_send.at[k - 1],
+            recv_sem=va_recv.at[k - 1], device_id={"z": z}, device_id_type=mesh_ids,
+        ).wait_recv()
+    for k in range(1, ys):
+        pltpu.make_async_remote_copy(
+            src_ref=wo_ref, dst_ref=wo_all.at[lax.rem(y + ys - k, ys), z], send_sem=oa_send.at[k - 1],
+            recv_sem=oa_recv.at[k - 1], device_id={"y": y}, device_id_type=mesh_ids,
+        ).wait_recv()
+    for k in range(1, ys):
+        v_second(k, y, lax.rem(y + k, ys)).start()
+    for k in range(1, zs):
+        o_second(k, z, lax.rem(z + k, zs)).start()
+    for k in range(1, zs):
+        v_first(k, lax.rem(z + k, zs)).wait_send()
+    for k in range(1, ys):
+        o_first(k, lax.rem(y + k, ys)).wait_send()
+    for k in range(1, ys):
+        v_second(k, lax.rem(y + ys - k, ys), y).wait_recv()
+    for k in range(1, zs):
+        o_second(k, lax.rem(z + zs - k, zs), z).wait_recv()
+    for k in range(1, ys):
+        v_second(k, y, lax.rem(y + k, ys)).wait_send()
+    for k in range(1, zs):
+        o_second(k, z, lax.rem(z + k, zs)).wait_send()
+
+
+def gather_weights(value_shard, output_shard):
+    ys = lax.axis_size("y")
+    zs = lax.axis_size("z")
+    anywhere = pl.BlockSpec(memory_space=pl.ANY)
+    wv_all, wo_all = pl.pallas_call(
+        functools.partial(gather_kernel, ys, zs),
+        out_shape=(
+            jax.ShapeDtypeStruct((ys, zs) + value_shard.shape, value_shard.dtype),
+            jax.ShapeDtypeStruct((ys, zs) + output_shard.shape, output_shard.dtype),
+        ),
+        in_specs=[anywhere] * 2,
+        out_specs=(anywhere, anywhere),
+        scratch_shapes=[pltpu.SemaphoreType.DMA((2,))]
+        + [pltpu.SemaphoreType.DMA((zs - 1,))] * 2
+        + [pltpu.SemaphoreType.DMA((ys - 1,))] * 2
+        + [pltpu.SemaphoreType.DMA((ys - 1,))] * 2
+        + [pltpu.SemaphoreType.DMA((zs - 1,))] * 2,
+        compiler_params=pltpu.CompilerParams(collective_id=1, has_side_effects=True),
+    )(value_shard, output_shard)
+    return (
+        wv_all.reshape((-1,) + value_shard.shape[1:]),
+        wo_all.reshape((-1,) + output_shard.shape[1:]),
+    )
+
+
 DP = ("y", "z")
-
-
-def exchange_rows(shard):
-    count = lax.axis_size(DP)
-    copies = jnp.broadcast_to(shard[None], (count,) + shard.shape)
-    parts = lax.all_to_all(copies, DP, 0, 0, tiled=False)
-    return parts.reshape((-1,) + shard.shape[1:])
 
 
 def scatter_in_stages(block):
@@ -232,8 +326,7 @@
     micro_count, example_count, seq_len, feature_width = inputs.shape
     feed_rows = inputs.reshape(micro_count, example_count * seq_len, feature_width)
     cot_rows = cotangent.reshape(micro_count, example_count * seq_len, feature_width)
-    value_matrix = lax.all_gather(value_weight[0], DP, axis=0, tiled=True)
-    output_matrix = exchange_rows(output_weight[0])
+    value_matrix, output_matrix = gather_weights(value_weight[0], output_weight[0])
     head_width = value_matrix.shape[1]
     gains = norm_gain[0]
     kept_inputs, kept_values, kept_grads, kept_dvalues = run_chain(

time: 383 us -> 373 us (0.974)
  Pallas kernels: 76.3 us -> 186 us
  waiting for transfers between devices: 218 us -> 109 us
  starting transfers between devices: 19 us -> 8.34 us
    pallas_call x0 -> x1, Pallas kernels: none -> 110 us  [gather_weights(): pl.pallas_call(functools.partial(gather_kernel, ys, zs), out_shape=(jax.S...]
    all_to_all x1 -> x0, waiting for transfers between devices: 94.2 us -> none  [exchange_rows(): parts = lax.all_to_all(copies, DP, 0, 0, tiled=False)]
    all_gather x1 -> x0, waiting for transfers between devices: 13.9 us -> none  [on_device(): value_matrix = lax.all_gather(value_weight[0], DP, axis=0, tiled=True)]
    all_to_all x1 -> x0, starting transfers between devices: 11.7 us -> none  [exchange_rows(): parts = lax.all_to_all(copies, DP, 0, 0, tiled=False)]
  transfers between devices with their start and end apart: 5 -> 3, of which waited for: 5 -> 3; matrix products, arithmetic and copies ran while one was open for 2% -> 2% of each run, Pallas kernels for 0% -> 0%
where the time goes in v4:
time: 373 us
  Pallas kernels  186 us (50%)
  waiting for transfers between devices  109 us (29%)
  blocking collectives  31.8 us (9%)
  between operations  16.7 us (4%)
  matrix products  10.2 us (3%)
  starting transfers between devices  8.34 us (2%)
  other arithmetic  5.46 us (1%)
  local copies, waits for them, and re-layouts  4.86 us (1%)
    pallas_call x1, Pallas kernels, gather_weights(): pl.pallas_call(functools.partial(gather_kernel, ys, zs), out_shape=(jax.S...  110 us
    pallas_call x1, Pallas kernels, run_chain(): pl.pallas_call(functools.partial(chain_kernel, sections), out_shape=(act,...  76.3 us
    reduce_scatter x1, waiting for transfers between devices, scatter_in_stages(): inner = lax.psum_scatter(block, 'y', scatter_dimension=0, tiled=True)  65 us
    psum x1, blocking collectives, on_device(): total_squares = lax.psum(partial_squares, 'section')  31.8 us
    reduce_scatter x1, waiting for transfers between devices, scatter_in_stages(): lax.psum_scatter(inner, 'z', scatter_dimension=0, tiled=True)  24.3 us
    all_to_all x1, waiting for transfers between devices, scatter_by_exchange(): arrived = lax.all_to_all(parts, DP, 0, 0, tiled=False)  19.6 us
    all_to_all x1, starting transfers between devices, scatter_by_exchange(): arrived = lax.all_to_all(parts, DP, 0, 0, tiled=False)  8.26 us
  transfers between devices with their start and end apart: 3, of which 3 were waited for; matrix products, arithmetic and copies ran while one was open for 2% of the time, Pallas kernels for 0%

profile of v4, /device:TPU:4, one launch (start us, length us, event | category | flops | bytes accessed | tf_op | source)
XLA Modules:
  0.0 372.6 jit_solution(7508092466585960840)
XLA Ops:
  7.2 0.0 reduce-scatter.3.cloned.1.call-start
  7.2 110.0 %shard_map.86 = (bf16[4,8,56,1024]{3,2,1,0:T(8,128)(2,1)}, bf16[4,8,32,1792]{3,2,1,0:T(8,128)(2,1)}) custom-call(bf16[56,1024]{1,0:T(8,128)(2,1)} %bitcast.53, bf16[32,1792]{1,0:T(8,128)(2,1)} %bitcast.54), custom_call_target="tpu_custom_call" | custom-call | tf_op jit(solution)/shard_map/pallas_call | solution.py:289
  117.2 2.0 copy-done
  119.2 1.0 copy-done.1
  120.2 1.0 copy-done.2
  121.3 0.7 copy-done.3
  122.0 76.3 %shard_map.87 = (bf16[2,64,1792]{2,1,0:T(8,128)(2,1)S(1)}, bf16[2,64,1024]{2,1,0:T(8,128)(2,1)S(1)}, bf16[2,64,1792]{2,1,0:T(8,128)(2,1)S(1)}, bf16[2,64,1024]{2,1,0:T(8,128)(2,1)S(1)}) custom-call(bf16[2,64,1792]{2,1,0:T(8,128)(2,1)S(1)} %bitcast.49, bf16[2,64,1792]{2,1,0:T(8,128)(2,1)S(1)} %bitcast.50, f32[1,1792]{1,0:T(1,128)S(1)} %copy-done.3, ...), custom_call_target="tpu_custom_call" | custom-call | tf_op jit(solution)/shard_map/pallas_call | solution.py:187
  198.3 0.2 multiply_reduce_fusion
  198.5 0.1 rsqrt.13
  198.6 0.2 fusion.1
  198.8 0.2 fusion.13
  199.0 0.2 fusion.11
  199.2 0.2 fusion.18
  199.4 0.2 fusion.16
  199.6 0.8 fusion.2
  200.4 0.8 fusion.4
  201.2 0.9 fusion.3
  202.0 0.8 fusion.5
  205.4 0.1 pad_maximum_fusion
  205.4 31.8 %psum.7 = f32[2,1]{0,1:T(1,128)S(1)} all-reduce(f32[2,1]{0,1:T(1,128)S(1)} %pad_maximum_fusion), channel_id=1, replica_groups=mesh['section'=8,'y'=4,'z'=8] {'section'}, use_global_device_ids=true, to_apply=%region_5.0 | all-reduce | flops 2 | bytes 16 | tf_op jit(solution)/shard_map/psum | solution.py:346
  237.3 3.1 bitcast_convert_fusion.1
  240.4 0.0 reduce-scatter.3.cloned.1.call-update
  240.4 3.1 bitcast_convert_fusion
  243.5 8.3 %all-to-all-start = ((bf16[32,32,1792]{2,1,0:T(8,128)(2,1)}), bf16[32,32,1792]{2,1,0:T(8,128)(2,1)}, u32[]{:S(2)}, u32[]{:S(2)}) async-start(bf16[32,32,1792]{2,1,0:T(8,128)(2,1)} %bitcast.51), calls=%async_computation.2 | async-start | bytes 7340032 | tf_op jit(solution)/shard_map/all_to_all | solution.py:321
  251.8 0.0 reduce-scatter.5.cloned.1.call-start
  251.8 65.0 %reduce-scatter.3.cloned.1.call-done = bf16[448,1024]{1,0:T(8,128)(2,1)} async-done(((bf16[1792,1024]{1,0:T(8,128)(2,1)}), bf16[448,1024]{1,0:T(8,128)(2,1)}) %reduce-scatter.3.cloned.1.call-update) | async-done | bytes 917520 | tf_op jit(solution)/shard_map/reduce_scatter | solution.py:314
  316.9 0.0 reduce-scatter.5.cloned.1.call-update
  316.9 19.6 %all-to-all-done = bf16[32,32,1792]{2,1,0:T(8,128)(2,1)} async-done(((bf16[32,32,1792]{2,1,0:T(8,128)(2,1)}), bf16[32,32,1792]{2,1,0:T(8,128)(2,1)}, u32[]{:S(2)}, u32[]{:S(2)}) %all-to-all-start) | async-done | bytes 3670048 | tf_op jit(solution)/shard_map/all_to_all | solution.py:321
  336.5 2.7 convert_reduce_fusion
  339.2 0.7 bitcast_add_fusion
  339.9 24.3 %reduce-scatter.5.cloned.1.call-done = bf16[56,1024]{1,0:T(8,128)(2,1)} async-done(((bf16[448,1024]{1,0:T(8,128)(2,1)}), bf16[56,1024]{1,0:T(8,128)(2,1)}) %reduce-scatter.5.cloned.1.call-update) | async-done | bytes 114704 | tf_op jit(solution)/shard_map/reduce_scatter | solution.py:315
  364.2 1.6 fusion.15
  (13 shorter events, 0.1 us)
Async XLA Ops:
  7.2 309.7 %reduce-scatter.3.cloned.1.call-start = ((), (), s32[]{:S(2)}) async-start(), calls=%async_computation.3 | async-start | bytes 4587520 | tf_op jit(solution)/shard_map/reduce_scatter | solution.py:314
  117.2 2.0 copy-start
  119.2 1.0 copy-start.1
  120.2 1.0 copy-start.2
  121.3 0.7 copy-start.3
  122.0 76.6 %copy-start.4 = (f32[1,1792]{1,0:T(1,128)S(1)}, f32[1,1792]{1,0:T(1,128)}, u32[]{:S(2)}) copy-start(f32[1,1792]{1,0:T(1,128)} %gain_ref.1) | copy-start | bytes 21508
  243.5 93.0 %all-to-all-start = ((bf16[32,32,1792]{2,1,0:T(8,128)(2,1)}), bf16[32,32,1792]{2,1,0:T(8,128)(2,1)}, u32[]{:S(2)}, u32[]{:S(2)}) async-start(bf16[32,32,1792]{2,1,0:T(8,128)(2,1)} %bitcast.51), calls=%async_computation.2 | async-start | bytes 7340032 | tf_op jit(solution)/shard_map/all_to_all | solution.py:321
  251.7 87.4 %copy-start.6 = (f32[1,32,1792]{2,1,0:T(8,128)S(1)}, f32[1,32,1792]{2,1,0:T(8,128)}, u32[]{:S(2)}) copy-start(f32[1,32,1792]{2,1,0:T(8,128)} %param.13) | copy-start | bytes 688132
  251.8 112.4 %copy-start.5 = (f32[1,56,1024]{2,1,0:T(8,128)S(1)}, f32[1,56,1024]{2,1,0:T(8,128)}, u32[]{:S(2)}) copy-start(f32[1,56,1024]{2,1,0:T(8,128)} %param.12) | copy-start | bytes 688132
  251.8 112.4 %reduce-scatter.5.cloned.1.call-start = ((), (), s32[]{:S(2)}) async-start(), calls=%async_computation.4 | async-start | bytes 1032192 | tf_op jit(solution)/shard_map/reduce_scatter | solution.py:315
Sparse Core Ops, SparseCore 0:
  240.5 76.3 reduce-scatter.2
  319.4 44.7 reduce-scatter.4

commit v5 on v4

--- a/solution.py
+++ b/solution.py
@@ -206,32 +206,85 @@
     )(feed_rows, cot_rows, gains.reshape(1, width), value_matrix, output_matrix)
 
 
-def gather_kernel(ys, zs, wv_ref, wo_ref, wv_all, wo_all, own_sem, va_send, va_recv, vb_send, vb_recv, oa_send, oa_recv, ob_send, ob_recv):
+def ring_copies(window, first_src, z, zs, sems):
+    mesh_ids = pl.DeviceIdType.MESH
+    right_send, right_recv, left_send, left_recv = sems
+    rights, lefts = zs // 2, (zs - 1) // 2
+
+    def right(t):
+        slot = lax.rem(z + zs - t, zs)
+        return pltpu.make_async_remote_copy(
+            src_ref=first_src if t == 0 else window(slot), dst_ref=window(slot),
+            send_sem=right_send.at[t], recv_sem=right_recv.at[t],
+            device_id={"z": lax.rem(z + 1, zs)}, device_id_type=mesh_ids,
+        )
+
+    def left(t):
+        slot = lax.rem(z + t, zs)
+        return pltpu.make_async_remote_copy(
+            src_ref=first_src if t == 0 else window(slot), dst_ref=window(slot),
+            send_sem=left_send.at[t], recv_sem=left_recv.at[t],
+            device_id={"z": lax.rem(z + zs - 1, zs)}, device_id_type=mesh_ids,
+        )
+
+    def right_in(t):
+        return pltpu.make_async_remote_copy(
+            src_ref=first_src, dst_ref=window(lax.rem(z + 2 * zs - 1 - t, zs)),
+            send_sem=right_send.at[t], recv_sem=right_recv.at[t],
+            device_id={"z": z}, device_id_type=mesh_ids,
+        )
+
+    def left_in(t):
+        return pltpu.make_async_remote_copy(
+            src_ref=first_src, dst_ref=window(lax.rem(z + 1 + t, zs)),
+            send_sem=left_send.at[t], recv_sem=left_recv.at[t],
+            device_id={"z": z}, device_id_type=mesh_ids,
+        )
+
+    def run():
+        for t in range(rights):
+            right(t).start()
+            if t < lefts:
+                left(t).start()
+            right_in(t).wait_recv()
+            if t < lefts:
+                left_in(t).wait_recv()
+
+    def finish():
+        for t in range(rights):
+            right(t).wait_send()
+        for t in range(lefts):
+            left(t).wait_send()
+
+    return run, finish
+
+
+def gather_kernel(ys, zs, wv_ref, wo_ref, wv_all, wo_all, own_sem, va, vb_send, vb_recv, oa_send, oa_recv, ob):
     y = lax.axis_index("y")
     z = lax.axis_index("z")
     mesh_ids = pl.DeviceIdType.MESH
     barrier = pltpu.get_barrier_semaphore()
-    for k in range(1, zs):
-        pl.semaphore_signal(barrier, inc=1, device_id={"z": lax.rem(z + k, zs)}, device_id_type=mesh_ids)
+    pl.semaphore_signal(barrier, inc=1, device_id={"z": lax.rem(z + 1, zs)}, device_id_type=mesh_ids)
+    pl.semaphore_signal(barrier, inc=1, device_id={"z": lax.rem(z + zs - 1, zs)}, device_id_type=mesh_ids)
     for k in range(1, ys):
         pl.semaphore_signal(barrier, inc=1, device_id={"y": lax.rem(y + k, ys)}, device_id_type=mesh_ids)
-    pl.semaphore_wait(barrier, zs + ys - 2)
+    pl.semaphore_wait(barrier, ys + 1)
 
     own_v = pltpu.make_async_copy(wv_ref, wv_all.at[y, z], own_sem.at[0])
     own_o = pltpu.make_async_copy(wo_ref, wo_all.at[y, z], own_sem.at[1])
     own_v.start()
     own_o.start()
 
-    def v_first(k, target):
-        return pltpu.make_async_remote_copy(
-            src_ref=wv_ref, dst_ref=wv_all.at[y, z], send_sem=va_send.at[k - 1],
-            recv_sem=va_recv.at[k - 1], device_id={"z": target}, device_id_type=mesh_ids,
-        )
-
     def o_first(k, target):
         return pltpu.make_async_remote_copy(
             src_ref=wo_ref, dst_ref=wo_all.at[y, z], send_sem=oa_send.at[k - 1],
             recv_sem=oa_recv.at[k - 1], device_id={"y": target}, device_id_type=mesh_ids,
+        )
+
+    def o_first_in(k):
+        return pltpu.make_async_remote_copy(
+            src_ref=wo_ref, dst_ref=wo_all.at[lax.rem(y + ys - k, ys), z], send_sem=oa_send.at[k - 1],
+            recv_sem=oa_recv.at[k - 1], device_id={"y": y}, device_id_type=mesh_ids,
         )
 
     def v_second(k, row, target):
@@ -241,51 +294,40 @@
             device_id={"y": target}, device_id_type=mesh_ids,
         )
 
-    def o_second(k, column, target):
-        return pltpu.make_async_remote_copy(
-            src_ref=wo_all.at[:, pl.ds(column, 1)], dst_ref=wo_all.at[:, pl.ds(column, 1)],
-            send_sem=ob_send.at[k - 1], recv_sem=ob_recv.at[k - 1],
-            device_id={"z": target}, device_id_type=mesh_ids,
-        )
-
-    for k in range(1, zs):
-        v_first(k, lax.rem(z + k, zs)).start()
     for k in range(1, ys):
         o_first(k, lax.rem(y + k, ys)).start()
+    v_ring, v_ring_done = ring_copies(lambda o: wv_all.at[y, o], wv_ref, z, zs, va)
+    v_ring()
     own_v.wait()
     own_o.wait()
-    for k in range(1, zs):
-        pltpu.make_async_remote_copy(
-            src_ref=wv_ref, dst_ref=wv_all.at[y, lax.rem(z + zs - k, zs)], send_sem=va_send.at[k - 1],
-            recv_sem=va_recv.at[k - 1], device_id={"z": z}, device_id_type=mesh_ids,
-        ).wait_recv()
-    for k in range(1, ys):
-        pltpu.make_async_remote_copy(
-            src_ref=wo_ref, dst_ref=wo_all.at[lax.rem(y + ys - k, ys), z], send_sem=oa_send.at[k - 1],
-            recv_sem=oa_recv.at[k - 1], device_id={"y": y}, device_id_type=mesh_ids,
-        ).wait_recv()
+    for k in range(1, ys):
+        o_first_in(k).wait_recv()
     for k in range(1, ys):
         v_second(k, y, lax.rem(y + k, ys)).start()
-    for k in range(1, zs):
-        o_second(k, z, lax.rem(z + k, zs)).start()
-    for k in range(1, zs):
-        v_first(k, lax.rem(z + k, zs)).wait_send()
+    o_ring, o_ring_done = ring_copies(
+        lambda o: wo_all.at[:, pl.ds(o, 1)], wo_all.at[:, pl.ds(z, 1)], z, zs, ob
+    )
+    o_ring()
+    v_ring_done()
     for k in range(1, ys):
         o_first(k, lax.rem(y + k, ys)).wait_send()
     for k in range(1, ys):
         v_second(k, lax.rem(y + ys - k, ys), y).wait_recv()
-    for k in range(1, zs):
-        o_second(k, lax.rem(z + zs - k, zs), z).wait_recv()
+    o_ring_done()
     for k in range(1, ys):
         v_second(k, y, lax.rem(y + k, ys)).wait_send()
-    for k in range(1, zs):
-        o_second(k, z, lax.rem(z + k, zs)).wait_send()
 
 
 def gather_weights(value_shard, output_shard):
     ys = lax.axis_size("y")
     zs = lax.axis_size("z")
     anywhere = pl.BlockSpec(memory_space=pl.ANY)
+    ring_sems = [
+        pltpu.SemaphoreType.DMA((zs // 2,)),
+        pltpu.SemaphoreType.DMA((zs // 2,)),
+        pltpu.SemaphoreType.DMA((max((zs - 1) // 2, 1),)),
+        pltpu.SemaphoreType.DMA((max((zs - 1) // 2, 1),)),
+    ]
     wv_all, wo_all = pl.pallas_call(
         functools.partial(gather_kernel, ys, zs),
         out_shape=(
@@ -294,11 +336,9 @@
         ),
         in_specs=[anywhere] * 2,
         out_specs=(anywhere, anywhere),
-        scratch_shapes=[pltpu.SemaphoreType.DMA((2,))]
-        + [pltpu.SemaphoreType.DMA((zs - 1,))] * 2
-        + [pltpu.SemaphoreType.DMA((ys - 1,))] * 2
-        + [pltpu.SemaphoreType.DMA((ys - 1,))] * 2
-        + [pltpu.SemaphoreType.DMA((zs - 1,))] * 2,
+        scratch_shapes=[pltpu.SemaphoreType.DMA((2,)), ring_sems]
+        + [pltpu.SemaphoreType.DMA((ys - 1,))] * 4
+        + [ring_sems],
         compiler_params=pltpu.CompilerParams(collective_id=1, has_side_effects=True),
     )(value_shard, output_shard)
     return (

time: 373 us -> 329 us (0.88)
  Pallas kernels: 186 us -> 144 us
    pallas_call x1, Pallas kernels: 110 us -> 68.2 us  [gather_weights(): pl.pallas_call(functools.partial(gather_kernel, ys, zs), out_shape=(jax.S...]
where the time goes in v5:
time: 329 us; the launch traced here: 328 us
  Pallas kernels  144 us (44%)
  waiting for transfers between devices  109 us (33%)
  blocking collectives  31.8 us (10%)
  between operations  16.7 us (5%)
  matrix products  10.2 us (3%)
  starting transfers between devices  5.97 us (2%)
  other arithmetic  5.46 us (2%)
  local copies, waits for them, and re-layouts  4.86 us (1%)
    pallas_call x1, Pallas kernels, run_chain(): pl.pallas_call(functools.partial(chain_kernel, sections), out_shape=(act,...  76.3 us
    pallas_call x1, Pallas kernels, gather_weights(): pl.pallas_call(functools.partial(gather_kernel, ys, zs), out_shape=(jax.S...  68.2 us
    reduce_scatter x1, waiting for transfers between devices, scatter_in_stages(): inner = lax.psum_scatter(block, 'y', scatter_dimension=0, tiled=True)  65.1 us
    psum x1, blocking collectives, on_device(): total_squares = lax.psum(partial_squares, 'section')  31.8 us
    reduce_scatter x1, waiting for transfers between devices, scatter_in_stages(): lax.psum_scatter(inner, 'z', scatter_dimension=0, tiled=True)  24.3 us
    all_to_all x1, waiting for transfers between devices, scatter_by_exchange(): arrived = lax.all_to_all(parts, DP, 0, 0, tiled=False)  19.6 us
  transfers between devices with their start and end apart: 3, of which 3 were waited for; matrix products, arithmetic and copies ran while one was open for 2% of the time, Pallas kernels for 0%

profile of v5, /device:TPU:4, one launch (start us, length us, event | category | flops | bytes accessed | tf_op | source)
XLA Modules:
  0.0 328.5 jit_solution(14807605111632030352)
XLA Ops:
  7.2 0.0 reduce-scatter.3.cloned.1.call-start
  7.2 68.2 %shard_map.86 = (bf16[4,8,56,1024]{3,2,1,0:T(8,128)(2,1)}, bf16[4,8,32,1792]{3,2,1,0:T(8,128)(2,1)}) custom-call(bf16[56,1024]{1,0:T(8,128)(2,1)} %bitcast.53, bf16[32,1792]{1,0:T(8,128)(2,1)} %bitcast.54), custom_call_target="tpu_custom_call" | custom-call | tf_op jit(solution)/shard_map/pallas_call | solution.py:331
  75.4 2.0 copy-done
  77.4 1.0 copy-done.1
  78.4 1.0 copy-done.2
  79.5 0.7 copy-done.3
  80.2 76.3 %shard_map.87 = (bf16[2,64,1792]{2,1,0:T(8,128)(2,1)S(1)}, bf16[2,64,1024]{2,1,0:T(8,128)(2,1)S(1)}, bf16[2,64,1792]{2,1,0:T(8,128)(2,1)S(1)}, bf16[2,64,1024]{2,1,0:T(8,128)(2,1)S(1)}) custom-call(bf16[2,64,1792]{2,1,0:T(8,128)(2,1)S(1)} %bitcast.49, bf16[2,64,1792]{2,1,0:T(8,128)(2,1)S(1)} %bitcast.50, f32[1,1792]{1,0:T(1,128)S(1)} %copy-done.3, ...), custom_call_target="tpu_custom_call" | custom-call | tf_op jit(solution)/shard_map/pallas_call | solution.py:187
  156.5 0.2 multiply_reduce_fusion
  156.7 0.1 rsqrt.13
  156.8 0.2 fusion.1
  157.0 0.2 fusion.13
  157.2 0.2 fusion.11
  157.4 0.2 fusion.18
  157.6 0.2 fusion.16
  157.8 0.8 fusion.2
  158.6 0.8 fusion.4
  159.4 0.9 fusion.3
  160.2 0.8 fusion.5
  163.5 0.1 pad_maximum_fusion
  163.6 31.8 %psum.7 = f32[2,1]{0,1:T(1,128)S(1)} all-reduce(f32[2,1]{0,1:T(1,128)S(1)} %pad_maximum_fusion), channel_id=1, replica_groups=mesh['section'=8,'y'=4,'z'=8] {'section'}, use_global_device_ids=true, to_apply=%region_5.0 | all-reduce | flops 2 | bytes 16 | tf_op jit(solution)/shard_map/psum | solution.py:386
  195.5 3.1 bitcast_convert_fusion.1
  198.6 0.0 reduce-scatter.3.cloned.1.call-update
  198.6 3.1 bitcast_convert_fusion
  201.7 5.9 %all-to-all-start = ((bf16[32,32,1792]{2,1,0:T(8,128)(2,1)}), bf16[32,32,1792]{2,1,0:T(8,128)(2,1)}, u32[]{:S(2)}, u32[]{:S(2)}) async-start(bf16[32,32,1792]{2,1,0:T(8,128)(2,1)} %bitcast.51), calls=%async_computation.2 | async-start | bytes 7340032 | tf_op jit(solution)/shard_map/all_to_all | solution.py:361
  207.6 0.0 reduce-scatter.5.cloned.1.call-start
  207.6 65.1 %reduce-scatter.3.cloned.1.call-done = bf16[448,1024]{1,0:T(8,128)(2,1)} async-done(((bf16[1792,1024]{1,0:T(8,128)(2,1)}), bf16[448,1024]{1,0:T(8,128)(2,1)}) %reduce-scatter.3.cloned.1.call-update) | async-done | bytes 917520 | tf_op jit(solution)/shard_map/reduce_scatter | solution.py:354
  272.7 0.0 reduce-scatter.5.cloned.1.call-update
  272.7 19.6 %all-to-all-done = bf16[32,32,1792]{2,1,0:T(8,128)(2,1)} async-done(((bf16[32,32,1792]{2,1,0:T(8,128)(2,1)}), bf16[32,32,1792]{2,1,0:T(8,128)(2,1)}, u32[]{:S(2)}, u32[]{:S(2)}) %all-to-all-start) | async-done | bytes 3670048 | tf_op jit(solution)/shard_map/all_to_all | solution.py:361
  292.3 2.7 convert_reduce_fusion
  295.0 0.7 bitcast_add_fusion
  295.7 24.3 %reduce-scatter.5.cloned.1.call-done = bf16[56,1024]{1,0:T(8,128)(2,1)} async-done(((bf16[448,1024]{1,0:T(8,128)(2,1)}), bf16[56,1024]{1,0:T(8,128)(2,1)}) %reduce-scatter.5.cloned.1.call-update) | async-done | bytes 114704 | tf_op jit(solution)/shard_map/reduce_scatter | solution.py:355
  320.0 1.6 fusion.15
  (13 shorter events, 0.1 us)
Async XLA Ops:
  7.2 265.5 %reduce-scatter.3.cloned.1.call-start = ((), (), s32[]{:S(2)}) async-start(), calls=%async_computation.3 | async-start | bytes 4587520 | tf_op jit(solution)/shard_map/reduce_scatter | solution.py:354
  75.4 2.0 copy-start
  77.4 1.0 copy-start.1
  78.4 1.0 copy-start.2
  79.5 0.7 copy-start.3
  80.2 76.6 %copy-start.4 = (f32[1,1792]{1,0:T(1,128)S(1)}, f32[1,1792]{1,0:T(1,128)}, u32[]{:S(2)}) copy-start(f32[1,1792]{1,0:T(1,128)} %gain_ref.1) | copy-start | bytes 21508
  201.7 90.7 %all-to-all-start = ((bf16[32,32,1792]{2,1,0:T(8,128)(2,1)}), bf16[32,32,1792]{2,1,0:T(8,128)(2,1)}, u32[]{:S(2)}, u32[]{:S(2)}) async-start(bf16[32,32,1792]{2,1,0:T(8,128)(2,1)} %bitcast.51), calls=%async_computation.2 | async-start | bytes 7340032 | tf_op jit(solution)/shard_map/all_to_all | solution.py:361
  207.6 87.4 %copy-start.6 = (f32[1,32,1792]{2,1,0:T(8,128)S(1)}, f32[1,32,1792]{2,1,0:T(8,128)}, u32[]{:S(2)}) copy-start(f32[1,32,1792]{2,1,0:T(8,128)} %param.13) | copy-start | bytes 688132
  207.6 112.4 %copy-start.5 = (f32[1,56,1024]{2,1,0:T(8,128)S(1)}, f32[1,56,1024]{2,1,0:T(8,128)}, u32[]{:S(2)}) copy-start(f32[1,56,1024]{2,1,0:T(8,128)} %param.12) | copy-start | bytes 688132
  207.6 112.4 %reduce-scatter.5.cloned.1.call-start = ((), (), s32[]{:S(2)}) async-start(), calls=%async_computation.4 | async-start | bytes 1032192 | tf_op jit(solution)/shard_map/reduce_scatter | solution.py:355
Sparse Core Ops, SparseCore 0:
  198.7 73.9 reduce-scatter.2
  275.3 44.7 reduce-scatter.4

commit v6 on v5

--- a/solution.py
+++ b/solution.py
@@ -347,19 +347,161 @@
     )
 
 
+def ring_sum(get, z, zs, bufs, sems):
+    mesh_ids = pl.DeviceIdType.MESH
+    rsend, rrecv, lsend, lrecv = bufs
+    rs_send, rs_recv, ls_send, ls_recv = sems
+    rights, lefts = zs // 2, (zs - 1) // 2
+
+    def right(t):
+        return pltpu.make_async_remote_copy(
+            src_ref=rsend.at[t], dst_ref=rrecv.at[t], send_sem=rs_send.at[t], recv_sem=rs_recv.at[t],
+            device_id={"z": lax.rem(z + 1, zs)}, device_id_type=mesh_ids,
+        )
+
+    def left(t):
+        return pltpu.make_async_remote_copy(
+            src_ref=lsend.at[t], dst_ref=lrecv.at[t], send_sem=ls_send.at[t], recv_sem=ls_recv.at[t],
+            device_id={"z": lax.rem(z + zs - 1, zs)}, device_id_type=mesh_ids,
+        )
+
+    for t in range(rights):
+        value = get(lax.rem(z + rights - t, zs))
+        if t > 0:
+            value = value + rrecv[t - 1].astype(jnp.float32)
+        rsend[t] = value.astype(rsend.dtype)
+        right(t).start()
+        if t < lefts:
+            value = get(lax.rem(z + zs - lefts + t, zs))
+            if t > 0:
+                value = value + lrecv[t - 1].astype(jnp.float32)
+            lsend[t] = value.astype(lsend.dtype)
+            left(t).start()
+        right(t).wait_recv()
+        if t < lefts:
+            left(t).wait_recv()
+    total = get(z) + rrecv[rights - 1].astype(jnp.float32)
+    if lefts > 0:
+        total = total + lrecv[lefts - 1].astype(jnp.float32)
+
+    def finish():
+        for t in range(rights):
+            right(t).wait_send()
+        for t in range(lefts):
+            left(t).wait_send()
+
+    return total, finish
+
+
+def direct_copies(source, landing, axis, me, count, send_sems, recv_sems):
+    def copy(k):
+        return pltpu.make_async_remote_copy(
+            src_ref=source.at[lax.rem(me + k, count)], dst_ref=landing.at[k - 1],
+            send_sem=send_sems.at[k - 1], recv_sem=recv_sems.at[k - 1],
+            device_id={axis: lax.rem(me + k, count)}, device_id_type=pl.DeviceIdType.MESH,
+        )
+
+    return [copy(k) for k in range(1, count)]
+
+
+def scatter_kernel(
+    ys, zs, xv_ref, xo_ref, out_v, out_o,
+    v_land, v_part, o_part, o_send, o_land, v_ring, o_ring, v_sems, o_sems, vd_send, vd_recv, od_send, od_recv,
+):
+    y = lax.axis_index("y")
+    z = lax.axis_index("z")
+    mesh_ids = pl.DeviceIdType.MESH
+    barrier = pltpu.get_barrier_semaphore()
+    pl.semaphore_signal(barrier, inc=1, device_id={"z": lax.rem(z + 1, zs)}, device_id_type=mesh_ids)
+    pl.semaphore_signal(barrier, inc=1, device_id={"z": lax.rem(z + zs - 1, zs)}, device_id_type=mesh_ids)
+    for k in range(1, ys):
+        pl.semaphore_signal(barrier, inc=1, device_id={"y": lax.rem(y + k, ys)}, device_id_type=mesh_ids)
+    pl.semaphore_wait(barrier, ys + 1)
+
+    v_copies = direct_copies(xv_ref, v_land, "y", y, ys, vd_send, vd_recv)
+    for c in v_copies:
+        c.start()
+    o_total, o_finish = ring_sum(lambda d: xo_ref[d].astype(jnp.float32), z, zs, o_ring, o_sems)
+    o_part[...] = o_total
+    o_send[...] = o_total.astype(o_send.dtype)
+    o_copies = direct_copies(o_send, o_land, "y", y, ys, od_send, od_recv)
+    for c in o_copies:
+        c.start()
+    v_sum = xv_ref[y].astype(jnp.float32)
+    for k, c in enumerate(v_copies):
+        c.wait_recv()
+        v_sum = v_sum + v_land[k].astype(jnp.float32)
+    v_part[...] = v_sum
+    v_total, v_finish = ring_sum(lambda d: v_part[d], z, zs, v_ring, v_sems)
+    out_v[...] = v_total
+    o_sum = o_part[y]
+    for k, c in enumerate(o_copies):
+        c.wait_recv()
+        o_sum = o_sum + o_land[k].astype(jnp.float32)
+    out_o[...] = o_sum
+    o_finish()
+    v_finish()
+    for c in v_copies + o_copies:
+        c.wait_send()
+
+
+def scatter_grads(value_block, output_block):
+    ys = lax.axis_size("y")
+    zs = lax.axis_size("z")
+    rows_v, cols_v = value_block.shape
+    rows_o, cols_o = output_block.shape
+    v_rows = rows_v // (ys * zs)
+    o_rows = rows_o // (ys * zs)
+    xv = value_block.reshape(ys, zs, v_rows, cols_v)
+    xo = output_block.reshape(ys, zs, o_rows, cols_o).transpose(1, 0, 2, 3)
+    vmem = pl.BlockSpec(memory_space=pltpu.VMEM)
+    rights, lefts = zs // 2, max((zs - 1) // 2, 1)
+    bf = value_block.dtype
+
+    def ring_space(block):
+        return [
+            pltpu.VMEM((rights,) + block, bf),
+            pltpu.VMEM((rights,) + block, bf),
+            pltpu.VMEM((lefts,) + block, bf),
+            pltpu.VMEM((lefts,) + block, bf),
+        ]
+
+    ring_sems = [
+        pltpu.SemaphoreType.DMA((rights,)),
+        pltpu.SemaphoreType.DMA((rights,)),
+        pltpu.SemaphoreType.DMA((lefts,)),
+        pltpu.SemaphoreType.DMA((lefts,)),
+    ]
+    return pl.pallas_call(
+        functools.partial(scatter_kernel, ys, zs),
+        out_shape=(
+            jax.ShapeDtypeStruct((v_rows, cols_v), jnp.float32),
+            jax.ShapeDtypeStruct((o_rows, cols_o), jnp.float32),
+        ),
+        in_specs=[vmem, vmem],
+        out_specs=(vmem, vmem),
+        scratch_shapes=[
+            pltpu.VMEM((ys - 1, zs, v_rows, cols_v), bf),
+            pltpu.VMEM((zs, v_rows, cols_v), jnp.float32),
+            pltpu.VMEM((ys, o_rows, cols_o), jnp.float32),
+            pltpu.VMEM((ys, o_rows, cols_o), bf),
+            pltpu.VMEM((ys - 1, o_rows, cols_o), bf),
+            ring_space((v_rows, cols_v)),
+            ring_space((ys, o_rows, cols_o)),
+            ring_sems,
+            ring_sems,
+            pltpu.SemaphoreType.DMA((ys - 1,)),
+            pltpu.SemaphoreType.DMA((ys - 1,)),
+            pltpu.SemaphoreType.DMA((ys - 1,)),
+            pltpu.SemaphoreType.DMA((ys - 1,)),
+        ],
+        compiler_params=pltpu.CompilerParams(
+            collective_id=2, has_side_effects=True, vmem_limit_bytes=48 * 1024 * 1024
+        ),
+    )(xv, xo)
+
+
 DP = ("y", "z")
-
-
-def scatter_in_stages(block):
-    inner = lax.psum_scatter(block, "y", scatter_dimension=0, tiled=True)
-    return lax.psum_scatter(inner, "z", scatter_dimension=0, tiled=True).astype(jnp.float32)
-
-
-def scatter_by_exchange(block):
-    count = lax.axis_size(DP)
-    parts = block.reshape((count, block.shape[0] // count) + block.shape[1:])
-    arrived = lax.all_to_all(parts, DP, 0, 0, tiled=False)
-    return jnp.sum(arrived.astype(jnp.float32), axis=0)
 
 
 def on_device(inputs, cotangent, value_weight, output_weight, norm_gain, value_noise, output_noise):
@@ -398,17 +540,13 @@
     )
     value_rows = kept_values.reshape(-1, head_width)
     columns = normed_rows
-    value_part = scatter_in_stages(
-        lax.dot_general(
-            columns, scaled_dvalues, (((0,), (0,)), ((), ())), preferred_element_type=jnp.float32
-        ).astype(jnp.bfloat16)
-    )
-    columns = value_rows
-    output_part = scatter_by_exchange(
-        lax.dot_general(
-            columns, scaled_grads, (((0,), (0,)), ((), ())), preferred_element_type=jnp.float32
-        ).astype(jnp.bfloat16)
-    )
+    value_block = lax.dot_general(
+        normed_rows, scaled_dvalues, (((0,), (0,)), ((), ())), preferred_element_type=jnp.float32
+    ).astype(jnp.bfloat16)
+    output_block = lax.dot_general(
+        value_rows, scaled_grads, (((0,), (0,)), ((), ())), preferred_element_type=jnp.float32
+    ).astype(jnp.bfloat16)
+    value_part, output_part = scatter_grads(value_block, output_block)
     grad_scale = math.sqrt(feature_width * head_width)
     value_grad = (value_part * grad_scale + value_noise[0])[None]
     output_grad = (output_part * grad_scale + output_noise[0])[None]

time: 329 us -> 270 us (0.82)
  waiting for transfers between devices: 109 us -> 0 us
  Pallas kernels: 144 us -> 217 us
  between operations: 16.7 us -> 3.35 us
  starting transfers between devices: 5.97 us -> 0 us
  matrix products: 10.2 us -> 6.32 us
  other arithmetic: 5.46 us -> 1.91 us
    reduce_scatter x2 -> x0, waiting for transfers between devices: 89.3 us -> none  [the longest x1 65.1 us: scatter_in_stages(): inner = lax.psum_scatter(block, 'y', scatter_dimension=0, tiled=True)]
    pallas_call x0 -> x1, Pallas kernels: none -> 72.8 us  [scatter_grads(): pl.pallas_call(functools.partial(scatter_kernel, ys, zs), out_shape=(jax....]
    all_to_all x1 -> x0, waiting for transfers between devices: 19.6 us -> none  [scatter_by_exchange(): arrived = lax.all_to_all(parts, DP, 0, 0, tiled=False)]
    all_to_all x1 -> x0, starting transfers between devices: 5.89 us -> none  [scatter_by_exchange(): arrived = lax.all_to_all(parts, DP, 0, 0, tiled=False)]
    dot_general x2, matrix products: 6.18 us -> 2.42 us  [the longest x1 1.23 us: on_device(): lax.dot_general(normed_rows, scaled_dvalues, (((0,), (0,)), ((), ())), pr...]
  transfers between devices with their start and end apart: 3 -> 0, of which waited for: 3 -> 0; matrix products, arithmetic and copies ran while one was open for 2% -> 0% of each run, Pallas kernels for 0% -> 0%
where the time goes in v6:
time: 270 us; the launch traced here: 268 us
  Pallas kernels  217 us (80%)
  blocking collectives  31.8 us (12%)
  local copies, waits for them, and re-layouts  6.95 us (3%)
  matrix products  6.32 us (2%)
  between operations  3.35 us (1%)
    pallas_call x1, Pallas kernels, run_chain(): pl.pallas_call(functools.partial(chain_kernel, sections), out_shape=(act,...  76.3 us
    pallas_call x1, Pallas kernels, scatter_grads(): pl.pallas_call(functools.partial(scatter_kernel, ys, zs), out_shape=(jax....  72.8 us
    pallas_call x1, Pallas kernels, gather_weights(): pl.pallas_call(functools.partial(gather_kernel, ys, zs), out_shape=(jax.S...  68.2 us
    psum x1, blocking collectives, on_device(): total_squares = lax.psum(partial_squares, 'section')  31.8 us

profile of v6, /device:TPU:4, one launch (start us, length us, event | category | flops | bytes accessed | tf_op | source)
XLA Modules:
  0.0 267.7 jit_solution(16448288990267645433)
XLA Ops:
  0.6 68.2 %shard_map.86 = (bf16[4,8,56,1024]{3,2,1,0:T(8,128)(2,1)}, bf16[4,8,32,1792]{3,2,1,0:T(8,128)(2,1)}) custom-call(bf16[56,1024]{1,0:T(8,128)(2,1)} %bitcast.63, bf16[32,1792]{1,0:T(8,128)(2,1)} %bitcast.64), custom_call_target="tpu_custom_call" | custom-call | tf_op jit(solution)/shard_map/pallas_call | solution.py:331
  68.8 0.0 copy-start
  68.8 2.0 copy-done
  70.8 0.0 copy-start.1
  70.8 1.0 copy-done.1
  71.9 1.0 copy-done.2
  72.9 0.7 copy-done.3
  73.6 76.3 %shard_map.87 = (bf16[2,64,1792]{2,1,0:T(8,128)(2,1)S(1)}, bf16[2,64,1024]{2,1,0:T(8,128)(2,1)S(1)}, bf16[2,64,1792]{2,1,0:T(8,128)(2,1)S(1)}, bf16[2,64,1024]{2,1,0:T(8,128)(2,1)S(1)}) custom-call(bf16[2,64,1792]{2,1,0:T(8,128)(2,1)S(1)} %bitcast.58, bf16[2,64,1792]{2,1,0:T(8,128)(2,1)S(1)} %bitcast.59, f32[1,1792]{1,0:T(1,128)S(1)} %copy-done.3, ...), custom_call_target="tpu_custom_call" | custom-call | tf_op jit(solution)/shard_map/pallas_call | solution.py:187
  149.9 0.2 multiply_reduce_fusion
  150.1 0.1 rsqrt.13
  150.2 0.0 copy-done.4
  150.2 0.2 fusion.1
  150.4 0.2 fusion.13
  150.6 0.8 fusion.2
  151.4 0.2 fusion.19
  151.6 0.8 fusion.3
  153.7 0.2 fusion.11
  153.9 0.8 fusion.4
  154.7 0.2 fusion.17
  154.9 0.8 fusion.5
  156.9 0.1 pad_maximum_fusion
  157.0 31.8 %psum.7 = f32[2,1]{0,1:T(1,128)S(1)} all-reduce(f32[2,1]{0,1:T(1,128)S(1)} %pad_maximum_fusion), channel_id=1, replica_groups=mesh['section'=8,'y'=4,'z'=8] {'section'}, use_global_device_ids=true, to_apply=%region_5.0 | all-reduce | flops 2 | bytes 16 | tf_op jit(solution)/shard_map/psum | solution.py:528
  188.9 1.2 bitcast_convert_fusion
  190.1 2.1 copy.11
  192.2 1.2 bitcast_convert_fusion.1
  193.4 0.0 copy-start.5
  193.4 0.0 copy-start.6
  193.4 72.8 %shard_map.88 = (f32[56,1024]{1,0:T(8,128)S(1)}, f32[32,1792]{1,0:T(8,128)S(1)}) custom-call(bf16[4,8,56,1024]{3,2,1,0:T(8,128)(2,1)S(1)} %bitcast.56, bf16[8,4,32,1792]{3,2,1,0:T(8,128)(2,1)} %bitcast.61), custom_call_target="tpu_custom_call" | custom-call | tf_op jit(solution)/shard_map/pallas_call | solution.py:475
  266.2 0.0 copy-done.5
  266.2 0.7 fusion.15
  267.0 0.0 copy-done.6
  267.0 0.7 fusion.16
  (6 shorter events, 0.0 us)
Async XLA Ops:
  68.8 2.0 copy-start
  70.8 1.0 copy-start.1
  71.9 1.0 copy-start.2
  72.9 0.7 copy-start.3
  73.6 76.6 %copy-start.4 = (f32[1,1792]{1,0:T(1,128)S(1)}, f32[1,1792]{1,0:T(1,128)}, u32[]{:S(2)}) copy-start(f32[1,1792]{1,0:T(1,128)} %gain_ref.1) | copy-start | bytes 21508
  193.4 72.8 %copy-start.5 = (f32[1,32,1792]{2,1,0:T(8,128)S(1)}, f32[1,32,1792]{2,1,0:T(8,128)}, u32[]{:S(2)}) copy-start(f32[1,32,1792]{2,1,0:T(8,128)} %param.13) | copy-start | bytes 688132
  193.4 73.5 %copy-start.6 = (f32[1,56,1024]{2,1,0:T(8,128)S(1)}, f32[1,56,1024]{2,1,0:T(8,128)}, u32[]{:S(2)}) copy-start(f32[1,56,1024]{2,1,0:T(8,128)} %param.12) | copy-start | bytes 688132

commit v7 on v6

--- a/solution.py
+++ b/solution.py
@@ -206,60 +206,60 @@
     )(feed_rows, cot_rows, gains.reshape(1, width), value_matrix, output_matrix)
 
 
-def ring_copies(window, first_src, z, zs, sems):
-    mesh_ids = pl.DeviceIdType.MESH
+class Ring:
+    def __init__(self, me, n, axis, step):
+        self.me, self.n, self.axis, self.step = me, n, axis, step
+        self.rights, self.lefts = n // 2, (n - 1) // 2
+
+    def at(self, offset):
+        return lax.rem(self.me + 2 * self.n + self.step * offset, self.n)
+
+    def copy(self, src, dst, send_sem, recv_sem, toward):
+        return pltpu.make_async_remote_copy(
+            src_ref=src, dst_ref=dst, send_sem=send_sem, recv_sem=recv_sem,
+            device_id={self.axis: toward}, device_id_type=pl.DeviceIdType.MESH,
+        )
+
+
+def ring_copies(window, first_src, ring, sems):
     right_send, right_recv, left_send, left_recv = sems
-    rights, lefts = zs // 2, (zs - 1) // 2
-
-    def right(t):
-        slot = lax.rem(z + zs - t, zs)
-        return pltpu.make_async_remote_copy(
-            src_ref=first_src if t == 0 else window(slot), dst_ref=window(slot),
-            send_sem=right_send.at[t], recv_sem=right_recv.at[t],
-            device_id={"z": lax.rem(z + 1, zs)}, device_id_type=mesh_ids,
-        )
-
-    def left(t):
-        slot = lax.rem(z + t, zs)
-        return pltpu.make_async_remote_copy(
-            src_ref=first_src if t == 0 else window(slot), dst_ref=window(slot),
-            send_sem=left_send.at[t], recv_sem=left_recv.at[t],
-            device_id={"z": lax.rem(z + zs - 1, zs)}, device_id_type=mesh_ids,
-        )
-
-    def right_in(t):
-        return pltpu.make_async_remote_copy(
-            src_ref=first_src, dst_ref=window(lax.rem(z + 2 * zs - 1 - t, zs)),
-            send_sem=right_send.at[t], recv_sem=right_recv.at[t],
-            device_id={"z": z}, device_id_type=mesh_ids,
-        )
-
-    def left_in(t):
-        return pltpu.make_async_remote_copy(
-            src_ref=first_src, dst_ref=window(lax.rem(z + 1 + t, zs)),
-            send_sem=left_send.at[t], recv_sem=left_recv.at[t],
-            device_id={"z": z}, device_id_type=mesh_ids,
-        )
-
-    def run():
-        for t in range(rights):
-            right(t).start()
-            if t < lefts:
-                left(t).start()
-            right_in(t).wait_recv()
-            if t < lefts:
-                left_in(t).wait_recv()
+
+    def right(t, slot):
+        return ring.copy(first_src if t == 0 else window(slot), window(slot), right_send.at[t], right_recv.at[t], ring.at(1))
+
+    def left(t, slot):
+        return ring.copy(first_src if t == 0 else window(slot), window(slot), left_send.at[t], left_recv.at[t], ring.at(-1))
+
+    def start(t):
+        if t < ring.rights:
+            right(t, ring.at(-t)).start()
+        if t < ring.lefts:
+            left(t, ring.at(t)).start()
+
+    def wait(t):
+        if t < ring.rights:
+            ring.copy(first_src, window(ring.at(-1 - t)), right_send.at[t], right_recv.at[t], ring.me).wait_recv()
+        if t < ring.lefts:
+            ring.copy(first_src, window(ring.at(1 + t)), left_send.at[t], left_recv.at[t], ring.me).wait_recv()
 
     def finish():
-        for t in range(rights):
-            right(t).wait_send()
-        for t in range(lefts):
-            left(t).wait_send()
-
-    return run, finish
-
-
-def gather_kernel(ys, zs, wv_ref, wo_ref, wv_all, wo_all, own_sem, va, vb_send, vb_recv, oa_send, oa_recv, ob):
+        for t in range(ring.rights):
+            right(t, ring.at(-t)).wait_send()
+        for t in range(ring.lefts):
+            left(t, ring.at(t)).wait_send()
+
+    return start, wait, finish, ring.rights
+
+
+def run_rings(rings):
+    for t in range(max(r[3] for r in rings)):
+        for r in rings:
+            r[0](t)
+        for r in rings:
+            r[1](t)
+
+
+def gather_kernel(ys, zs, wv_ref, wo_ref, wv_all, wo_all, own_sem, va, vb, vc, oa_send, oa_recv, ob, oc):
     y = lax.axis_index("y")
     z = lax.axis_index("z")
     mesh_ids = pl.DeviceIdType.MESH
@@ -287,47 +287,48 @@
             recv_sem=oa_recv.at[k - 1], device_id={"y": y}, device_id_type=mesh_ids,
         )
 
-    def v_second(k, row, target):
-        return pltpu.make_async_remote_copy(
-            src_ref=wv_all.at[pl.ds(row, 1)], dst_ref=wv_all.at[pl.ds(row, 1)],
-            send_sem=vb_send.at[k - 1], recv_sem=vb_recv.at[k - 1],
-            device_id={"y": target}, device_id_type=mesh_ids,
-        )
-
     for k in range(1, ys):
         o_first(k, lax.rem(y + k, ys)).start()
-    v_ring, v_ring_done = ring_copies(lambda o: wv_all.at[y, o], wv_ref, z, zs, va)
-    v_ring()
+    v_ring = ring_copies(lambda o: wv_all.at[y, o], wv_ref, Ring(z, zs, "z", 1), va)
+    run_rings([v_ring])
     own_v.wait()
     own_o.wait()
     for k in range(1, ys):
         o_first_in(k).wait_recv()
-    for k in range(1, ys):
-        v_second(k, y, lax.rem(y + k, ys)).start()
-    o_ring, o_ring_done = ring_copies(
-        lambda o: wo_all.at[:, pl.ds(o, 1)], wo_all.at[:, pl.ds(z, 1)], z, zs, ob
-    )
-    o_ring()
-    v_ring_done()
+    v_half = wv_all.shape[-1] // 2
+    o_half = wo_all.shape[-1] // 2
+    second = []
+    for part, (step, sems_v, sems_o) in enumerate(((1, vb, ob), (-1, vc, oc))):
+        v_cols = pl.ds(part * v_half, v_half)
+        o_cols = pl.ds(part * o_half, o_half)
+        second.append(ring_copies(
+            lambda o, c=v_cols: wv_all.at[pl.ds(o, 1), :, :, c], wv_all.at[pl.ds(y, 1), :, :, v_cols],
+            Ring(y, ys, "y", step), sems_v,
+        ))
+        second.append(ring_copies(
+            lambda o, c=o_cols: wo_all.at[:, pl.ds(o, 1), :, c], wo_all.at[:, pl.ds(z, 1), :, o_cols],
+            Ring(z, zs, "z", step), sems_o,
+        ))
+    run_rings(second)
+    v_ring[2]()
     for k in range(1, ys):
         o_first(k, lax.rem(y + k, ys)).wait_send()
-    for k in range(1, ys):
-        v_second(k, lax.rem(y + ys - k, ys), y).wait_recv()
-    o_ring_done()
-    for k in range(1, ys):
-        v_second(k, y, lax.rem(y + k, ys)).wait_send()
+    for r in second:
+        r[2]()
 
 
 def gather_weights(value_shard, output_shard):
     ys = lax.axis_size("y")
     zs = lax.axis_size("z")
     anywhere = pl.BlockSpec(memory_space=pl.ANY)
-    ring_sems = [
-        pltpu.SemaphoreType.DMA((zs // 2,)),
-        pltpu.SemaphoreType.DMA((zs // 2,)),
-        pltpu.SemaphoreType.DMA((max((zs - 1) // 2, 1),)),
-        pltpu.SemaphoreType.DMA((max((zs - 1) // 2, 1),)),
-    ]
+    def ring_sems(n):
+        return [
+            pltpu.SemaphoreType.DMA((n // 2,)),
+            pltpu.SemaphoreType.DMA((n // 2,)),
+            pltpu.SemaphoreType.DMA((max((n - 1) // 2, 1),)),
+            pltpu.SemaphoreType.DMA((max((n - 1) // 2, 1),)),
+        ]
+
     wv_all, wo_all = pl.pallas_call(
         functools.partial(gather_kernel, ys, zs),
         out_shape=(
@@ -336,9 +337,16 @@
         ),
         in_specs=[anywhere] * 2,
         out_specs=(anywhere, anywhere),
-        scratch_shapes=[pltpu.SemaphoreType.DMA((2,)), ring_sems]
-        + [pltpu.SemaphoreType.DMA((ys - 1,))] * 4
-        + [ring_sems],
+        scratch_shapes=[
+            pltpu.SemaphoreType.DMA((2,)),
+            ring_sems(zs),
+            ring_sems(ys),
+            ring_sems(ys),
+            pltpu.SemaphoreType.DMA((ys - 1,)),
+            pltpu.SemaphoreType.DMA((ys - 1,)),
+            ring_sems(zs),
+            ring_sems(zs),
+        ],
         compiler_params=pltpu.CompilerParams(collective_id=1, has_side_effects=True),
     )(value_shard, output_shard)
     return (
@@ -347,50 +355,49 @@
     )
 
 
-def ring_sum(get, z, zs, bufs, sems):
-    mesh_ids = pl.DeviceIdType.MESH
+def ring_sum(get, ring, bufs, sems):
     rsend, rrecv, lsend, lrecv = bufs
     rs_send, rs_recv, ls_send, ls_recv = sems
-    rights, lefts = zs // 2, (zs - 1) // 2
 
     def right(t):
-        return pltpu.make_async_remote_copy(
-            src_ref=rsend.at[t], dst_ref=rrecv.at[t], send_sem=rs_send.at[t], recv_sem=rs_recv.at[t],
-            device_id={"z": lax.rem(z + 1, zs)}, device_id_type=mesh_ids,
-        )
+        return ring.copy(rsend.at[t], rrecv.at[t], rs_send.at[t], rs_recv.at[t], ring.at(1))
 
     def left(t):
-        return pltpu.make_async_remote_copy(
-            src_ref=lsend.at[t], dst_ref=lrecv.at[t], send_sem=ls_send.at[t], recv_sem=ls_recv.at[t],
-            device_id={"z": lax.rem(z + zs - 1, zs)}, device_id_type=mesh_ids,
-        )
-
-    for t in range(rights):
-        value = get(lax.rem(z + rights - t, zs))
-        if t > 0:
-            value = value + rrecv[t - 1].astype(jnp.float32)
-        rsend[t] = value.astype(rsend.dtype)
-        right(t).start()
-        if t < lefts:
-            value = get(lax.rem(z + zs - lefts + t, zs))
+        return ring.copy(lsend.at[t], lrecv.at[t], ls_send.at[t], ls_recv.at[t], ring.at(-1))
+
+    def start(t):
+        if t < ring.rights:
+            value = get(ring.at(ring.rights - t))
+            if t > 0:
+                value = value + rrecv[t - 1].astype(jnp.float32)
+            rsend[t] = value.astype(rsend.dtype)
+            right(t).start()
+        if t < ring.lefts:
+            value = get(ring.at(t - ring.lefts))
             if t > 0:
                 value = value + lrecv[t - 1].astype(jnp.float32)
             lsend[t] = value.astype(lsend.dtype)
             left(t).start()
-        right(t).wait_recv()
-        if t < lefts:
+
+    def wait(t):
+        if t < ring.rights:
+            right(t).wait_recv()
+        if t < ring.lefts:
             left(t).wait_recv()
-    total = get(z) + rrecv[rights - 1].astype(jnp.float32)
-    if lefts > 0:
-        total = total + lrecv[lefts - 1].astype(jnp.float32)
 
     def finish():
-        for t in range(rights):
+        for t in range(ring.rights):
             right(t).wait_send()
-        for t in range(lefts):
+        for t in range(ring.lefts):
             left(t).wait_send()
 
-    return total, finish
+    def total():
+        result = get(ring.me) + rrecv[ring.rights - 1].astype(jnp.float32)
+        if ring.lefts > 0:
+            result = result + lrecv[ring.lefts - 1].astype(jnp.float32)
+        return result
+
+    return start, wait, finish, ring.rights, total
 
 
 def direct_copies(source, landing, axis, me, count, send_sems, recv_sems):
@@ -406,7 +413,7 @@
 
 def scatter_kernel(
     ys, zs, xv_ref, xo_ref, out_v, out_o,
-    v_land, v_part, o_part, o_send, o_land, v_ring, o_ring, v_sems, o_sems, vd_send, vd_recv, od_send, od_recv,
+    v_part, o_part, o_send, o_land, v_rings, o_rings, v_ring, v_sems, o_sems, vz_sems, od_send, od_recv,
 ):
     y = lax.axis_index("y")
     z = lax.axis_index("z")
@@ -418,30 +425,38 @@
         pl.semaphore_signal(barrier, inc=1, device_id={"y": lax.rem(y + k, ys)}, device_id_type=mesh_ids)
     pl.semaphore_wait(barrier, ys + 1)
 
-    v_copies = direct_copies(xv_ref, v_land, "y", y, ys, vd_send, vd_recv)
-    for c in v_copies:
-        c.start()
-    o_total, o_finish = ring_sum(lambda d: xo_ref[d].astype(jnp.float32), z, zs, o_ring, o_sems)
-    o_part[...] = o_total
-    o_send[...] = o_total.astype(o_send.dtype)
+    v_half = xv_ref.shape[-1] // 2
+    o_half = xo_ref.shape[-1] // 2
+    first = []
+    for part, step in enumerate((1, -1)):
+        vc = slice(part * v_half, (part + 1) * v_half)
+        oc = slice(part * o_half, (part + 1) * o_half)
+        first.append(ring_sum(
+            lambda d, c=vc: xv_ref[d, :, :, c].astype(jnp.float32), Ring(y, ys, "y", step), v_rings[part], v_sems[part]
+        ))
+        first.append(ring_sum(
+            lambda d, c=oc: xo_ref[d, :, :, c].astype(jnp.float32), Ring(z, zs, "z", step), o_rings[part], o_sems[part]
+        ))
+    run_rings(first)
+    for part in range(2):
+        o_total = first[2 * part + 1][4]()
+        o_part[:, :, part * o_half:(part + 1) * o_half] = o_total
+        o_send[:, :, part * o_half:(part + 1) * o_half] = o_total.astype(o_send.dtype)
+        v_part[:, :, part * v_half:(part + 1) * v_half] = first[2 * part][4]()
     o_copies = direct_copies(o_send, o_land, "y", y, ys, od_send, od_recv)
     for c in o_copies:
         c.start()
-    v_sum = xv_ref[y].astype(jnp.float32)
-    for k, c in enumerate(v_copies):
-        c.wait_recv()
-        v_sum = v_sum + v_land[k].astype(jnp.float32)
-    v_part[...] = v_sum
-    v_total, v_finish = ring_sum(lambda d: v_part[d], z, zs, v_ring, v_sems)
-    out_v[...] = v_total
+    v_second = ring_sum(lambda d: v_part[d], Ring(z, zs, "z", 1), v_ring, vz_sems)
+    run_rings([v_second])
+    out_v[...] = v_second[4]()
     o_sum = o_part[y]
     for k, c in enumerate(o_copies):
         c.wait_recv()
         o_sum = o_sum + o_land[k].astype(jnp.float32)
     out_o[...] = o_sum
-    o_finish()
-    v_finish()
-    for c in v_copies + o_copies:
+    for r in first + [v_second]:
+        r[2]()
+    for c in o_copies:
         c.wait_send()
 
 
@@ -455,23 +470,26 @@
     xv = value_block.reshape(ys, zs, v_rows, cols_v)
     xo = output_block.reshape(ys, zs, o_rows, cols_o).transpose(1, 0, 2, 3)
     vmem = pl.BlockSpec(memory_space=pltpu.VMEM)
-    rights, lefts = zs // 2, max((zs - 1) // 2, 1)
     bf = value_block.dtype
 
-    def ring_space(block):
+    def ring_space(n, block):
         return [
-            pltpu.VMEM((rights,) + block, bf),
-            pltpu.VMEM((rights,) + block, bf),
-            pltpu.VMEM((lefts,) + block, bf),
-            pltpu.VMEM((lefts,) + block, bf),
+            pltpu.VMEM((n // 2,) + block, bf),
+            pltpu.VMEM((n // 2,) + block, bf),
+            pltpu.VMEM((max((n - 1) // 2, 1),) + block, bf),
+            pltpu.VMEM((max((n - 1) // 2, 1),) + block, bf),
         ]
 
-    ring_sems = [
-        pltpu.SemaphoreType.DMA((rights,)),
-        pltpu.SemaphoreType.DMA((rights,)),
-        pltpu.SemaphoreType.DMA((lefts,)),
-        pltpu.SemaphoreType.DMA((lefts,)),
-    ]
+    def ring_sems(n):
+        return [
+            pltpu.SemaphoreType.DMA((n // 2,)),
+            pltpu.SemaphoreType.DMA((n // 2,)),
+            pltpu.SemaphoreType.DMA((max((n - 1) // 2, 1),)),
+            pltpu.SemaphoreType.DMA((max((n - 1) // 2, 1),)),
+        ]
+
+    v_block = (zs, v_rows, cols_v // 2)
+    o_block = (ys, o_rows, cols_o // 2)
     return pl.pallas_call(
         functools.partial(scatter_kernel, ys, zs),
         out_shape=(
@@ -481,17 +499,16 @@
         in_specs=[vmem, vmem],
         out_specs=(vmem, vmem),
         scratch_shapes=[
-            pltpu.VMEM((ys - 1, zs, v_rows, cols_v), bf),
             pltpu.VMEM((zs, v_rows, cols_v), jnp.float32),
             pltpu.VMEM((ys, o_rows, cols_o), jnp.float32),
             pltpu.VMEM((ys, o_rows, cols_o), bf),
             pltpu.VMEM((ys - 1, o_rows, cols_o), bf),
-            ring_space((v_rows, cols_v)),
-            ring_space((ys, o_rows, cols_o)),
-            ring_sems,
-            ring_sems,
-            pltpu.SemaphoreType.DMA((ys - 1,)),
-            pltpu.SemaphoreType.DMA((ys - 1,)),
+            [ring_space(ys, v_block), ring_space(ys, v_block)],
+            [ring_space(zs, o_block), ring_space(zs, o_block)],
+            ring_space(zs, (v_rows, cols_v)),
+            [ring_sems(ys), ring_sems(ys)],
+            [ring_sems(zs), ring_sems(zs)],
+            ring_sems(zs),
             pltpu.SemaphoreType.DMA((ys - 1,)),
             pltpu.SemaphoreType.DMA((ys - 1,)),
         ],

time: 270 us -> 283 us (1.048)
  Pallas kernels: 217 us -> 229 us
    pallas_call x1, Pallas kernels: 68.2 us -> 76.2 us  [gather_weights(): pl.pallas_call(functools.partial(gather_kernel, ys, zs), out_shape=(jax.S...]
    pallas_call x1, Pallas kernels: 72.8 us -> 76.8 us  [scatter_grads(): pl.pallas_call(functools.partial(scatter_kernel, ys, zs), out_shape=(jax....]
where the time goes in v7:
time: 283 us; the launch traced here: 280 us
  Pallas kernels  229 us (81%)
  blocking collectives  31.8 us (11%)
  local copies, waits for them, and re-layouts  6.95 us (2%)
  matrix products  6.32 us (2%)
  between operations  3.35 us (1%)
    pallas_call x1, Pallas kernels, scatter_grads(): pl.pallas_call(functools.partial(scatter_kernel, ys, zs), out_shape=(jax....  76.8 us
    pallas_call x1, Pallas kernels, run_chain(): pl.pallas_call(functools.partial(chain_kernel, sections), out_shape=(act,...  76.3 us
    pallas_call x1, Pallas kernels, gather_weights(): pl.pallas_call(functools.partial(gather_kernel, ys, zs), out_shape=(jax.S...  76.2 us
    psum x1, blocking collectives, on_device(): total_squares = lax.psum(partial_squares, 'section')  31.8 us

profile of v7, /device:TPU:4, one launch (start us, length us, event | category | flops | bytes accessed | tf_op | source)
XLA Modules:
  0.0 279.8 jit_solution(3758608631037541521)
XLA Ops:
  0.6 76.2 %shard_map.86 = (bf16[4,8,56,1024]{3,2,1,0:T(8,128)(2,1)}, bf16[4,8,32,1792]{3,2,1,0:T(8,128)(2,1)}) custom-call(bf16[56,1024]{1,0:T(8,128)(2,1)} %bitcast.63, bf16[32,1792]{1,0:T(8,128)(2,1)} %bitcast.64), custom_call_target="tpu_custom_call" | custom-call | tf_op jit(solution)/shard_map/pallas_call | solution.py:332
  76.9 0.0 copy-start
  76.9 2.0 copy-done
  78.9 0.0 copy-start.1
  78.9 1.0 copy-done.1
  79.9 1.0 copy-done.2
  81.0 0.7 copy-done.3
  81.6 76.3 %shard_map.87 = (bf16[2,64,1792]{2,1,0:T(8,128)(2,1)S(1)}, bf16[2,64,1024]{2,1,0:T(8,128)(2,1)S(1)}, bf16[2,64,1792]{2,1,0:T(8,128)(2,1)S(1)}, bf16[2,64,1024]{2,1,0:T(8,128)(2,1)S(1)}) custom-call(bf16[2,64,1792]{2,1,0:T(8,128)(2,1)S(1)} %bitcast.58, bf16[2,64,1792]{2,1,0:T(8,128)(2,1)S(1)} %bitcast.59, f32[1,1792]{1,0:T(1,128)S(1)} %copy-done.3, ...), custom_call_target="tpu_custom_call" | custom-call | tf_op jit(solution)/shard_map/pallas_call | solution.py:187
  158.0 0.2 multiply_reduce_fusion
  158.2 0.1 rsqrt.13
  158.3 0.0 copy-done.4
  158.3 0.2 fusion.1
  158.5 0.2 fusion.13
  158.7 0.8 fusion.2
  159.5 0.2 fusion.19
  159.7 0.8 fusion.3
  161.8 0.2 fusion.11
  162.0 0.8 fusion.4
  162.7 0.2 fusion.17
  162.9 0.8 fusion.5
  165.0 0.1 pad_maximum_fusion
  165.1 31.8 %psum.7 = f32[2,1]{0,1:T(1,128)S(1)} all-reduce(f32[2,1]{0,1:T(1,128)S(1)} %pad_maximum_fusion), channel_id=1, replica_groups=mesh['section'=8,'y'=4,'z'=8] {'section'}, use_global_device_ids=true, to_apply=%region_5.0 | all-reduce | flops 2 | bytes 16 | tf_op jit(solution)/shard_map/psum | solution.py:545
  196.9 1.2 bitcast_convert_fusion
  198.1 2.1 copy.11
  200.2 1.2 bitcast_convert_fusion.1
  201.5 0.0 copy-start.5
  201.5 0.0 copy-start.6
  201.5 76.8 %shard_map.88 = (f32[56,1024]{1,0:T(8,128)S(1)}, f32[32,1792]{1,0:T(8,128)S(1)}) custom-call(bf16[4,8,56,1024]{3,2,1,0:T(8,128)(2,1)S(1)} %bitcast.56, bf16[8,4,32,1792]{3,2,1,0:T(8,128)(2,1)} %bitcast.61), custom_call_target="tpu_custom_call" | custom-call | tf_op jit(solution)/shard_map/pallas_call | solution.py:493
  278.3 0.0 copy-done.5
  278.3 0.7 fusion.15
  279.0 0.0 copy-done.6
  279.0 0.7 fusion.16
  (6 shorter events, 0.0 us)
Async XLA Ops:
  76.9 2.0 copy-start
  78.9 1.0 copy-start.1
  79.9 1.0 copy-start.2
  81.0 0.7 copy-start.3
  81.6 76.6 %copy-start.4 = (f32[1,1792]{1,0:T(1,128)S(1)}, f32[1,1792]{1,0:T(1,128)}, u32[]{:S(2)}) copy-start(f32[1,1792]{1,0:T(1,128)} %gain_ref.1) | copy-start | bytes 21508
  201.5 76.9 %copy-start.5 = (f32[1,32,1792]{2,1,0:T(8,128)S(1)}, f32[1,32,1792]{2,1,0:T(8,128)}, u32[]{:S(2)}) copy-start(f32[1,32,1792]{2,1,0:T(8,128)} %param.13) | copy-start | bytes 688132
  201.5 77.6 %copy-start.6 = (f32[1,56,1024]{2,1,0:T(8,128)S(1)}, f32[1,56,1024]{2,1,0:T(8,128)}, u32[]{:S(2)}) copy-start(f32[1,56,1024]{2,1,0:T(8,128)} %param.12) | copy-start | bytes 688132

commit v8 on v6

--- a/solution.py
+++ b/solution.py
@@ -49,10 +49,10 @@
 
 
 def chain_kernel(
-    sections,
+    sections, seq_len,
     seed_ref, cot_ref, gain_ref, wv_ref, wo_ref,
-    kin_ref, kval_ref, kgrad_ref, kdv_ref,
-    fbuf, fres, bbuf, bres, work, fsend, frecv, bsend, brecv,
+    kin_ref, kval_ref, kgrad_ref, kdv_ref, total_ref,
+    fbuf, fres, bbuf, bres, work, fsend, frecv, bsend, brecv, sq_mine, sq_all, sq_send, sq_recv,
 ):
     place = lax.axis_index("section")
     micro_count, rows, width = seed_ref.shape
@@ -63,17 +63,11 @@
     last = place == sections - 1
 
     barrier = pltpu.get_barrier_semaphore()
-
-    @pl.when(place > 0)
-    def _():
-        pl.semaphore_signal(barrier, inc=1, device_id={"section": behind}, device_id_type=pl.DeviceIdType.MESH)
-
-    @pl.when(place < sections - 1)
-    def _():
-        pl.semaphore_signal(barrier, inc=1, device_id={"section": ahead}, device_id_type=pl.DeviceIdType.MESH)
-
-    peers = (place + sections - 1) // sections + (2 * sections - 2 - place) // sections
-    pl.semaphore_wait(barrier, peers)
+    for k in range(1, sections):
+        pl.semaphore_signal(
+            barrier, inc=1, device_id={"section": lax.rem(place + k, sections)}, device_id_type=pl.DeviceIdType.MESH
+        )
+    pl.semaphore_wait(barrier, sections - 1)
 
     @pl.when(first)
     def _():
@@ -167,6 +161,40 @@
         def _():
             backward_copy(m).start()
 
+    lane = lax.broadcasted_iota(jnp.int32, sq_mine.shape, 1)
+    row = lax.broadcasted_iota(jnp.int32, sq_mine.shape, 0)
+    squares = jnp.zeros(sq_mine.shape, jnp.float32)
+    for m in range(micro_count):
+        wide = kin_ref[m].astype(jnp.float32)
+        inverse = lax.rsqrt(jnp.mean(wide * wide, axis=-1, keepdims=True) + 1e-06)
+        normed = (wide * inverse * gain_ref[...]).astype(jnp.bfloat16)
+        for e in range(rows // seq_len):
+            span = slice(e * seq_len, (e + 1) * seq_len)
+            pairs = ((normed[span], kdv_ref[m, span]), (kval_ref[m, span], kgrad_ref[m, span]))
+            term = 0.0
+            for left_part, right_part in pairs:
+                gram_left = lax.dot_general(left_part, left_part, contract, preferred_element_type=jnp.float32)
+                gram_right = lax.dot_general(right_part, right_part, contract, preferred_element_type=jnp.float32)
+                term = term + jnp.sum(gram_left * gram_right)
+            squares = jnp.where((row == m) & (lane == e), term, squares)
+    sq_mine[...] = squares
+
+    def share(k):
+        return pltpu.make_async_remote_copy(
+            src_ref=sq_mine, dst_ref=sq_all.at[k - 1], send_sem=sq_send.at[k - 1], recv_sem=sq_recv.at[k - 1],
+            device_id={"section": lax.rem(place + k, sections)}, device_id_type=pl.DeviceIdType.MESH,
+        )
+
+    for k in range(1, sections):
+        share(k).start()
+    total = squares
+    for k in range(1, sections):
+        share(k).wait_recv()
+        total = total + sq_all[k - 1]
+    total_ref[...] = total
+
+    for k in range(1, sections):
+        share(k).wait_send()
     for m in range(micro_count):
         @pl.when(place < sections - 1)
         def _():
@@ -177,7 +205,7 @@
             backward_copy(m).wait_send()
 
 
-def run_chain(feed_rows, cot_rows, gains, value_matrix, output_matrix):
+def run_chain(feed_rows, cot_rows, gains, value_matrix, output_matrix, seq_len):
     sections = lax.axis_size("section")
     micro_count, rows, width = feed_rows.shape
     heads = value_matrix.shape[1]
@@ -185,10 +213,10 @@
     act = jax.ShapeDtypeStruct((micro_count, rows, width), jnp.bfloat16)
     head_act = jax.ShapeDtypeStruct((micro_count, rows, heads), jnp.bfloat16)
     return pl.pallas_call(
-        functools.partial(chain_kernel, sections),
-        out_shape=(act, head_act, act, head_act),
+        functools.partial(chain_kernel, sections, seq_len),
+        out_shape=(act, head_act, act, head_act, jax.ShapeDtypeStruct((8, 128), jnp.float32)),
         in_specs=[vmem] * 5,
-        out_specs=(vmem,) * 4,
+        out_specs=(vmem,) * 5,
         scratch_shapes=[
             pltpu.VMEM((micro_count, rows, width), jnp.bfloat16),
             pltpu.VMEM((micro_count, rows, width), jnp.bfloat16),
@@ -199,6 +227,10 @@
             pltpu.SemaphoreType.DMA((micro_count,)),
             pltpu.SemaphoreType.DMA((micro_count,)),
             pltpu.SemaphoreType.DMA((micro_count,)),
+            pltpu.VMEM((8, 128), jnp.float32),
+            pltpu.VMEM((sections - 1, 8, 128), jnp.float32),
+            pltpu.SemaphoreType.DMA((sections - 1,)),
+            pltpu.SemaphoreType.DMA((sections - 1,)),
         ],
         compiler_params=pltpu.CompilerParams(
             collective_id=0, has_side_effects=True, vmem_limit_bytes=48 * 1024 * 1024
@@ -511,21 +543,13 @@
     value_matrix, output_matrix = gather_weights(value_weight[0], output_weight[0])
     head_width = value_matrix.shape[1]
     gains = norm_gain[0]
-    kept_inputs, kept_values, kept_grads, kept_dvalues = run_chain(
-        feed_rows, cot_rows, gains, value_matrix, output_matrix
+    kept_inputs, kept_values, kept_grads, kept_dvalues, square_table = run_chain(
+        feed_rows, cot_rows, gains, value_matrix, output_matrix, seq_len
     )
     unused_wide, unused_inverse, normed_rows = norm_parts(
         kept_inputs.reshape(-1, feature_width), gains
     )
-    normed_kept = normed_rows.reshape(kept_inputs.shape)
-    partial_squares = jnp.stack(
-        [
-            example_sums(normed_kept[m], kept_dvalues[m], seq_len)
-            + example_sums(kept_values[m], kept_grads[m], seq_len)
-            for m in range(micro_count)
-        ]
-    )
-    total_squares = lax.psum(partial_squares, "section")
+    total_squares = square_table[:micro_count, : example_count]
     clip_weight = 1.0 / (jnp.sqrt(total_squares) + 0.01)
     token_weight = jnp.repeat(clip_weight, seq_len, axis=1)[:, :, None]
     scaled_dvalues = (

time: 270 us -> 258 us (0.956)
  blocking collectives: 31.8 us -> 0 us
  Pallas kernels: 217 us -> 245 us
  matrix products: 6.32 us -> 2.42 us
    psum x1 -> x0, blocking collectives: 31.8 us -> none  [on_device(): total_squares = lax.psum(partial_squares, 'section')]
    pallas_call x1, Pallas kernels: 76.3 us -> 108 us  [run_chain(): pl.pallas_call(functools.partial(chain_kernel, sections, seq_len), out_sh...]
    dot_general x8 -> x0, matrix products: 3.9 us -> none  [the longest x4 1.95 us: example_sums(): jnp.einsum('eth,esh->ets', second, second, preferred_element_type=jnp.flo...]
    pallas_call x1, Pallas kernels: 72.8 us -> 69.3 us  [scatter_grads(): pl.pallas_call(functools.partial(scatter_kernel, ys, zs), out_shape=(jax....]
where the time goes in v8:
time: 258 us; the launch traced here: 257 us
  Pallas kernels  245 us (95%)
  local copies, waits for them, and re-layouts  6.85 us (3%)
    pallas_call x1, Pallas kernels, run_chain(): pl.pallas_call(functools.partial(chain_kernel, sections, seq_len), out_sh...  108 us
    pallas_call x1, Pallas kernels, scatter_grads(): pl.pallas_call(functools.partial(scatter_kernel, ys, zs), out_shape=(jax....  69.3 us
    pallas_call x1, Pallas kernels, gather_weights(): pl.pallas_call(functools.partial(gather_kernel, ys, zs), out_shape=(jax.S...  68.2 us

profile of v8, /device:TPU:4, one launch (start us, length us, event | category | flops | bytes accessed | tf_op | source)
XLA Modules:
  0.0 257.5 jit_solution(8543073616558957351)
XLA Ops:
  0.6 0.7 reduce.1
  1.3 68.2 %shard_map.86 = (bf16[4,8,56,1024]{3,2,1,0:T(8,128)(2,1)}, bf16[4,8,32,1792]{3,2,1,0:T(8,128)(2,1)}) custom-call(bf16[56,1024]{1,0:T(8,128)(2,1)} %bitcast.35, bf16[32,1792]{1,0:T(8,128)(2,1)} %bitcast.36), custom_call_target="tpu_custom_call" | custom-call | tf_op jit(solution)/shard_map/pallas_call | solution.py:363
  69.5 0.0 copy-start
  69.5 2.0 copy-done
  71.6 0.0 copy-start.1
  71.6 1.0 copy-done.1
  72.6 0.0 copy-start.2
  72.6 1.0 copy-done.2
  73.6 0.0 copy-start.3
  73.6 0.7 copy-done.3
  74.3 107.6 %shard_map.87 = (bf16[2,64,1792]{2,1,0:T(8,128)(2,1)S(1)}, bf16[2,64,1024]{2,1,0:T(8,128)(2,1)S(1)}, bf16[2,64,1792]{2,1,0:T(8,128)(2,1)S(1)}, bf16[2,64,1024]{2,1,0:T(8,128)(2,1)S(1)}, f32[8,128]{1,0:T(8,128)S(1)}) custom-call(bf16[2,64,1792]{2,1,0:T(8,128)(2,1)S(1)} %bitcast.30, bf16[2,64,1792]{2,1,0:T(8,128)(2,1)S(1)} %bitcast.31, ...), custom_call_target="tpu_custom_call" | custom-call | tf_op jit(solution)/shard_map/pallas_call | solution.py:215
  181.9 0.1 fusion.10
  182.0 0.2 fusion
  182.2 1.2 bitcast_convert_fusion.1
  183.5 1.2 bitcast_convert_fusion
  184.6 2.1 copy.11
  186.7 0.0 copy-start.4
  186.7 0.0 copy-start.5
  186.7 69.3 %shard_map.88 = (f32[56,1024]{1,0:T(8,128)S(1)}, f32[32,1792]{1,0:T(8,128)S(1)}) custom-call(bf16[4,8,56,1024]{3,2,1,0:T(8,128)(2,1)S(1)} %bitcast.28, bf16[8,4,32,1792]{3,2,1,0:T(8,128)(2,1)} %bitcast.33), custom_call_target="tpu_custom_call" | custom-call | tf_op jit(solution)/shard_map/pallas_call | solution.py:507
  256.0 0.0 copy-done.4
  256.0 0.7 fusion.9
  256.7 0.0 copy-done.5
  256.7 0.7 fusion.8
  (1 shorter events, 0.0 us)
Async XLA Ops:
  69.5 2.0 copy-start
  71.6 1.0 copy-start.1
  72.6 1.0 copy-start.2
  73.6 0.7 copy-start.3
  186.7 69.3 %copy-start.4 = (f32[1,56,1024]{2,1,0:T(8,128)S(1)}, f32[1,56,1024]{2,1,0:T(8,128)}, u32[]{:S(2)}) copy-start(f32[1,56,1024]{2,1,0:T(8,128)} %param.12) | copy-start | bytes 688132
  186.7 70.0 %copy-start.5 = (f32[1,32,1792]{2,1,0:T(8,128)S(1)}, f32[1,32,1792]{2,1,0:T(8,128)}, u32[]{:S(2)}) copy-start(f32[1,32,1792]{2,1,0:T(8,128)} %param.13) | copy-start | bytes 688132

commit v9 on v8

--- a/solution.py
+++ b/solution.py
@@ -43,9 +43,6 @@
     gram_first = jnp.einsum("eth,esh->ets", first, first, preferred_element_type=jnp.float32)
     gram_second = jnp.einsum("eth,esh->ets", second, second, preferred_element_type=jnp.float32)
     return jnp.sum(gram_first * gram_second, axis=(1, 2))
-
-
-TILE = 256
 
 
 def chain_kernel(
@@ -89,8 +86,10 @@
             device_id={"section": behind}, device_id_type=pl.DeviceIdType.MESH,
         )
 
-    def columns(i):
-        return pl.ds(pl.multiple_of(i * TILE, TILE), TILE)
+    head_tile, width_tile = heads, width
+
+    def columns(i, tile):
+        return pl.ds(pl.multiple_of(i * tile, tile), tile)
 
     for m in range(micro_count):
         @pl.when(place > 0)
@@ -104,22 +103,22 @@
         normed = (wide * inverse * gain_ref[...]).astype(jnp.bfloat16)
 
         def value_tile(i, carry):
-            kval_ref[m, :, columns(i)] = jnp.dot(
-                normed, wv_ref[:, columns(i)], preferred_element_type=jnp.float32
+            kval_ref[m, :, columns(i, head_tile)] = jnp.dot(
+                normed, wv_ref[:, columns(i, head_tile)], preferred_element_type=jnp.float32
             ).astype(jnp.bfloat16)
             return carry
 
-        lax.fori_loop(0, heads // TILE, value_tile, 0)
+        lax.fori_loop(0, heads // head_tile, value_tile, 0)
         values = kval_ref[m]
 
         def result_tile(i, carry):
-            fres[m, :, columns(i)] = (
-                fbuf[m, :, columns(i)].astype(jnp.float32)
-                + jnp.dot(values, wo_ref[:, columns(i)], preferred_element_type=jnp.float32)
+            fres[m, :, columns(i, width_tile)] = (
+                fbuf[m, :, columns(i, width_tile)].astype(jnp.float32)
+                + jnp.dot(values, wo_ref[:, columns(i, width_tile)], preferred_element_type=jnp.float32)
             ).astype(jnp.bfloat16)
             return carry
 
-        lax.fori_loop(0, width // TILE, result_tile, 0)
+        lax.fori_loop(0, width // width_tile, result_tile, 0)
 
         @pl.when(place < sections - 1)
         def _():
@@ -135,21 +134,21 @@
         kgrad_ref[m] = grad
 
         def dvalue_tile(i, carry):
-            kdv_ref[m, :, columns(i)] = lax.dot_general(
-                grad, wo_ref[columns(i), :], contract, preferred_element_type=jnp.float32
+            kdv_ref[m, :, columns(i, head_tile)] = lax.dot_general(
+                grad, wo_ref[columns(i, head_tile), :], contract, preferred_element_type=jnp.float32
             ).astype(jnp.bfloat16)
             return carry
 
-        lax.fori_loop(0, heads // TILE, dvalue_tile, 0)
+        lax.fori_loop(0, heads // head_tile, dvalue_tile, 0)
         dvalues = kdv_ref[m]
 
         def dnormed_tile(i, carry):
-            work[:, columns(i)] = lax.dot_general(
-                dvalues, wv_ref[columns(i), :], contract, preferred_element_type=jnp.float32
-            ) * gain_ref[:, columns(i)]
+            work[:, columns(i, width_tile)] = lax.dot_general(
+                dvalues, wv_ref[columns(i, width_tile), :], contract, preferred_element_type=jnp.float32
+            ) * gain_ref[:, columns(i, width_tile)]
             return carry
 
-        lax.fori_loop(0, width // TILE, dnormed_tile, 0)
+        lax.fori_loop(0, width // width_tile, dnormed_tile, 0)
         wide = kin_ref[m].astype(jnp.float32)
         inverse = lax.rsqrt(jnp.mean(wide * wide, axis=-1, keepdims=True) + 1e-06)
         dnormed = work[...]

time: 258 us -> 234 us (0.907)
  Pallas kernels: 245 us -> 221 us
    pallas_call x1, Pallas kernels: 108 us -> 83.7 us  [run_chain(): pl.pallas_call(functools.partial(chain_kernel, sections, seq_len), out_sh...]
where the time goes in v9:
time: 234 us
  Pallas kernels  221 us (94%)
  local copies, waits for them, and re-layouts  6.85 us (3%)
  other arithmetic  2.46 us (1%)
  matrix products  2.42 us (1%)
    pallas_call x1, Pallas kernels, run_chain(): pl.pallas_call(functools.partial(chain_kernel, sections, seq_len), out_sh...  83.7 us
    pallas_call x1, Pallas kernels, scatter_grads(): pl.pallas_call(functools.partial(scatter_kernel, ys, zs), out_shape=(jax....  69.3 us
    pallas_call x1, Pallas kernels, gather_weights(): pl.pallas_call(functools.partial(gather_kernel, ys, zs), out_shape=(jax.S...  68.2 us
    unnamed x12, local copies, waits for them, and re-layouts  4.77 us

profile of v9, /device:TPU:4, one launch (start us, length us, event | category | flops | bytes accessed | tf_op | source)
XLA Modules:
  0.0 233.6 jit_solution(4477894173946623429)
XLA Ops:
  0.6 0.7 reduce.1
  1.3 68.2 %shard_map.86 = (bf16[4,8,56,1024]{3,2,1,0:T(8,128)(2,1)}, bf16[4,8,32,1792]{3,2,1,0:T(8,128)(2,1)}) custom-call(bf16[56,1024]{1,0:T(8,128)(2,1)} %bitcast.35, bf16[32,1792]{1,0:T(8,128)(2,1)} %bitcast.36), custom_call_target="tpu_custom_call" | custom-call | tf_op jit(solution)/shard_map/pallas_call | solution.py:362
  69.5 0.0 copy-start
  69.5 2.0 copy-done
  71.6 0.0 copy-start.1
  71.6 1.0 copy-done.1
  72.6 0.0 copy-start.2
  72.6 1.0 copy-done.2
  73.6 0.0 copy-start.3
  73.6 0.7 copy-done.3
  74.3 83.7 %shard_map.87 = (bf16[2,64,1792]{2,1,0:T(8,128)(2,1)S(1)}, bf16[2,64,1024]{2,1,0:T(8,128)(2,1)S(1)}, bf16[2,64,1792]{2,1,0:T(8,128)(2,1)S(1)}, bf16[2,64,1024]{2,1,0:T(8,128)(2,1)S(1)}, f32[8,128]{1,0:T(8,128)S(1)}) custom-call(bf16[2,64,1792]{2,1,0:T(8,128)(2,1)S(1)} %bitcast.30, bf16[2,64,1792]{2,1,0:T(8,128)(2,1)S(1)} %bitcast.31, ...), custom_call_target="tpu_custom_call" | custom-call | tf_op jit(solution)/shard_map/pallas_call | solution.py:214
  158.0 0.1 fusion.10
  158.1 0.2 fusion
  158.3 1.2 bitcast_convert_fusion.1
  159.6 1.2 bitcast_convert_fusion
  160.7 2.1 copy.11
  162.8 0.0 copy-start.4
  162.8 0.0 copy-start.5
  162.8 69.3 %shard_map.88 = (f32[56,1024]{1,0:T(8,128)S(1)}, f32[32,1792]{1,0:T(8,128)S(1)}) custom-call(bf16[4,8,56,1024]{3,2,1,0:T(8,128)(2,1)S(1)} %bitcast.28, bf16[8,4,32,1792]{3,2,1,0:T(8,128)(2,1)} %bitcast.33), custom_call_target="tpu_custom_call" | custom-call | tf_op jit(solution)/shard_map/pallas_call | solution.py:506
  232.1 0.0 copy-done.4
  232.1 0.7 fusion.9
  232.8 0.0 copy-done.5
  232.8 0.7 fusion.8
  (1 shorter events, 0.0 us)
Async XLA Ops:
  69.5 2.0 copy-start
  71.6 1.0 copy-start.1
  72.6 1.0 copy-start.2
  73.6 0.7 copy-start.3
  162.8 69.3 %copy-start.4 = (f32[1,56,1024]{2,1,0:T(8,128)S(1)}, f32[1,56,1024]{2,1,0:T(8,128)}, u32[]{:S(2)}) copy-start(f32[1,56,1024]{2,1,0:T(8,128)} %param.12) | copy-start | bytes 688132
  162.8 70.0 %copy-start.5 = (f32[1,32,1792]{2,1,0:T(8,128)S(1)}, f32[1,32,1792]{2,1,0:T(8,128)}, u32[]{:S(2)}) copy-start(f32[1,32,1792]{2,1,0:T(8,128)} %param.13) | copy-start | bytes 688132

commit v10 on v9

--- a/solution.py
+++ b/solution.py
@@ -118,10 +118,9 @@
             ).astype(jnp.bfloat16)
             return carry
 
-        lax.fori_loop(0, width // width_tile, result_tile, 0)
-
         @pl.when(place < sections - 1)
         def _():
+            lax.fori_loop(0, width // width_tile, result_tile, 0)
             forward_copy(m).start()
 
     contract = (((1,), (1,)), ((), ()))

time: 234 us -> 234 us (level)
  no operation moved by 1% of the time
where the time goes in v10:
time: 234 us; the launch traced here: 233 us
  Pallas kernels  221 us (94%)
  local copies, waits for them, and re-layouts  6.85 us (3%)
  other arithmetic  2.46 us (1%)
  matrix products  2.42 us (1%)
    pallas_call x1, Pallas kernels, run_chain(): pl.pallas_call(functools.partial(chain_kernel, sections, seq_len), out_sh...  83.5 us
    pallas_call x1, Pallas kernels, scatter_grads(): pl.pallas_call(functools.partial(scatter_kernel, ys, zs), out_shape=(jax....  69.3 us
    pallas_call x1, Pallas kernels, gather_weights(): pl.pallas_call(functools.partial(gather_kernel, ys, zs), out_shape=(jax.S...  68.2 us
    unnamed x12, local copies, waits for them, and re-layouts  4.77 us

profile of v10, /device:TPU:4, one launch (start us, length us, event | category | flops | bytes accessed | tf_op | source)
XLA Modules:
  0.0 233.4 jit_solution(6230365076217127005)
XLA Ops:
  0.6 0.7 reduce.1
  1.3 68.2 %shard_map.86 = (bf16[4,8,56,1024]{3,2,1,0:T(8,128)(2,1)}, bf16[4,8,32,1792]{3,2,1,0:T(8,128)(2,1)}) custom-call(bf16[56,1024]{1,0:T(8,128)(2,1)} %bitcast.35, bf16[32,1792]{1,0:T(8,128)(2,1)} %bitcast.36), custom_call_target="tpu_custom_call" | custom-call | tf_op jit(solution)/shard_map/pallas_call | solution.py:361
  69.5 0.0 copy-start
  69.5 2.0 copy-done
  71.6 0.0 copy-start.1
  71.6 1.0 copy-done.1
  72.6 0.0 copy-start.2
  72.6 1.0 copy-done.2
  73.6 0.0 copy-start.3
  73.6 0.7 copy-done.3
  74.3 83.5 %shard_map.87 = (bf16[2,64,1792]{2,1,0:T(8,128)(2,1)S(1)}, bf16[2,64,1024]{2,1,0:T(8,128)(2,1)S(1)}, bf16[2,64,1792]{2,1,0:T(8,128)(2,1)S(1)}, bf16[2,64,1024]{2,1,0:T(8,128)(2,1)S(1)}, f32[8,128]{1,0:T(8,128)S(1)}) custom-call(bf16[2,64,1792]{2,1,0:T(8,128)(2,1)S(1)} %bitcast.30, bf16[2,64,1792]{2,1,0:T(8,128)(2,1)S(1)} %bitcast.31, ...), custom_call_target="tpu_custom_call" | custom-call | tf_op jit(solution)/shard_map/pallas_call | solution.py:213
  157.8 0.1 fusion.10
  157.9 0.2 fusion
  158.1 1.2 bitcast_convert_fusion.1
  159.4 1.2 bitcast_convert_fusion
  160.6 2.1 copy.11
  162.7 0.0 copy-start.4
  162.7 0.0 copy-start.5
  162.7 69.3 %shard_map.88 = (f32[56,1024]{1,0:T(8,128)S(1)}, f32[32,1792]{1,0:T(8,128)S(1)}) custom-call(bf16[4,8,56,1024]{3,2,1,0:T(8,128)(2,1)S(1)} %bitcast.28, bf16[8,4,32,1792]{3,2,1,0:T(8,128)(2,1)} %bitcast.33), custom_call_target="tpu_custom_call" | custom-call | tf_op jit(solution)/shard_map/pallas_call | solution.py:505
  232.0 0.0 copy-done.4
  232.0 0.7 fusion.9
  232.7 0.0 copy-done.5
  232.7 0.7 fusion.8
  (1 shorter events, 0.0 us)
Async XLA Ops:
  69.5 2.0 copy-start
  71.6 1.0 copy-start.1
  72.6 1.0 copy-start.2
  73.6 0.7 copy-start.3
  162.7 69.3 %copy-start.4 = (f32[1,56,1024]{2,1,0:T(8,128)S(1)}, f32[1,56,1024]{2,1,0:T(8,128)}, u32[]{:S(2)}) copy-start(f32[1,56,1024]{2,1,0:T(8,128)} %param.12) | copy-start | bytes 688132
  162.7 70.0 %copy-start.5 = (f32[1,32,1792]{2,1,0:T(8,128)S(1)}, f32[1,32,1792]{2,1,0:T(8,128)}, u32[]{:S(2)}) copy-start(f32[1,32,1792]{2,1,0:T(8,128)} %param.13) | copy-start | bytes 688132

commit v11 on v9

--- a/solution.py
+++ b/solution.py
@@ -436,8 +436,8 @@
 
 
 def scatter_kernel(
-    ys, zs, xv_ref, xo_ref, out_v, out_o,
-    v_land, v_part, o_part, o_send, o_land, v_ring, o_ring, v_sems, o_sems, vd_send, vd_recv, od_send, od_recv,
+    ys, zs, ht_ref, sdu_ref, ut_ref, sg_ref, out_v, out_o,
+    xv_ref, xo_ref, v_land, v_part, o_part, o_send, o_land, v_ring, o_ring, v_sems, o_sems, vd_send, vd_recv, od_send, od_recv,
 ):
     y = lax.axis_index("y")
     z = lax.axis_index("z")
@@ -448,6 +448,20 @@
     for k in range(1, ys):
         pl.semaphore_signal(barrier, inc=1, device_id={"y": lax.rem(y + k, ys)}, device_id_type=mesh_ids)
     pl.semaphore_wait(barrier, ys + 1)
+
+    v_rows, o_rows = xv_ref.shape[2], xo_ref.shape[2]
+    for a in range(ys):
+        group = jnp.dot(
+            ht_ref[a * zs * v_rows:(a + 1) * zs * v_rows, :], sdu_ref[...], preferred_element_type=jnp.float32
+        )
+        for b in range(zs):
+            xv_ref[a, b] = group[b * v_rows:(b + 1) * v_rows].astype(xv_ref.dtype)
+    for a in range(ys):
+        group = jnp.dot(
+            ut_ref[a * zs * o_rows:(a + 1) * zs * o_rows, :], sg_ref[...], preferred_element_type=jnp.float32
+        )
+        for b in range(zs):
+            xo_ref[b, a] = group[b * o_rows:(b + 1) * o_rows].astype(xo_ref.dtype)
 
     v_copies = direct_copies(xv_ref, v_land, "y", y, ys, vd_send, vd_recv)
     for c in v_copies:
@@ -476,18 +490,16 @@
         c.wait_send()
 
 
-def scatter_grads(value_block, output_block):
+def scatter_grads(normed_rows, scaled_dvalues, value_rows, scaled_grads):
     ys = lax.axis_size("y")
     zs = lax.axis_size("z")
-    rows_v, cols_v = value_block.shape
-    rows_o, cols_o = output_block.shape
+    rows_v, cols_v = normed_rows.shape[1], scaled_dvalues.shape[1]
+    rows_o, cols_o = value_rows.shape[1], scaled_grads.shape[1]
     v_rows = rows_v // (ys * zs)
     o_rows = rows_o // (ys * zs)
-    xv = value_block.reshape(ys, zs, v_rows, cols_v)
-    xo = output_block.reshape(ys, zs, o_rows, cols_o).transpose(1, 0, 2, 3)
     vmem = pl.BlockSpec(memory_space=pltpu.VMEM)
     rights, lefts = zs // 2, max((zs - 1) // 2, 1)
-    bf = value_block.dtype
+    bf = scaled_dvalues.dtype
 
     def ring_space(block):
         return [
@@ -509,9 +521,11 @@
             jax.ShapeDtypeStruct((v_rows, cols_v), jnp.float32),
             jax.ShapeDtypeStruct((o_rows, cols_o), jnp.float32),
         ),
-        in_specs=[vmem, vmem],
+        in_specs=[vmem] * 4,
         out_specs=(vmem, vmem),
         scratch_shapes=[
+            pltpu.VMEM((ys, zs, v_rows, cols_v), bf),
+            pltpu.VMEM((zs, ys, o_rows, cols_o), bf),
             pltpu.VMEM((ys - 1, zs, v_rows, cols_v), bf),
             pltpu.VMEM((zs, v_rows, cols_v), jnp.float32),
             pltpu.VMEM((ys, o_rows, cols_o), jnp.float32),
@@ -529,7 +543,7 @@
         compiler_params=pltpu.CompilerParams(
             collective_id=2, has_side_effects=True, vmem_limit_bytes=48 * 1024 * 1024
         ),
-    )(xv, xo)
+    )(normed_rows.T, scaled_dvalues, value_rows.T, scaled_grads)
 
 
 DP = ("y", "z")
@@ -563,13 +577,7 @@
     )
     value_rows = kept_values.reshape(-1, head_width)
     columns = normed_rows
-    value_block = lax.dot_general(
-        normed_rows, scaled_dvalues, (((0,), (0,)), ((), ())), preferred_element_type=jnp.float32
-    ).astype(jnp.bfloat16)
-    output_block = lax.dot_general(
-        value_rows, scaled_grads, (((0,), (0,)), ((), ())), preferred_element_type=jnp.float32
-    ).astype(jnp.bfloat16)
-    value_part, output_part = scatter_grads(value_block, output_block)
+    value_part, output_part = scatter_grads(normed_rows, scaled_dvalues, value_rows, scaled_grads)
     grad_scale = math.sqrt(feature_width * head_width)
     value_grad = (value_part * grad_scale + value_noise[0])[None]
     output_grad = (output_part * grad_scale + output_noise[0])[None]

time: 234 us -> 230 us (0.983)
  matrix products: 2.42 us -> 0 us
    dot_general x2 -> x0, matrix products: 2.42 us -> none  [the longest x1 1.24 us: on_device(): lax.dot_general(normed_rows, scaled_dvalues, (((0,), (0,)), ((), ())), pr...]
    unnamed x12 -> x14, local copies, waits for them, and re-layouts: 4.77 us -> 4.78 us
where the time goes in v11:
time: 230 us
  Pallas kernels  221 us (96%)
  local copies, waits for them, and re-layouts  5.23 us (2%)
    pallas_call x1, Pallas kernels, run_chain(): pl.pallas_call(functools.partial(chain_kernel, sections, seq_len), out_sh...  83.7 us
    pallas_call x1, Pallas kernels, scatter_grads(): pl.pallas_call(functools.partial(scatter_kernel, ys, zs), out_shape=(jax....  69.5 us
    pallas_call x1, Pallas kernels, gather_weights(): pl.pallas_call(functools.partial(gather_kernel, ys, zs), out_shape=(jax.S...  68.2 us
    unnamed x14, local copies, waits for them, and re-layouts  4.78 us

profile of v11, /device:TPU:4, one launch (start us, length us, event | category | flops | bytes accessed | tf_op | source)
XLA Modules:
  0.0 229.6 jit_solution(13093815650968826098)
XLA Ops:
  0.6 68.2 %shard_map.86 = (bf16[4,8,56,1024]{3,2,1,0:T(8,128)(2,1)}, bf16[4,8,32,1792]{3,2,1,0:T(8,128)(2,1)}) custom-call(bf16[56,1024]{1,0:T(8,128)(2,1)} %bitcast.35, bf16[32,1792]{1,0:T(8,128)(2,1)} %bitcast.36), custom_call_target="tpu_custom_call" | custom-call | tf_op jit(solution)/shard_map/pallas_call | solution.py:362
  68.8 0.0 copy-start
  68.8 2.0 copy-done
  70.8 0.0 copy-start.1
  70.8 1.0 copy-done.1
  71.9 0.0 copy-start.2
  71.9 1.0 copy-done.2
  72.9 0.0 copy-start.3
  72.9 0.7 copy-done.3
  73.6 0.0 copy-start.4
  73.6 83.7 %shard_map.87 = (bf16[2,64,1792]{2,1,0:T(8,128)(2,1)S(1)}, bf16[2,64,1024]{2,1,0:T(8,128)(2,1)S(1)}, bf16[2,64,1792]{2,1,0:T(8,128)(2,1)S(1)}, bf16[2,64,1024]{2,1,0:T(8,128)(2,1)S(1)}, f32[8,128]{1,0:T(8,128)S(1)}) custom-call(bf16[2,64,1792]{2,1,0:T(8,128)(2,1)S(1)} %bitcast.31, bf16[2,64,1792]{2,1,0:T(8,128)(2,1)S(1)} %bitcast.32, ...), custom_call_target="tpu_custom_call" | custom-call | tf_op jit(solution)/shard_map/pallas_call | solution.py:214
  157.3 0.0 copy-start.5
  157.3 0.1 fusion.3
  157.4 0.0 copy-start.6
  157.4 0.2 multiply_convert_fusion
  157.7 0.1 rsqrt.12
  157.8 0.2 copy.11
  158.0 0.0 copy-done.4
  158.0 0.3 fusion.ht_ref
  158.3 0.1 multiply_convert_fusion.2
  158.4 0.2 copy.12
  158.6 69.5 %shard_map.88 = (f32[56,1024]{1,0:T(8,128)S(1)}, f32[32,1792]{1,0:T(8,128)S(1)}) custom-call(bf16[1792,128]{1,0:T(8,128)(2,1)S(1)} %fusion.ht_ref, bf16[128,1024]{1,0:T(8,128)(2,1)S(1)} %bitcast.29, bf16[1024,128]{1,0:T(8,128)(2,1)S(1)} %bitcast.30, bf16[128,1792]{1,0:T(8,128)(2,1)S(1)} %bitcast.27), custom_call_target="tpu_custom_call" | custom-call | tf_op jit(solution)/shard_map/pallas_call | solution.py:518
  228.1 0.0 copy-done.5
  228.2 0.7 fusion.1
  228.9 0.0 copy-done.6
  228.9 0.7 fusion.2
  (2 shorter events, 0.0 us)
Async XLA Ops:
  68.8 2.0 copy-start
  70.8 1.0 copy-start.1
  71.9 1.0 copy-start.2
  72.9 0.7 copy-start.3
  73.6 84.4 %copy-start.4 = (f32[1,1792]{1,0:T(1,128)S(1)}, f32[1,1792]{1,0:T(1,128)}, u32[]{:S(2)}) copy-start(f32[1,1792]{1,0:T(1,128)} %gain_ref.1) | copy-start | bytes 21508
  157.3 70.9 %copy-start.5 = (f32[1,32,1792]{2,1,0:T(8,128)S(1)}, f32[1,32,1792]{2,1,0:T(8,128)}, u32[]{:S(2)}) copy-start(f32[1,32,1792]{2,1,0:T(8,128)} %param.13) | copy-start | bytes 688132
  157.4 71.5 %copy-start.6 = (f32[1,56,1024]{2,1,0:T(8,128)S(1)}, f32[1,56,1024]{2,1,0:T(8,128)}, u32[]{:S(2)}) copy-start(f32[1,56,1024]{2,1,0:T(8,128)} %param.12) | copy-start | bytes 688132

commit v12 on v11

--- a/solution.py
+++ b/solution.py
@@ -447,8 +447,6 @@
     pl.semaphore_signal(barrier, inc=1, device_id={"z": lax.rem(z + zs - 1, zs)}, device_id_type=mesh_ids)
     for k in range(1, ys):
         pl.semaphore_signal(barrier, inc=1, device_id={"y": lax.rem(y + k, ys)}, device_id_type=mesh_ids)
-    pl.semaphore_wait(barrier, ys + 1)
-
     v_rows, o_rows = xv_ref.shape[2], xo_ref.shape[2]
     for a in range(ys):
         group = jnp.dot(
@@ -462,6 +460,7 @@
         )
         for b in range(zs):
             xo_ref[b, a] = group[b * o_rows:(b + 1) * o_rows].astype(xo_ref.dtype)
+    pl.semaphore_wait(barrier, ys + 1)
 
     v_copies = direct_copies(xv_ref, v_land, "y", y, ys, vd_send, vd_recv)
     for c in v_copies:

time: 230 us -> 229 us (level)
  no operation moved by 1% of the time
where the time goes in v12:
time: 229 us
  Pallas kernels  221 us (97%)
  local copies, waits for them, and re-layouts  5.23 us (2%)
    pallas_call x1, Pallas kernels, run_chain(): pl.pallas_call(functools.partial(chain_kernel, sections, seq_len), out_sh...  83.7 us
    pallas_call x1, Pallas kernels, scatter_grads(): pl.pallas_call(functools.partial(scatter_kernel, ys, zs), out_shape=(jax....  68.8 us
    pallas_call x1, Pallas kernels, gather_weights(): pl.pallas_call(functools.partial(gather_kernel, ys, zs), out_shape=(jax.S...  68.2 us
    unnamed x14, local copies, waits for them, and re-layouts  4.78 us

profile of v12, /device:TPU:4, one launch (start us, length us, event | category | flops | bytes accessed | tf_op | source)
XLA Modules:
  0.0 228.9 jit_solution(306309040612654908)
XLA Ops:
  0.6 68.2 %shard_map.86 = (bf16[4,8,56,1024]{3,2,1,0:T(8,128)(2,1)}, bf16[4,8,32,1792]{3,2,1,0:T(8,128)(2,1)}) custom-call(bf16[56,1024]{1,0:T(8,128)(2,1)} %bitcast.35, bf16[32,1792]{1,0:T(8,128)(2,1)} %bitcast.36), custom_call_target="tpu_custom_call" | custom-call | tf_op jit(solution)/shard_map/pallas_call | solution.py:362
  68.8 0.0 copy-start
  68.8 2.0 copy-done
  70.8 0.0 copy-start.1
  70.8 1.0 copy-done.1
  71.9 0.0 copy-start.2
  71.9 1.0 copy-done.2
  72.9 0.0 copy-start.3
  72.9 0.7 copy-done.3
  73.6 0.0 copy-start.4
  73.6 83.7 %shard_map.87 = (bf16[2,64,1792]{2,1,0:T(8,128)(2,1)S(1)}, bf16[2,64,1024]{2,1,0:T(8,128)(2,1)S(1)}, bf16[2,64,1792]{2,1,0:T(8,128)(2,1)S(1)}, bf16[2,64,1024]{2,1,0:T(8,128)(2,1)S(1)}, f32[8,128]{1,0:T(8,128)S(1)}) custom-call(bf16[2,64,1792]{2,1,0:T(8,128)(2,1)S(1)} %bitcast.31, bf16[2,64,1792]{2,1,0:T(8,128)(2,1)S(1)} %bitcast.32, ...), custom_call_target="tpu_custom_call" | custom-call | tf_op jit(solution)/shard_map/pallas_call | solution.py:214
  157.3 0.0 copy-start.5
  157.3 0.1 fusion.3
  157.4 0.0 copy-start.6
  157.4 0.2 multiply_convert_fusion
  157.7 0.1 rsqrt.12
  157.8 0.2 copy.11
  158.0 0.0 copy-done.4
  158.0 0.3 fusion.ht_ref
  158.3 0.1 multiply_convert_fusion.2
  158.4 0.2 copy.12
  158.6 68.8 %shard_map.88 = (f32[56,1024]{1,0:T(8,128)S(1)}, f32[32,1792]{1,0:T(8,128)S(1)}) custom-call(bf16[1792,128]{1,0:T(8,128)(2,1)S(1)} %fusion.ht_ref, bf16[128,1024]{1,0:T(8,128)(2,1)S(1)} %bitcast.29, bf16[1024,128]{1,0:T(8,128)(2,1)S(1)} %bitcast.30, bf16[128,1792]{1,0:T(8,128)(2,1)S(1)} %bitcast.27), custom_call_target="tpu_custom_call" | custom-call | tf_op jit(solution)/shard_map/pallas_call | solution.py:517
  227.4 0.0 copy-done.5
  227.4 0.7 fusion.1
  228.1 0.0 copy-done.6
  228.1 0.7 fusion.2
  (2 shorter events, 0.0 us)
Async XLA Ops:
  68.8 2.0 copy-start
  70.8 1.0 copy-start.1
  71.9 1.0 copy-start.2
  72.9 0.7 copy-start.3
  73.6 84.4 %copy-start.4 = (f32[1,1792]{1,0:T(1,128)S(1)}, f32[1,1792]{1,0:T(1,128)}, u32[]{:S(2)}) copy-start(f32[1,1792]{1,0:T(1,128)} %gain_ref.1) | copy-start | bytes 21508
  157.3 70.1 %copy-start.5 = (f32[1,32,1792]{2,1,0:T(8,128)S(1)}, f32[1,32,1792]{2,1,0:T(8,128)}, u32[]{:S(2)}) copy-start(f32[1,32,1792]{2,1,0:T(8,128)} %param.13) | copy-start | bytes 688132
  157.4 70.7 %copy-start.6 = (f32[1,56,1024]{2,1,0:T(8,128)S(1)}, f32[1,56,1024]{2,1,0:T(8,128)}, u32[]{:S(2)}) copy-start(f32[1,56,1024]{2,1,0:T(8,128)} %param.12) | copy-start | bytes 688132

commit v13 on v12

--- a/solution.py
+++ b/solution.py
@@ -64,7 +64,6 @@
         pl.semaphore_signal(
             barrier, inc=1, device_id={"section": lax.rem(place + k, sections)}, device_id_type=pl.DeviceIdType.MESH
         )
-    pl.semaphore_wait(barrier, sections - 1)
 
     @pl.when(first)
     def _():
@@ -73,6 +72,8 @@
     @pl.when(last)
     def _():
         bbuf[...] = cot_ref[...]
+
+    pl.semaphore_wait(barrier, sections - 1)
 
     def forward_copy(m):
         return pltpu.make_async_remote_copy(
@@ -299,12 +300,11 @@
     pl.semaphore_signal(barrier, inc=1, device_id={"z": lax.rem(z + zs - 1, zs)}, device_id_type=mesh_ids)
     for k in range(1, ys):
         pl.semaphore_signal(barrier, inc=1, device_id={"y": lax.rem(y + k, ys)}, device_id_type=mesh_ids)
-    pl.semaphore_wait(barrier, ys + 1)
-
     own_v = pltpu.make_async_copy(wv_ref, wv_all.at[y, z], own_sem.at[0])
     own_o = pltpu.make_async_copy(wo_ref, wo_all.at[y, z], own_sem.at[1])
     own_v.start()
     own_o.start()
+    pl.semaphore_wait(barrier, ys + 1)
 
     def o_first(k, target):
         return pltpu.make_async_remote_copy(

time: 229 us -> 229 us (level)
  no operation moved by 1% of the time
where the time goes in v13:
time: 229 us
  Pallas kernels  221 us (97%)
  local copies, waits for them, and re-layouts  5.23 us (2%)
    pallas_call x1, Pallas kernels, run_chain(): pl.pallas_call(functools.partial(chain_kernel, sections, seq_len), out_sh...  83.6 us
    pallas_call x1, Pallas kernels, scatter_grads(): pl.pallas_call(functools.partial(scatter_kernel, ys, zs), out_shape=(jax....  68.8 us
    pallas_call x1, Pallas kernels, gather_weights(): pl.pallas_call(functools.partial(gather_kernel, ys, zs), out_shape=(jax.S...  68.2 us
    unnamed x14, local copies, waits for them, and re-layouts  4.78 us

profile of v13, /device:TPU:4, one launch (start us, length us, event | category | flops | bytes accessed | tf_op | source)
XLA Modules:
  0.0 228.8 jit_solution(4465749996273871585)
XLA Ops:
  0.6 68.2 %shard_map.86 = (bf16[4,8,56,1024]{3,2,1,0:T(8,128)(2,1)}, bf16[4,8,32,1792]{3,2,1,0:T(8,128)(2,1)}) custom-call(bf16[56,1024]{1,0:T(8,128)(2,1)} %bitcast.35, bf16[32,1792]{1,0:T(8,128)(2,1)} %bitcast.36), custom_call_target="tpu_custom_call" | custom-call | tf_op jit(solution)/shard_map/pallas_call | solution.py:362
  68.8 0.0 copy-start
  68.8 2.0 copy-done
  70.8 0.0 copy-start.1
  70.8 1.0 copy-done.1
  71.9 0.0 copy-start.2
  71.9 1.0 copy-done.2
  72.9 0.0 copy-start.3
  72.9 0.7 copy-done.3
  73.6 0.0 copy-start.4
  73.6 83.6 %shard_map.87 = (bf16[2,64,1792]{2,1,0:T(8,128)(2,1)S(1)}, bf16[2,64,1024]{2,1,0:T(8,128)(2,1)S(1)}, bf16[2,64,1792]{2,1,0:T(8,128)(2,1)S(1)}, bf16[2,64,1024]{2,1,0:T(8,128)(2,1)S(1)}, f32[8,128]{1,0:T(8,128)S(1)}) custom-call(bf16[2,64,1792]{2,1,0:T(8,128)(2,1)S(1)} %bitcast.31, bf16[2,64,1792]{2,1,0:T(8,128)(2,1)S(1)} %bitcast.32, ...), custom_call_target="tpu_custom_call" | custom-call | tf_op jit(solution)/shard_map/pallas_call | solution.py:215
  157.2 0.0 copy-start.5
  157.2 0.1 fusion.3
  157.4 0.0 copy-start.6
  157.4 0.2 multiply_convert_fusion
  157.6 0.1 rsqrt.12
  157.7 0.2 copy.11
  157.9 0.0 copy-done.4
  158.0 0.3 fusion.ht_ref
  158.3 0.1 multiply_convert_fusion.2
  158.4 0.2 copy.12
  158.6 68.8 %shard_map.88 = (f32[56,1024]{1,0:T(8,128)S(1)}, f32[32,1792]{1,0:T(8,128)S(1)}) custom-call(bf16[1792,128]{1,0:T(8,128)(2,1)S(1)} %fusion.ht_ref, bf16[128,1024]{1,0:T(8,128)(2,1)S(1)} %bitcast.29, bf16[1024,128]{1,0:T(8,128)(2,1)S(1)} %bitcast.30, bf16[128,1792]{1,0:T(8,128)(2,1)S(1)} %bitcast.27), custom_call_target="tpu_custom_call" | custom-call | tf_op jit(solution)/shard_map/pallas_call | solution.py:517
  227.4 0.0 copy-done.5
  227.4 0.7 fusion.1
  228.1 0.0 copy-done.6
  228.1 0.7 fusion.2
  (2 shorter events, 0.0 us)
Async XLA Ops:
  68.8 2.0 copy-start
  70.8 1.0 copy-start.1
  71.9 1.0 copy-start.2
  72.9 0.7 copy-start.3
  73.6 84.4 %copy-start.4 = (f32[1,1792]{1,0:T(1,128)S(1)}, f32[1,1792]{1,0:T(1,128)}, u32[]{:S(2)}) copy-start(f32[1,1792]{1,0:T(1,128)} %gain_ref.1) | copy-start | bytes 21508
  157.2 70.1 %copy-start.5 = (f32[1,32,1792]{2,1,0:T(8,128)S(1)}, f32[1,32,1792]{2,1,0:T(8,128)}, u32[]{:S(2)}) copy-start(f32[1,32,1792]{2,1,0:T(8,128)} %param.13) | copy-start | bytes 688132
  157.4 70.7 %copy-start.6 = (f32[1,56,1024]{2,1,0:T(8,128)S(1)}, f32[1,56,1024]{2,1,0:T(8,128)}, u32[]{:S(2)}) copy-start(f32[1,56,1024]{2,1,0:T(8,128)} %param.12) | copy-start | bytes 688132
